TPU v7x, 256 devices: a whole 4x4x8 slice. The times are simulated.
256 devices in a mesh: batch: 4 (over x_lo, core), ctx: 16 (over x_hi, z), head: 4 (over y).
Axes of the slice: x: 4 (x_hi: 2, x_lo: 2; x = x_hi * 2 + x_lo), y: 4, z: 8, core: 2. Of those that a mesh axis runs over, the one named last changes fastest.
Arguments:
- query_raw: bfloat16 [32768, 2560], P(('batch', 'ctx'), 'head'), parts along dimension 0, may hold values from -400 to 400
- key_raw: bfloat16 [32768, 2560], P(('batch', 'ctx'), 'head'), parts along dimension 0, may hold values from -400 to 400
- value_rows: bfloat16 [32768, 2560], P(('batch', 'ctx'), 'head'), parts along dimension 0, may hold values from -6 to 6
- query_gain: float32 [2560], P('head'), may hold values from 1.2 to 2
- key_gain: float32 [2560], P('head'), may hold values from 1.2 to 2
- segment: int32 [32768], P(('batch', 'ctx')), parts along dimension 0, may hold values from 0 to 5, never falling along the last dimension, each value on 1 to 2048 neighbouring positions
- destination: int32 [32768], P(('batch', 'ctx')), parts along dimension 0, may hold values from 0 to 8191, as said below
- timestep: int32 [24], P('batch'), parts along dimension 0, may hold values from 0 to 49
- out_weight: bfloat16 [2560, 5120], P('head'), may hold values from -0.3125 to 0.3125
- gate_table: float32 [50, 5120], P(None, 'head'), may hold values from 0.5 to 1.5
Outputs:
- gated: bfloat16 [32768, 5120], P(('batch', 'ctx'), 'head'), parts along dimension 0
There are 4 independent parts, one for each index of `batch`. A program takes and returns all parts, laid end to end along the dimension named above; an argument that names none is the same for every part. Nothing has to cross between parts.
Inputs may be any that keep to these rules, and one draw needn't show every extreme that they name: `segment`: the positions of one video are contiguous and the numbers never fall; each of the 6 videos has 1 to 2048 positions, some video exactly 2048. `destination`: A permutation of the 8192 rows. The 512 positions of each block b of 512 go 32 to every block c, and fill rows c*512 + b*32 to c*512 + (b+1)*32 - 1.
All inputs are finite; a program needn't handle non-finite values.
Results may differ from a plain program's by a relative error of at most 0.01555.
Values may be sent and summed in bfloat16 or wider, within the bound.
A program may use at most 192 MiB of HBM per device.

v0:
```python
import math

import jax
import jax.numpy as jnp
from jax import lax
from jax.sharding import PartitionSpec as P

HD = 128


def for_sending(array):

    def short(part):
        return part.astype(jnp.bfloat16) if part.dtype == jnp.float32 else part

    return jax.tree.map(short, array)


def attend(running, queries, query_mark, key_rows, value_part, key_mark, head_count, score_scale):
    maxima, totals, accumulated = running
    query_count = queries.shape[0]
    query_heads = queries.reshape(query_count, head_count, HD)
    key_heads = key_rows.reshape(key_rows.shape[0], head_count, HD)
    value_heads = value_part.reshape(value_part.shape[0], head_count, HD)
    scores = (
        jnp.einsum("qhd,khd->hqk", query_heads, key_heads, preferred_element_type=jnp.float32)
        * score_scale
    )
    allowed = (query_mark[:, None] == key_mark[None, :])[None]
    scores = jnp.where(allowed, scores, -1e30)
    new_max = jnp.maximum(maxima, jnp.max(scores, axis=2))
    factor = jnp.exp(maxima - new_max)
    weights = jnp.where(allowed, jnp.exp(scores - new_max[:, :, None]), 0.0)
    totals = totals * factor + jnp.sum(weights, axis=2)
    update = jnp.einsum(
        "hqk,khd->qhd",
        weights.astype(jnp.bfloat16),
        value_heads,
        preferred_element_type=jnp.float32,
    )
    accumulated = accumulated * jnp.transpose(factor)[:, :, None] + update
    return (new_max, totals, accumulated)


def attend_blocks(
    running, queries, query_mark, key_rows, value_part, key_mark, head_count, score_scale
):
    block_rows = queries.shape[0]
    block_count = key_rows.shape[0] // block_rows
    stacked = (
        key_rows.reshape(block_count, block_rows, key_rows.shape[1]),
        value_part.reshape(block_count, block_rows, value_part.shape[1]),
        key_mark.reshape(block_count, block_rows),
    )

    def advance(state, shard_piece):
        return (
            attend(
                state,
                queries,
                query_mark,
                shard_piece[0],
                shard_piece[1],
                shard_piece[2],
                head_count,
                score_scale,
            ),
            None,
        )

    running, unused = lax.scan(advance, running, stacked)
    return running


def local(
    query_raw,
    key_raw,
    value_rows,
    query_gain,
    key_gain,
    segment,
    destination,
    timestep,
    out_weight,
    gate_table,
):
    row_count = query_raw.shape[0]
    row_width = query_raw.shape[1]
    head_count = row_width // HD
    ctx_size = lax.axis_size("ctx")
    total_width = row_width * lax.axis_size("head")
    score_scale = 1.0 / math.sqrt(HD)
    query_float = query_raw.astype(jnp.float32)
    key_float = key_raw.astype(jnp.float32)
    query_sum, key_sum = lax.psum(
        (jnp.sum(query_float * query_float, axis=1), jnp.sum(key_float * key_float, axis=1)), "head"
    )
    queries = (
        query_float * lax.rsqrt(query_sum / total_width + 1e-06)[:, None] * query_gain
    ).astype(jnp.bfloat16)
    normed_keys = (key_float * lax.rsqrt(key_sum / total_width + 1e-06)[:, None] * key_gain).astype(
        jnp.bfloat16
    )
    slot_count = row_count // ctx_size
    target = destination // row_count * slot_count + destination % slot_count

    def placed(array):
        return jnp.zeros_like(array).at[target].set(array)

    initial = (
        jnp.full((head_count, row_count), -1e30, jnp.float32),
        jnp.zeros((head_count, row_count), jnp.float32),
        jnp.zeros((row_count, head_count, HD), jnp.float32),
    )
    own_queries, own_keys, own_values, own_segment = (
        lax.all_to_all(placed(queries), "ctx", split_axis=0, concat_axis=0, tiled=True),
        lax.all_to_all(placed(normed_keys), "ctx", split_axis=0, concat_axis=0, tiled=True),
        lax.all_to_all(placed(value_rows), "ctx", split_axis=0, concat_axis=0, tiled=True),
        lax.all_to_all(placed(segment), "ctx", split_axis=0, concat_axis=0, tiled=True),
    )
    running = attend_blocks(
        initial,
        own_queries,
        own_segment,
        lax.all_gather(own_keys, "ctx", axis=0, tiled=True),
        lax.all_gather(own_values, "ctx", axis=0, tiled=True),
        lax.all_gather(for_sending(own_segment), "ctx", axis=0, tiled=True),
        head_count,
        score_scale,
    )
    attended = (
        (running[2] / jnp.transpose(running[1])[:, :, None])
        .reshape(row_count, row_width)
        .astype(jnp.bfloat16)
    )
    head_terms = jnp.dot(attended, out_weight, preferred_element_type=jnp.float32)
    mixed_rows = lax.psum_scatter(
        head_terms.astype(jnp.bfloat16), "head", scatter_dimension=1, tiled=True
    ).astype(jnp.float32)
    video_gates = jnp.dot(
        jax.nn.one_hot(timestep, gate_table.shape[0], dtype=jnp.float32),
        gate_table,
        precision=lax.Precision.HIGHEST,
    )
    token_gates = jnp.dot(
        jax.nn.one_hot(own_segment, timestep.shape[0], dtype=jnp.float32),
        video_gates,
        precision=lax.Precision.HIGHEST,
    )
    return (mixed_rows * token_gates).astype(jnp.bfloat16)


def solution(mesh):
    placed = (
        P(("batch", "ctx"), "head"),
        P(("batch", "ctx"), "head"),
        P(("batch", "ctx"), "head"),
        P("head"),
        P("head"),
        P(("batch", "ctx")),
        P(("batch", "ctx")),
        P("batch"),
        P("head", None),
        P(None, "head"),
    )
    return jax.shard_map(
        local, mesh=mesh, in_specs=placed, out_specs=P(("batch", "ctx"), "head"), check_vma=False
    )
```

profile of v0, /device:TPU:1, one launch (start us, length us, event | category | flops | bytes accessed | tf_op | source)
XLA Modules:
  0.0 667.3 jit_solution(7085351126897524053)
XLA Ops:
  9.9 9.6 %all-reduce = (f32[512]{0:T(512)S(1)}, f32[512]{0:T(512)S(1)}) all-reduce(f32[512]{0:T(512)S(1)} %fusion.18, f32[512]{0:T(512)S(1)} %fusion.21), channel_id=1, replica_groups=mesh['batch'=4,'ctx'=16,'head'=4] {'head'}, use_global_device_ids=true, to_apply=%region_1.0 | all-reduce | flops 1024 | bytes 8192 | tf_op jit(solution)/shard_map/psum | solution.py:95
  22.9 27.1 %all_to_all.48 = bf16[16,32,640]{2,1,0:T(8,128)(2,1)} all-to-all(bf16[16,32,640]{2,1,0:T(8,128)(2,1)S(1)} %bitcast.79), channel_id=1, replica_groups=mesh['batch'=4,'ctx'=16,'head'=4] {'ctx'}, dimensions={0} | all-to-all | bytes 1310720 | tf_op jit(solution)/shard_map/all_to_all | solution.py:117
  53.4 28.8 %all_to_all.49 = bf16[16,32,640]{2,1,0:T(8,128)(2,1)} all-to-all(bf16[16,32,640]{2,1,0:T(8,128)(2,1)S(1)} %bitcast.80), channel_id=1, replica_groups=mesh['batch'=4,'ctx'=16,'head'=4] {'ctx'}, dimensions={0} | all-to-all | bytes 1310720 | tf_op jit(solution)/shard_map/all_to_all | solution.py:118
  85.5 7.6 %all-to-all-start = ((s32[16,32,1]{1,2,0:T(1,128)}), s32[16,32,1]{1,2,0:T(1,128)S(1)}, u32[]{:S(2)}, u32[]{:S(2)}) async-start(s32[16,32,1]{1,2,0:T(1,128)} %all_to_all.32), calls=%async_computation | async-start | bytes 16384 | tf_op jit(solution)/shard_map/all_to_all | solution.py:119
  96.8 5.1 all-to-all-done
  107.3 40.6 %all-gather = s32[16,1,512]{2,1,0:T(1,128)S(1)} all-gather(s32[1,1,512]{2,1,0:T(1,128)S(1)} %reshape.107), channel_id=1, replica_groups=mesh['batch'=4,'ctx'=16,'head'=4] {'ctx'}, dimensions={0}, use_global_device_ids=true | all-gather | bytes 34816 | tf_op jit(solution)/shard_map/all_gather | solution.py:127
  149.0 67.2 %all-gather.4.cloned.1.call-done = bf16[8192,640]{1,0:T(8,128)(2,1)} async-done(((bf16[512,640]{1,0:T(8,128)(2,1)}), bf16[8192,640]{1,0:T(8,128)(2,1)}) %all-gather.4.cloned.1.call-update) | async-done | bytes 10485776 | tf_op jit(solution)/shard_map/all_gather | solution.py:125
  216.1 153.3 %all-gather.6.cloned.1.call-done = bf16[8192,640]{1,0:T(8,128)(2,1)} async-done(((bf16[512,640]{1,0:T(8,128)(2,1)}), bf16[8192,640]{1,0:T(8,128)(2,1)}) %all-gather.6.cloned.1.call-update) | async-done | bytes 10485776 | tf_op jit(solution)/shard_map/all_gather | solution.py:126
  369.4 221.9 %while.15 = (s32[]{:T(128)}, f32[5,512]{1,0:T(8,128)S(1)}, f32[5,512]{1,0:T(8,128)S(1)}, f32[512,5,128]{0,2,1:T(8,128)}, s32[512]{0:T(512)S(1)}, /*index=5*/s32[...) while((s32[]{:T(128)}, f32[5,512]{1,0:T(8,128)S(1)}, ...), condition=%wide.region_11.12_spmd.clone, body=%wide.region_8.11_spmd.clone.sunk | while | flops 689388544 | bytes 42508464 | solution.py:71
  371.3 4.5 fusion.66
  376.2 5.4 fusion.70
  384.8 4.5 fusion.66
  389.7 5.8 fusion.70
  398.7 4.5 fusion.66
  403.6 5.8 fusion.70
  412.6 4.5 fusion.66
  417.5 5.8 fusion.70
  426.5 4.5 fusion.66
  431.4 5.8 fusion.70
  445.3 5.8 fusion.70
  459.2 5.8 fusion.70
  473.1 5.8 fusion.70
  486.9 5.8 fusion.70
  500.8 5.8 fusion.70
  514.7 5.8 fusion.70
  528.6 5.8 fusion.70
  542.5 5.8 fusion.70
  556.4 5.8 fusion.70
  570.3 5.8 fusion.70
  584.2 5.8 fusion.70
  592.8 8.9 %convolution_convert_fusion = bf16[512,5120]{1,0:T(8,128)(2,1)} fusion(bf16[512,640]{0,1:T(8,128)(2,1)S(1)} %bitcast.83, bf16[640,5120]{1,0:T(8,128)(2,1)} %param.20), kind=kOutput, calls=%fused_computation.26 | convolution fusion | flops 3358064640 | bytes 12451840 | tf_op jit(solution)/shard_map/dot_general | solution.py:136
  602.6 54.5 %reduce-scatter.2.cloned.1.call-done = bf16[512,1280]{1,0:T(8,128)(2,1)} async-done(((bf16[512,5120]{1,0:T(8,128)(2,1)}), bf16[512,1280]{1,0:T(8,128)(2,1)}) %reduce-scatter.2.cloned.1.call-update) | async-done | bytes 1310736 | tf_op jit(solution)/shard_map/reduce_scatter | solution.py:137
  (272 shorter events, 135.0 us)
Async XLA Ops:
  6.5 595.2 %copy-start = (f32[50,1280]{1,0:T(8,128)S(1)}, f32[50,1280]{1,0:T(8,128)}, u32[]{:S(2)}) copy-start(f32[50,1280]{1,0:T(8,128)} %param.21) | copy-start | bytes 768004
  6.5 209.6 %all-gather.4.cloned.1.call-start = ((), (), s32[]{:S(2)}) async-start(), calls=%async_computation.5 | async-start | bytes 11141120 | tf_op jit(solution)/shard_map/all_gather | solution.py:125
  22.9 70.3 %copy-start.1 = (bf16[512,640]{1,0:T(8,128)(2,1)S(1)}, bf16[512,640]{1,0:T(8,128)(2,1)}, u32[]{:S(2)}) copy-start(bf16[512,640]{1,0:T(8,128)(2,1)} %param.12) | copy-start | bytes 1966084
  22.9 70.3 %copy-start.2 = (f32[640]{0:T(1024)S(1)}, f32[640]{0:T(1024)}, u32[]{:S(2)}) copy-start(f32[640]{0:T(1024)} %param.15) | copy-start | bytes 7684
  50.0 319.4 %all-gather.6.cloned.1.call-start = ((), (), s32[]{:S(2)}) async-start(), calls=%async_computation.6 | async-start | bytes 11141120 | tf_op jit(solution)/shard_map/all_gather | solution.py:126
  85.5 16.4 %all-to-all-start = ((s32[16,32,1]{1,2,0:T(1,128)}), s32[16,32,1]{1,2,0:T(1,128)S(1)}, u32[]{:S(2)}, u32[]{:S(2)}) async-start(s32[16,32,1]{1,2,0:T(1,128)} %all_to_all.32), calls=%async_computation | async-start | bytes 16384 | tf_op jit(solution)/shard_map/all_to_all | solution.py:119
  101.9 46.0 %all-to-all-start.2 = ((bf16[16,32,640]{2,1,0:T(8,128)(2,1)}), bf16[16,32,640]{2,1,0:T(8,128)(2,1)S(1)}, u32[]{:S(2)}, u32[]{:S(2)}) async-start(bf16[16,32,640]{2,1,0:T(8,128)(2,1)} %bitcast.3), calls=%async_computation.2 | async-start | bytes 1310720 | tf_op jit(solution)/shard_map/all_to_all | solution.py:116
  105.9 551.3 %reduce-scatter.2.cloned.1.call-start = ((), (), s32[]{:S(2)}) async-start(), calls=%async_computation.7 | async-start | bytes 6553600 | tf_op jit(solution)/shard_map/reduce_scatter | solution.py:137
  389.4 6.1 slice-start
  389.7 5.8 slice-start.1
  403.3 6.1 slice-start
  417.2 6.1 slice-start
  431.1 6.1 slice-start
  431.4 5.8 slice-start.1
  445.0 6.1 slice-start
  445.2 5.8 slice-start.1
  458.9 6.1 slice-start
  459.1 5.8 slice-start.1
  472.8 6.1 slice-start
  473.0 5.8 slice-start.1
  486.6 6.1 slice-start
  500.5 6.1 slice-start
  514.4 6.1 slice-start
  514.7 5.8 slice-start.1
  528.3 6.1 slice-start
  528.6 5.8 slice-start.1
  542.2 6.1 slice-start
  542.5 5.8 slice-start.1
  556.1 6.1 slice-start
  556.4 5.8 slice-start.1
  570.0 6.1 slice-start
  583.9 6.1 slice-start
  (9 other events, 46.7 us)
Sparse Core Ops, SparseCore 0:
  50.2 165.9 all-gather.3
  218.7 150.6 all-gather.5
  601.9 55.2 reduce-scatter.1
where the time goes:
time: 669 us; the launch traced here: 667 us
  waiting for transfers between devices  280 us (42%)
  matrix products  178 us (27%)
  blocking collectives  106 us (16%)
  local copies, waits for them, and re-layouts  40.4 us (6%)
  other arithmetic  36.7 us (5%)
  between operations  13.2 us (2%)
  starting transfers between devices  11.6 us (2%)
    all_gather x1, waiting for transfers between devices, local(): lax.all_gather(own_values, 'ctx', axis=0, tiled=True)  153 us
    dot_general x16, matrix products, attend(): jnp.einsum('hqk,khd->qhd', weights.astype(jnp.bfloat16), value_heads, pre...  92.3 us
    dot_general x16, matrix products, attend(): jnp.einsum('qhd,khd->hqk', query_heads, key_heads, preferred_element_type...  72.6 us
    all_gather x1, waiting for transfers between devices, local(): lax.all_gather(own_keys, 'ctx', axis=0, tiled=True)  67.2 us
    reduce_scatter x1, waiting for transfers between devices, local(): lax.psum_scatter(head_terms.astype(jnp.bfloat16), 'head', scatter_dimensi...  54.5 us
    all_gather x1, blocking collectives, local(): lax.all_gather(for_sending(own_segment), 'ctx', axis=0, tiled=True)  40.6 us
    dynamic_slice x64, local copies, waits for them, and re-layouts, attend_blocks(): running, unused = lax.scan(advance, running, stacked)  31.2 us
    all_to_all x1, blocking collectives, local(): lax.all_to_all(placed(value_rows), 'ctx', split_axis=0, concat_axis=0, ti...  28.8 us
  transfers between devices with their start and end apart: 5, of which 4 were waited for; matrix products, arithmetic and copies ran while one was open for 2% of the time, Pallas kernels for 0%

commit v1 on v0

v1 whole, which is shorter than its diff:
```python
import functools
import math

import jax
import jax.numpy as jnp
from jax import lax
from jax.experimental import pallas as pl
from jax.experimental.pallas import tpu as pltpu
from jax.sharding import PartitionSpec as P

HD = 128
REACH = 4


def flash_kernel(
    need_ref, qp_ref, kt_ref, kp_ref,
    q_ref, k_ref, v_ref, qs_ref, ks_ref,
    o_ref, m_scr, l_scr, acc_scr, *, offsets, score_scale
):
    j = pl.program_id(0)
    o = pl.program_id(1)

    @pl.when(o == 0)
    def _():
        m_scr[...] = jnp.full_like(m_scr, -1e30)
        l_scr[...] = jnp.zeros_like(l_scr)
        acc_scr[...] = jnp.zeros_like(acc_scr)

    @pl.when(need_ref[j * offsets + o] != 0)
    def _():
        q = q_ref[0]
        k = k_ref[0]
        s = lax.dot_general(
            q, k, (((1,), (1,)), ((), ())), preferred_element_type=jnp.float32
        ) * score_scale
        mask = qs_ref[0] == ks_ref[0]
        s = jnp.where(mask, s, -1e30)
        m_prev = m_scr[...]
        m_new = jnp.maximum(m_prev, jnp.max(s, axis=1, keepdims=True))
        alpha = jnp.exp(m_prev - m_new)
        p = jnp.where(mask, jnp.exp(s - m_new), 0.0)
        l_scr[...] = alpha * l_scr[...] + jnp.sum(p, axis=1, keepdims=True)
        acc_scr[...] = alpha * acc_scr[...] + jnp.dot(
            p.astype(jnp.bfloat16), v_ref[0], preferred_element_type=jnp.float32
        )
        m_scr[...] = m_new

    @pl.when(o == offsets - 1)
    def _():
        o_ref[0] = (acc_scr[...] / l_scr[...]).astype(o_ref.dtype)


def flash(need, qp, kt, kp, q_tiles, k_tiles, v_tiles, seg_rows, seg_cols, score_scale):
    slots, rows, width = q_tiles.shape
    offsets = 2 * REACH + 1
    kern = functools.partial(flash_kernel, offsets=offsets, score_scale=score_scale)
    grid_spec = pltpu.PrefetchScalarGridSpec(
        num_scalar_prefetch=4,
        grid=(slots, offsets),
        in_specs=[
            pl.BlockSpec((1, rows, width), lambda j, o, nd, qp, kt, kp: (j, 0, 0)),
            pl.BlockSpec((1, rows, width), lambda j, o, nd, qp, kt, kp: (kt[j * offsets + o], 0, 0)),
            pl.BlockSpec((1, rows, width), lambda j, o, nd, qp, kt, kp: (kt[j * offsets + o], 0, 0)),
            pl.BlockSpec((1, rows, 1), lambda j, o, nd, qp, kt, kp: (qp[j], 0, 0)),
            pl.BlockSpec((1, 1, rows), lambda j, o, nd, qp, kt, kp: (kp[j * offsets + o], 0, 0)),
        ],
        out_specs=pl.BlockSpec((1, rows, width), lambda j, o, nd, qp, kt, kp: (j, 0, 0)),
        scratch_shapes=[
            pltpu.VMEM((rows, 1), jnp.float32),
            pltpu.VMEM((rows, 1), jnp.float32),
            pltpu.VMEM((rows, width), jnp.float32),
        ],
    )
    return pl.pallas_call(
        kern,
        grid_spec=grid_spec,
        out_shape=jax.ShapeDtypeStruct((slots, rows, width), jnp.bfloat16),
        compiler_params=pltpu.CompilerParams(
            dimension_semantics=("arbitrary", "arbitrary")
        ),
    )(need, qp, kt, kp, q_tiles, k_tiles, v_tiles, seg_rows, seg_cols)


def local(
    query_raw,
    key_raw,
    value_rows,
    query_gain,
    key_gain,
    segment,
    destination,
    timestep,
    out_weight,
    gate_table,
):
    row_count = query_raw.shape[0]
    row_width = query_raw.shape[1]
    head_count = row_width // HD
    ctx_size = lax.axis_size("ctx")
    total_width = row_width * lax.axis_size("head")
    score_scale = 1.0 / math.sqrt(HD)
    me = lax.axis_index("ctx")
    tiles = head_count * ctx_size
    slots = tiles // ctx_size

    query_float = query_raw.astype(jnp.float32)
    key_float = key_raw.astype(jnp.float32)
    query_sum, key_sum = lax.psum(
        (jnp.sum(query_float * query_float, axis=1), jnp.sum(key_float * key_float, axis=1)), "head"
    )
    queries = (
        query_float * lax.rsqrt(query_sum / total_width + 1e-06)[:, None] * query_gain
    ).astype(jnp.bfloat16)
    normed_keys = (key_float * lax.rsqrt(key_sum / total_width + 1e-06)[:, None] * key_gain).astype(
        jnp.bfloat16
    )

    qkv = jnp.stack([queries, normed_keys, value_rows]).reshape(3, row_count, head_count, HD)
    qkv = jnp.transpose(qkv, (0, 2, 1, 3))

    inverse = pow(slots, -1, ctx_size)
    own = []
    for j in range(slots):
        target = lax.rem(inverse * (me - j + ctx_size), ctx_size)
        head = (slots * target + j) // ctx_size
        piece = lax.dynamic_index_in_dim(qkv, head, axis=1, keepdims=False)
        perm = [((slots * e + j) % ctx_size, e) for e in range(ctx_size)]
        own.append(lax.ppermute(piece, "ctx", perm))
    own = jnp.stack(own, axis=1)

    kv_own = own[1:]
    left = lax.ppermute(
        kv_own[:, slots - REACH:], "ctx", [(e, e + 1) for e in range(ctx_size - 1)]
    )
    right = lax.ppermute(
        kv_own[:, :REACH], "ctx", [(e, e - 1) for e in range(1, ctx_size)]
    )
    kv_all = jnp.concatenate([left, kv_own, right], axis=1)

    seg_all = lax.all_gather(segment, "ctx", axis=0, tiled=True)
    dest_all = lax.all_gather(destination, "ctx", axis=0, tiled=True)
    seg_blocks = seg_all.reshape(ctx_size, row_count)
    seg_lo = seg_blocks[:, 0]
    seg_hi = seg_blocks[:, -1]

    offsets = 2 * REACH + 1
    jj = jnp.arange(slots, dtype=jnp.int32)[:, None]
    oo = jnp.arange(offsets, dtype=jnp.int32)[None, :] - REACH
    t_q = slots * me + jj
    t_k = t_q + oo
    p_q = t_q % ctx_size
    valid = (t_k >= 0) & (t_k < tiles)
    t_kc = jnp.clip(t_k, 0, tiles - 1)
    p_k = t_kc % ctx_size
    same_head = (t_kc // ctx_size) == (t_q // ctx_size)
    meet = (seg_lo[p_q] <= seg_hi[p_k]) & (seg_lo[p_k] <= seg_hi[p_q])
    need = (valid & same_head & meet).astype(jnp.int32).reshape(-1)
    kt = (jj + oo + REACH).astype(jnp.int32).reshape(-1)
    qp = p_q[:, 0].astype(jnp.int32)
    kp = p_k.astype(jnp.int32).reshape(-1)

    attended = flash(
        need, qp, kt, kp,
        own[0], kv_all[0], kv_all[1],
        seg_blocks.reshape(ctx_size, row_count, 1),
        seg_blocks.reshape(ctx_size, 1, row_count),
        score_scale,
    )

    slot_count = row_count // ctx_size
    dest_blocks = dest_all.reshape(ctx_size, row_count)
    dest_mine = dest_blocks[qp]
    place = (dest_mine // row_count) * slot_count + dest_mine % slot_count
    placed = jnp.zeros_like(attended).at[jj, place].set(attended)
    placed = placed.reshape(slots, ctx_size, slot_count, HD).transpose(1, 0, 2, 3)
    got = lax.all_to_all(placed, "ctx", split_axis=0, concat_axis=0, tiled=True)
    got = got.reshape(head_count, ctx_size, slot_count, HD).transpose(1, 2, 0, 3)
    owned_attended = got.reshape(row_count, row_width)

    owned_video_all = jnp.zeros_like(seg_all).at[dest_all].set(seg_all)
    owned_video = lax.dynamic_slice_in_dim(owned_video_all, me * row_count, row_count)

    head_terms = jnp.dot(owned_attended, out_weight, preferred_element_type=jnp.float32)
    mixed_rows = lax.psum_scatter(
        head_terms.astype(jnp.bfloat16), "head", scatter_dimension=1, tiled=True
    ).astype(jnp.float32)
    video_gates = jnp.dot(
        jax.nn.one_hot(timestep, gate_table.shape[0], dtype=jnp.float32),
        gate_table,
        precision=lax.Precision.HIGHEST,
    )
    token_gates = jnp.dot(
        jax.nn.one_hot(owned_video, timestep.shape[0], dtype=jnp.float32),
        video_gates,
        precision=lax.Precision.HIGHEST,
    )
    return (mixed_rows * token_gates).astype(jnp.bfloat16)


def solution(mesh):
    placed = (
        P(("batch", "ctx"), "head"),
        P(("batch", "ctx"), "head"),
        P(("batch", "ctx"), "head"),
        P("head"),
        P("head"),
        P(("batch", "ctx")),
        P(("batch", "ctx")),
        P("batch"),
        P("head", None),
        P(None, "head"),
    )
    return jax.shard_map(
        local, mesh=mesh, in_specs=placed, out_specs=P(("batch", "ctx"), "head"), check_vma=False
    )
```

time: 669 us -> 333 us (0.50)
  waiting for transfers between devices: 280 us -> 51 us
  matrix products: 178 us -> 12.7 us
  Pallas kernels: 0 us -> 44.8 us
  other arithmetic: 36.7 us -> 3.89 us
  blocking collectives: 106 us -> 127 us
  local copies, waits for them, and re-layouts: 40.4 us -> 54.6 us
  starting transfers between devices: 11.6 us -> 24.3 us
    all_gather x2 -> x0, waiting for transfers between devices: 220 us -> none  [the longest x1 153 us: local(): lax.all_gather(own_values, 'ctx', axis=0, tiled=True)]
    dot_general x34 -> x2, matrix products: 177 us -> 12.5 us  [the longest x1 8.85 us: local(): jnp.dot(owned_attended, out_weight, preferred_element_type=jnp.float32)]
    all_gather x1 -> x2, blocking collectives: 40.6 us -> 87.4 us  [the longest x1 58.7 us: local(): seg_all = lax.all_gather(segment, 'ctx', axis=0, tiled=True)]
    pallas_call x0 -> x1, Pallas kernels: none -> 44.8 us  [flash(): pl.pallas_call(kern, grid_spec=grid_spec, out_shape=jax.ShapeDtypeStruct(...]
    dynamic_slice x64 -> x1, local copies, waits for them, and re-layouts: 31.2 us -> 0.08 us  [local(): lax.dynamic_slice_in_dim(owned_video_all, me * row_count, row_count)]
    all_to_all x2 -> x1, blocking collectives: 55.9 us -> 30 us  [local(): got = lax.all_to_all(placed, 'ctx', split_axis=0, concat_axis=0, tiled=True)]
    scatter x2 -> x1, local copies, waits for them, and re-layouts: 5.92 us -> 30.7 us  [local(): owned_video_all = jnp.zeros_like(seg_all).at[dest_all].set(seg_all)]
    ppermute x0 -> x7, starting transfers between devices: none -> 24.3 us  [the longest x5 19.6 us: local(): own.append(lax.ppermute(piece, 'ctx', perm))]
  transfers between devices with their start and end apart: 5 -> 8, of which waited for: 4 -> 3; matrix products, arithmetic and copies ran while one was open for 2% -> 13% of each run, Pallas kernels for 0% -> 0%
where the time goes in v1:
time: 333 us; the launch traced here: 332 us
  blocking collectives  127 us (38%)
  local copies, waits for them, and re-layouts  54.6 us (16%)
  waiting for transfers between devices  51 us (15%)
  Pallas kernels  44.8 us (13%)
  starting transfers between devices  24.3 us (7%)
  between operations  13.7 us (4%)
  matrix products  12.7 us (4%)
  other arithmetic  3.89 us (1%)
    all_gather x1, blocking collectives, local(): seg_all = lax.all_gather(segment, 'ctx', axis=0, tiled=True)  58.7 us
    pallas_call x1, Pallas kernels, flash(): pl.pallas_call(kern, grid_spec=grid_spec, out_shape=jax.ShapeDtypeStruct(...  44.8 us
    reduce_scatter x1, waiting for transfers between devices, local(): lax.psum_scatter(head_terms.astype(jnp.bfloat16), 'head', scatter_dimensi...  38 us
    scatter x1, local copies, waits for them, and re-layouts, local(): owned_video_all = jnp.zeros_like(seg_all).at[dest_all].set(seg_all)  30.7 us
    all_to_all x1, blocking collectives, local(): got = lax.all_to_all(placed, 'ctx', split_axis=0, concat_axis=0, tiled=True)  30 us
    all_gather x1, blocking collectives, local(): dest_all = lax.all_gather(destination, 'ctx', axis=0, tiled=True)  28.7 us
    ppermute x5, starting transfers between devices, local(): own.append(lax.ppermute(piece, 'ctx', perm))  19.6 us
    unnamed x33, local copies, waits for them, and re-layouts  9.75 us
  transfers between devices with their start and end apart: 8, of which 3 were waited for; matrix products, arithmetic and copies ran while one was open for 13% of the time, Pallas kernels for 0%

profile of v1, /device:TPU:1, one launch (start us, length us, event | category | flops | bytes accessed | tf_op | source)
XLA Modules:
  0.0 332.1 jit_solution(16056840625718152038)
XLA Ops:
  6.5 1.5 copy.46
  9.0 9.6 %all-reduce = (f32[512]{0:T(512)S(1)}, f32[512]{0:T(512)S(1)}) all-reduce(f32[512]{0:T(512)S(1)} %fusion.4, f32[512]{0:T(512)S(1)} %fusion.1), channel_id=1, replica_groups=mesh['batch'=4,'ctx'=16,'head'=4] {'head'}, use_global_device_ids=true, to_apply=%region_3.0 | all-reduce | flops 1024 | bytes 8192 | tf_op jit(solution)/shard_map/psum | solution.py:108
  19.6 4.4 %collective-permute-start.1 = (bf16[3,512,128]{2,1,0:T(8,128)(2,1)S(1)}, bf16[3,512,128]{2,1,0:T(8,128)(2,1)S(1)}, u32[]{:S(2)}, u32[]{:S(2)}) collective-permute-start(bf16[3,512,128]{2,1,0:T(8,128)(2,1)S(1)} %bitcast.95), channel_id=1, source_target_pairs={{4,0},{24,4},{44,8},{0,12},{20,16},{40,20},{60,24},{16,28},{36,32}... | collective-permute-start | bytes 1179656 | tf_op jit(solution)/shard_map/ppermute | solution.py:128
  24.2 1.8 collective-permute-start.2
  26.2 1.1 collective-permute-start.3
  27.4 0.9 copy.53
  28.3 10.6 %collective-permute-start.4 = (bf16[3,512,128]{2,1,0:T(8,128)(2,1)}, bf16[3,512,128]{2,1,0:T(8,128)(2,1)S(1)}, u32[]{:S(2)}, u32[]{:S(2)}) collective-permute-start(bf16[3,512,128]{2,1,0:T(8,128)(2,1)} %bitcast.98), channel_id=1, source_target_pairs={{16,0},{36,4},{56,8},{12,12},{32,16},{52,20},{8,24},{28,28},{48,32... | collective-permute-start | bytes 1179656 | tf_op jit(solution)/shard_map/ppermute | solution.py:128
  38.9 0.9 copy.49
  39.9 1.6 collective-permute-start
  41.7 58.7 %all-gather.1.ks_ref = s32[16,1,512]{2,1,0:T(1,128)S(1)} all-gather(s32[1,1,512]{2,1,0:T(1,128)S(1)} %bitcast.102), channel_id=1, replica_groups=mesh['batch'=4,'ctx'=16,'head'=4] {'ctx'}, dimensions={0}, use_global_device_ids=true | all-gather | bytes 34816 | tf_op jit(solution)/shard_map/all_gather | solution.py:140
  100.6 0.8 gather_fusion.2
  101.4 0.8 gather_fusion.3
  102.2 0.6 gather_fusion.1
  102.8 0.6 gather_fusion.4
  104.9 0.6 add.331.kt_ref
  105.5 3.0 reshape_reshape.8.qs_ref
  108.5 28.7 %all-gather = s32[16,1,512]{2,1,0:T(1,128)S(1)} all-gather(s32[1,1,512]{2,1,0:T(1,128)S(1)} %bitcast.103), channel_id=1, replica_groups=mesh['batch'=4,'ctx'=16,'head'=4] {'ctx'}, dimensions={0}, use_global_device_ids=true | all-gather | bytes 34816 | tf_op jit(solution)/shard_map/all_gather | solution.py:141
  137.2 0.6 gather_fusion
  138.6 0.6 and_convert_fusion.need_ref
  139.4 3.4 %collective-permute-start.5 = (bf16[2,4,512,128]{3,2,1,0:T(8,128)(2,1)S(1)}, bf16[2,4,512,128]{3,2,1,0:T(8,128)(2,1)S(1)}, u32[]{:S(2)}, u32[]{:S(2)}) collective-permute-start(bf16[2,4,512,128]{3,2,1,0:T(8,128)(2,1)S(1)} %get-tuple-element.16), channel_id=1, source_target_pairs={{0,4},{4,8},{8,12},{12,16},{16,20},{20,24},{24,28},{28,32},{32,36}... | collective-permute-start | bytes 3145736 | tf_op jit(solution)/shard_map/ppermute | solution.py:132
  142.9 1.3 collective-permute-start.6
  144.5 0.9 slice_bitcast_fusion.2.q_ref
  145.4 9.1 %collective-permute-done.5 = bf16[2,4,512,128]{3,2,1,0:T(8,128)(2,1)S(1)} collective-permute-done((bf16[2,4,512,128]{3,2,1,0:T(8,128)(2,1)S(1)}, bf16[2,4,512,128]{3,2,1,0:T(8,128)(2,1)S(1)}, u32[]{:S(2)}, u32[]{:S(2)}) %collective-permute-start.5) | collective-permute-done | bytes 1048608 | tf_op jit(solution)/shard_map/ppermute | solution.py:132
  154.6 3.8 %collective-permute-done.6 = bf16[2,4,512,128]{3,2,1,0:T(8,128)(2,1)S(1)} collective-permute-done((bf16[2,4,512,128]{3,2,1,0:T(8,128)(2,1)S(1)}, bf16[2,4,512,128]{3,2,1,0:T(8,128)(2,1)S(1)}, u32[]{:S(2)}, u32[]{:S(2)}) %collective-permute-start.6) | collective-permute-done | bytes 1048608 | tf_op jit(solution)/shard_map/ppermute | solution.py:135
  158.8 2.0 slice_bitcast_fusion
  160.8 44.8 %shard_map.100 = bf16[5,512,128]{2,1,0:T(8,128)(2,1)} custom-call(s32[45]{0:T(128)} %and_convert_fusion.need_ref, s32[5]{0:T(128)} %and_select_fusion.1.qp_ref, s32[45]{0:T(128)} %add.331.kt_ref, s32[45]{0:T(128)} %and_select_fusion.kp_ref, bf16[5,512,128]{2,1,0:T(8,128)(2,1)} %slice_bitcast_fusion.2.q_ref, bf16[13,512,128]{2,1,0:T(8,128)(2,1)} %get-tuple-element.10.k_ref, ...), custom_call_target="tpu_custom_call" | custom-call | tf_op jit(solution)/shard_map/pallas_call | solution.py:74
  205.6 7.5 %scatter_custom_fusion.1 = bf16[2560,128]{1,0:T(8,128)(2,1)S(1)} fusion(s32[2560]{0:T(1024)S(1)} %reshape.455, bf16[2560,128]{1,0:T(8,128)(2,1)} %bitcast.93, bf16[]{:T(256)} %constant.171.clone.1), kind=kCustom, calls=%fused_computation.33 | custom fusion | bytes 655872
  213.2 30.0 %all_to_all.5 = bf16[16,5,32,128]{3,2,1,0:T(8,128)(2,1)S(1)} all-to-all(bf16[16,5,32,128]{3,2,1,0:T(8,128)(2,1)S(1)} %copy.55), channel_id=1, replica_groups=mesh['batch'=4,'ctx'=16,'head'=4] {'ctx'}, dimensions={0} | all-to-all | bytes 1310720 | tf_op jit(solution)/shard_map/all_to_all | solution.py:176
  243.7 8.9 %convolution_convert_fusion = bf16[512,5120]{1,0:T(8,128)(2,1)} fusion(bf16[640,5120]{1,0:T(8,128)(2,1)} %param.18, bf16[64,8,5,128]{3,2,1,0:T(8,128)(2,1)S(1)} %bitcast.91), kind=kOutput, calls=%fused_computation.7 | convolution fusion | flops 3358064640 | bytes 12451840 | tf_op jit(solution)/shard_map/dot_general | solution.py:183
  252.6 30.7 %scatter_custom_fusion = s32[8192]{0:T(1024)S(1)} fusion(s32[8192]{0:T(1024)S(1)} %compare_select_fusion, s32[8192]{0:T(1024)} %bitcast.94, s32[]{:T(128)} %constant.175.clone.1), kind=kCustom, calls=%fused_computation.56 | custom fusion | bytes 33280 | tf_op jit(solution)/shard_map/scatter | solution.py:180
  283.6 38.0 %reduce-scatter.2.cloned.1.call-done = bf16[512,1280]{1,0:T(8,128)(2,1)} async-done(((bf16[512,5120]{1,0:T(8,128)(2,1)}), bf16[512,1280]{1,0:T(8,128)(2,1)}) %reduce-scatter.2.cloned.1.call-update) | async-done | bytes 1310736 | tf_op jit(solution)/shard_map/reduce_scatter | solution.py:184
  321.6 3.6 %fusion = bf16[512,1280]{1,0:T(8,128)(2,1)} fusion(f32[6,1280]{1,0:T(8,128)S(1)} %fusion.21, bf16[512,1280]{1,0:T(8,128)(2,1)} %reduce-scatter.2.cloned.1.call-done, s32[512]{0:T(512)S(1)} %dynamic_slice.9), kind=kOutput, calls=%fused_computation.10 | convolution fusion | flops 49155072 | bytes 2654208 | tf_op jit(solution)/shard_map/dot_general | solution.py:192
  (85 shorter events, 6.8 us)
Async XLA Ops:
  6.5 276.8 %copy-start = (f32[50,1280]{1,0:T(8,128)S(1)}, f32[50,1280]{1,0:T(8,128)}, u32[]{:S(2)}) copy-start(f32[50,1280]{1,0:T(8,128)} %param.19) | copy-start | bytes 768004
  6.5 1.7 copy-start.1
  6.5 315.1 %reduce-scatter.2.cloned.1.call-start = ((), (), s32[]{:S(2)}) async-start(), calls=%async_computation.2 | async-start | bytes 6553600 | tf_op jit(solution)/shard_map/reduce_scatter | solution.py:184
  6.5 2.1 copy-start.2
  8.0 10.5 %copy-start.4 = (f32[640]{0:T(1024)S(1)}, f32[640]{0:T(1024)}, u32[]{:S(2)}) copy-start(f32[640]{0:T(1024)} %param.13) | copy-start | bytes 7684
  8.5 10.3 %copy-start.5 = (f32[640]{0:T(1024)S(1)}, f32[640]{0:T(1024)}, u32[]{:S(2)}) copy-start(f32[640]{0:T(1024)} %param.14) | copy-start | bytes 7684
  19.4 22.3 %copy-start.6 = (s32[512]{0:T(512)S(1)}, s32[512]{0:T(512)}, u32[]{:S(2)}) copy-start(s32[512]{0:T(512)} %param.15) | copy-start | bytes 6148
  19.6 119.6 %collective-permute-start.1 = (bf16[3,512,128]{2,1,0:T(8,128)(2,1)S(1)}, bf16[3,512,128]{2,1,0:T(8,128)(2,1)S(1)}, u32[]{:S(2)}, u32[]{:S(2)}) collective-permute-start(bf16[3,512,128]{2,1,0:T(8,128)(2,1)S(1)} %bitcast.95), channel_id=1, source_target_pairs={{4,0},{24,4},{44,8},{0,12},{20,16},{40,20},{60,24},{16,28},{36,32}... | collective-permute-start | bytes 1179656 | tf_op jit(solution)/shard_map/ppermute | solution.py:128
  24.2 114.9 %collective-permute-start.2 = (bf16[3,512,128]{2,1,0:T(8,128)(2,1)S(1)}, bf16[3,512,128]{2,1,0:T(8,128)(2,1)S(1)}, u32[]{:S(2)}, u32[]{:S(2)}) collective-permute-start(bf16[3,512,128]{2,1,0:T(8,128)(2,1)S(1)} %bitcast.96), channel_id=1, source_target_pairs={{8,0},{28,4},{48,8},{4,12},{24,16},{44,20},{0,24},{20,28},{40,32},... | collective-permute-start | bytes 1179656 | tf_op jit(solution)/shard_map/ppermute | solution.py:128
  26.2 112.9 %collective-permute-start.3 = (bf16[3,512,128]{2,1,0:T(8,128)(2,1)S(1)}, bf16[3,512,128]{2,1,0:T(8,128)(2,1)S(1)}, u32[]{:S(2)}, u32[]{:S(2)}) collective-permute-start(bf16[3,512,128]{2,1,0:T(8,128)(2,1)S(1)} %bitcast.97), channel_id=1, source_target_pairs={{12,0},{32,4},{52,8},{8,12},{28,16},{48,20},{4,24},{24,28},{44,32}... | collective-permute-start | bytes 1179656 | tf_op jit(solution)/shard_map/ppermute | solution.py:128
  28.3 110.9 %collective-permute-start.4 = (bf16[3,512,128]{2,1,0:T(8,128)(2,1)}, bf16[3,512,128]{2,1,0:T(8,128)(2,1)S(1)}, u32[]{:S(2)}, u32[]{:S(2)}) collective-permute-start(bf16[3,512,128]{2,1,0:T(8,128)(2,1)} %bitcast.98), channel_id=1, source_target_pairs={{16,0},{36,4},{56,8},{12,12},{32,16},{52,20},{8,24},{28,28},{48,32... | collective-permute-start | bytes 1179656 | tf_op jit(solution)/shard_map/ppermute | solution.py:128
  39.9 99.3 %collective-permute-start = (bf16[3,512,128]{2,1,0:T(8,128)(2,1)}, bf16[3,512,128]{2,1,0:T(8,128)(2,1)S(1)}, u32[]{:S(2)}, u32[]{:S(2)}) collective-permute-start(bf16[3,512,128]{2,1,0:T(8,128)(2,1)} %bitcast.99), channel_id=1, source_target_pairs={{0,0},{20,4},{40,8},{60,12},{16,16},{36,20},{56,24},{12,28},{32,32... | collective-permute-start | bytes 1179656 | tf_op jit(solution)/shard_map/ppermute | solution.py:128
  100.4 3.8 %copy-start.3 = (s32[16,1,512]{2,1,0:T(1,128)}, s32[16,1,512]{2,1,0:T(1,128)S(1)}, u32[]{:S(2)}) copy-start(s32[16,1,512]{2,1,0:T(1,128)S(1)} %all-gather.1.ks_ref) | copy-start | bytes 98308
  105.5 3.0 copy-start.7
  105.5 32.4 %copy-start.10 = (s32[2]{0:T(128)S(1)}, s32[2]{0:T(128)}, u32[]{:S(2)}) copy-start(s32[2]{0:T(128)} %constant.199) | copy-start | bytes 28
  105.5 32.4 %copy-start.9 = (s32[2]{0:T(128)S(1)}, s32[2]{0:T(128)}, u32[]{:S(2)}) copy-start(s32[2]{0:T(128)} %constant.202) | copy-start | bytes 28
  139.4 15.1 %collective-permute-start.5 = (bf16[2,4,512,128]{3,2,1,0:T(8,128)(2,1)S(1)}, bf16[2,4,512,128]{3,2,1,0:T(8,128)(2,1)S(1)}, u32[]{:S(2)}, u32[]{:S(2)}) collective-permute-start(bf16[2,4,512,128]{3,2,1,0:T(8,128)(2,1)S(1)} %get-tuple-element.16), channel_id=1, source_target_pairs={{0,4},{4,8},{8,12},{12,16},{16,20},{20,24},{24,28},{28,32},{32,36}... | collective-permute-start | bytes 3145736 | tf_op jit(solution)/shard_map/ppermute | solution.py:132
  142.9 15.5 %collective-permute-start.6 = (bf16[2,4,512,128]{3,2,1,0:T(8,128)(2,1)S(1)}, bf16[2,4,512,128]{3,2,1,0:T(8,128)(2,1)S(1)}, u32[]{:S(2)}, u32[]{:S(2)}) collective-permute-start(bf16[2,4,512,128]{3,2,1,0:T(8,128)(2,1)S(1)} %get-tuple-element.17), channel_id=1, source_target_pairs={{4,0},{8,4},{12,8},{16,12},{20,16},{24,20},{28,24},{32,28},{36,32}... | collective-permute-start | bytes 3145736 | tf_op jit(solution)/shard_map/ppermute | solution.py:135
  252.6 30.8 %copy-start.8 = (s32[6]{0:T(128)S(1)}, s32[6]{0:T(128)}, u32[]{:S(2)}) copy-start(s32[6]{0:T(128)} %param.17) | copy-start | bytes 76
Sparse Core Ops, SparseCore 0:
  252.7 68.8 reduce-scatter.1

commit v2 on v1

--- a/solution.py
+++ b/solution.py
@@ -79,6 +79,16 @@
             dimension_semantics=("arbitrary", "arbitrary")
         ),
     )(need, qp, kt, kp, q_tiles, k_tiles, v_tiles, seg_rows, seg_cols)
+
+
+def doubling_gather(piece, me, size):
+    held = piece[None]
+    shift = 1
+    while shift < size:
+        came = lax.ppermute(held, "ctx", [(e, (e + shift) % size) for e in range(size)])
+        held = jnp.concatenate([came, held], axis=0)
+        shift *= 2
+    return jnp.roll(held, me + 1, axis=0)
 
 
 def local(
@@ -103,6 +113,9 @@
     tiles = head_count * ctx_size
     slots = tiles // ctx_size
 
+    marks = doubling_gather(jnp.stack([segment, destination]), me, ctx_size)
+    seg_blocks = marks[:, 0]
+    dest_blocks = marks[:, 1]
     query_float = query_raw.astype(jnp.float32)
     key_float = key_raw.astype(jnp.float32)
     query_sum, key_sum = lax.psum(
@@ -137,9 +150,6 @@
     )
     kv_all = jnp.concatenate([left, kv_own, right], axis=1)
 
-    seg_all = lax.all_gather(segment, "ctx", axis=0, tiled=True)
-    dest_all = lax.all_gather(destination, "ctx", axis=0, tiled=True)
-    seg_blocks = seg_all.reshape(ctx_size, row_count)
     seg_lo = seg_blocks[:, 0]
     seg_hi = seg_blocks[:, -1]
 
@@ -168,17 +178,27 @@
     )
 
     slot_count = row_count // ctx_size
-    dest_blocks = dest_all.reshape(ctx_size, row_count)
     dest_mine = dest_blocks[qp]
     place = (dest_mine // row_count) * slot_count + dest_mine % slot_count
-    placed = jnp.zeros_like(attended).at[jj, place].set(attended)
+    chooser = (
+        place[:, None, :] == jnp.arange(row_count, dtype=jnp.int32)[None, :, None]
+    ).astype(jnp.bfloat16)
+    placed = jnp.einsum(
+        "jsr,jrd->jsd", chooser, attended, preferred_element_type=jnp.float32
+    ).astype(jnp.bfloat16)
     placed = placed.reshape(slots, ctx_size, slot_count, HD).transpose(1, 0, 2, 3)
     got = lax.all_to_all(placed, "ctx", split_axis=0, concat_axis=0, tiled=True)
     got = got.reshape(head_count, ctx_size, slot_count, HD).transpose(1, 2, 0, 3)
     owned_attended = got.reshape(row_count, row_width)
 
-    owned_video_all = jnp.zeros_like(seg_all).at[dest_all].set(seg_all)
-    owned_video = lax.dynamic_slice_in_dim(owned_video_all, me * row_count, row_count)
+    wanted = (
+        me * row_count
+        + jnp.arange(ctx_size, dtype=jnp.int32)[:, None, None] * slot_count
+        + jnp.arange(slot_count, dtype=jnp.int32)[None, :, None]
+    )
+    owned_video = jnp.sum(
+        jnp.where(dest_blocks[:, None, :] == wanted, seg_blocks[:, None, :], 0), axis=2
+    ).reshape(row_count)
 
     head_terms = jnp.dot(owned_attended, out_weight, preferred_element_type=jnp.float32)
     mixed_rows = lax.psum_scatter(

time: 333 us -> 295 us (0.89)
  blocking collectives: 127 us -> 46 us
  waiting for transfers between devices: 51 us -> 124 us
  local copies, waits for them, and re-layouts: 54.6 us -> 18.8 us
    all_gather x2 -> x0, blocking collectives: 87.4 us -> none  [the longest x1 58.7 us: local(): seg_all = lax.all_gather(segment, 'ctx', axis=0, tiled=True)]
    ppermute x0 -> x4, waiting for transfers between devices: none -> 40.2 us  [doubling_gather(): lax.ppermute(held, 'ctx', [(e, (e + shift) % size) for e in range(size)])]
    scatter x1 -> x0, local copies, waits for them, and re-layouts: 30.7 us -> none  [local(): owned_video_all = jnp.zeros_like(seg_all).at[dest_all].set(seg_all)]
    reduce_scatter x1, waiting for transfers between devices: 38 us -> 50.3 us  [local(): lax.psum_scatter(head_terms.astype(jnp.bfloat16), 'head', scatter_dimensi...]
    ppermute x5, waiting for transfers between devices: 0.01 us -> 10.8 us  [local(): own.append(lax.ppermute(piece, 'ctx', perm))]
    ppermute x1, waiting for transfers between devices: 9.15 us -> 19.1 us  [local(): lax.ppermute(kv_own[:, slots - REACH:], 'ctx', [(e, e + 1) for e in range...]
    unnamed x33 -> x44, local copies, waits for them, and re-layouts: 9.75 us -> 2.79 us
    all_to_all x1, blocking collectives: 30 us -> 37 us  [local(): got = lax.all_to_all(placed, 'ctx', split_axis=0, concat_axis=0, tiled=True)]
  transfers between devices with their start and end apart: 8 -> 12, of which waited for: 3 -> 6; matrix products, arithmetic and copies ran while one was open for 13% -> 7% of each run, Pallas kernels for 0% -> 0%
where the time goes in v2:
time: 295 us; the launch traced here: 294 us
  waiting for transfers between devices  124 us (42%)
  blocking collectives  46 us (16%)
  Pallas kernels  44.8 us (15%)
  starting transfers between devices  25.1 us (9%)
  local copies, waits for them, and re-layouts  18.8 us (6%)
  matrix products  14.8 us (5%)
  between operations  13.9 us (5%)
  other arithmetic  6.39 us (2%)
    reduce_scatter x1, waiting for transfers between devices, local(): lax.psum_scatter(head_terms.astype(jnp.bfloat16), 'head', scatter_dimensi...  50.3 us
    pallas_call x1, Pallas kernels, flash(): pl.pallas_call(kern, grid_spec=grid_spec, out_shape=jax.ShapeDtypeStruct(...  44.8 us
    ppermute x4, waiting for transfers between devices, doubling_gather(): lax.ppermute(held, 'ctx', [(e, (e + shift) % size) for e in range(size)])  40.2 us
    all_to_all x1, blocking collectives, local(): got = lax.all_to_all(placed, 'ctx', split_axis=0, concat_axis=0, tiled=True)  37 us
    ppermute x1, waiting for transfers between devices, local(): lax.ppermute(kv_own[:, slots - REACH:], 'ctx', [(e, e + 1) for e in range...  19.1 us
    ppermute x5, starting transfers between devices, local(): own.append(lax.ppermute(piece, 'ctx', perm))  16.2 us
    ppermute x5, waiting for transfers between devices, local(): own.append(lax.ppermute(piece, 'ctx', perm))  10.8 us
    psum x1, blocking collectives, local(): lax.psum((jnp.sum(query_float * query_float, axis=1), jnp.sum(key_float *...  9.03 us
  transfers between devices with their start and end apart: 12, of which 6 were waited for; matrix products, arithmetic and copies ran while one was open for 7% of the time, Pallas kernels for 0%

profile of v2, /device:TPU:1, one launch (start us, length us, event | category | flops | bytes accessed | tf_op | source)
XLA Modules:
  0.0 294.1 jit_solution(13526813601386118827)
XLA Ops:
  6.5 0.8 add_bitcast_fusion
  7.3 2.5 collective-permute-start
  9.8 1.4 copy.26
  12.2 9.0 %all-reduce = (f32[512]{0:T(512)S(1)}, f32[512]{0:T(512)S(1)}) all-reduce(f32[512]{0:T(512)S(1)} %fusion.7, f32[512]{0:T(512)S(1)} %fusion.4), channel_id=1, replica_groups=mesh['batch'=4,'ctx'=16,'head'=4] {'head'}, use_global_device_ids=true, to_apply=%region_3.4 | all-reduce | flops 1024 | bytes 8192 | tf_op jit(solution)/shard_map/psum | solution.py:121
  22.3 0.7 collective-permute-start.4
  23.2 8.1 %collective-permute-start.5 = (bf16[3,512,128]{2,1,0:T(8,128)(2,1)S(1)}, bf16[3,512,128]{2,1,0:T(8,128)(2,1)S(1)}, u32[]{:S(2)}, u32[]{:S(2)}) collective-permute-start(bf16[3,512,128]{2,1,0:T(8,128)(2,1)S(1)} %bitcast.73), channel_id=1, source_target_pairs={{4,0},{24,4},{44,8},{0,12},{20,16},{40,20},{60,24},{16,28},{36,32}... | collective-permute-start | bytes 1179656 | tf_op jit(solution)/shard_map/ppermute | solution.py:141
  31.5 5.5 %collective-permute-start.6 = (bf16[3,512,128]{2,1,0:T(8,128)(2,1)S(1)}, bf16[3,512,128]{2,1,0:T(8,128)(2,1)S(1)}, u32[]{:S(2)}, u32[]{:S(2)}) collective-permute-start(bf16[3,512,128]{2,1,0:T(8,128)(2,1)S(1)} %bitcast.74), channel_id=1, source_target_pairs={{8,0},{28,4},{48,8},{4,12},{24,16},{44,20},{0,24},{20,28},{40,32},... | collective-permute-start | bytes 1179656 | tf_op jit(solution)/shard_map/ppermute | solution.py:141
  37.0 0.9 copy.32
  39.1 31.9 %collective-permute-done.1 = s32[2,2,512]{2,1,0:T(2,128)S(1)} collective-permute-done((s32[2,2,512]{2,1,0:T(2,128)S(1)}, s32[2,2,512]{2,1,0:T(2,128)S(1)}, u32[]{:S(2)}, u32[]{:S(2)}) %collective-permute-start.1) | collective-permute-done | bytes 8224 | tf_op jit(solution)/shard_map/ppermute | solution.py:88
  71.6 8.3 %collective-permute-done.2 = s32[4,2,512]{2,1,0:T(2,128)S(1)} collective-permute-done((s32[4,2,512]{2,1,0:T(2,128)S(1)}, s32[4,2,512]{2,1,0:T(2,128)S(1)}, u32[]{:S(2)}, u32[]{:S(2)}) %collective-permute-start.2) | collective-permute-done | bytes 16416 | tf_op jit(solution)/shard_map/ppermute | solution.py:88
  80.5 2.9 collective-permute-start.3
  85.9 0.9 copy.33
  86.8 1.9 collective-permute-start.8
  89.2 1.2 gather_fusion.4
  90.4 1.2 gather_fusion.1
  91.6 0.8 gather_fusion.3
  92.4 0.8 gather_fusion.2
  93.3 0.7 compare_and_fusion
  94.2 2.6 copy.34.qs_ref
  98.0 10.8 %collective-permute-done.8 = bf16[3,512,128]{2,1,0:T(8,128)(2,1)S(1)} collective-permute-done((bf16[3,512,128]{2,1,0:T(8,128)(2,1)}, bf16[3,512,128]{2,1,0:T(8,128)(2,1)S(1)}, u32[]{:S(2)}, u32[]{:S(2)}) %collective-permute-start.8) | collective-permute-done | bytes 393248 | tf_op jit(solution)/shard_map/ppermute | solution.py:141
  109.1 1.4 collective-permute-start.9
  110.4 1.5 collective-permute-start.10
  112.3 0.9 slice_bitcast_fusion.2.q_ref
  113.2 19.1 %collective-permute-done.9 = bf16[2,4,512,128]{3,2,1,0:T(8,128)(2,1)S(1)} collective-permute-done((bf16[2,4,512,128]{3,2,1,0:T(8,128)(2,1)S(1)}, bf16[2,4,512,128]{3,2,1,0:T(8,128)(2,1)S(1)}, u32[]{:S(2)}, u32[]{:S(2)}) %collective-permute-start.9) | collective-permute-done | bytes 1048608 | tf_op jit(solution)/shard_map/ppermute | solution.py:145
  132.3 3.9 %collective-permute-done.10 = bf16[2,4,512,128]{3,2,1,0:T(8,128)(2,1)S(1)} collective-permute-done((bf16[2,4,512,128]{3,2,1,0:T(8,128)(2,1)S(1)}, bf16[2,4,512,128]{3,2,1,0:T(8,128)(2,1)S(1)}, u32[]{:S(2)}, u32[]{:S(2)}) %collective-permute-start.10) | collective-permute-done | bytes 1048608 | tf_op jit(solution)/shard_map/ppermute | solution.py:148
  136.5 2.0 slice_bitcast_fusion
  138.5 44.8 %shard_map.100 = bf16[5,512,128]{2,1,0:T(8,128)(2,1)} custom-call(s32[45]{0:T(128)} %and_convert_fusion.need_ref, s32[5]{0:T(128)} %and_select_fusion.1.qp_ref, s32[45]{0:T(128)} %add.345.kt_ref, s32[45]{0:T(128)} %and_select_fusion.kp_ref, bf16[5,512,128]{2,1,0:T(8,128)(2,1)} %slice_bitcast_fusion.2.q_ref, bf16[13,512,128]{2,1,0:T(8,128)(2,1)} %get-tuple-element.10.k_ref, ...), custom_call_target="tpu_custom_call" | custom-call | tf_op jit(solution)/shard_map/pallas_call | solution.py:74
  183.4 2.0 fusion.3
  185.5 37.0 %all_to_all.5 = bf16[16,5,32,128]{3,2,1,0:T(8,128)(2,1)S(1)} all-to-all(bf16[16,5,32,128]{3,2,1,0:T(8,128)(2,1)S(1)} %bitcast.59), channel_id=1, replica_groups=mesh['batch'=4,'ctx'=16,'head'=4] {'ctx'}, dimensions={0} | all-to-all | bytes 1310720 | tf_op jit(solution)/shard_map/all_to_all | solution.py:190
  222.9 8.8 %convolution_convert_fusion = bf16[512,5120]{1,0:T(8,128)(2,1)} fusion(bf16[640,5120]{1,0:T(8,128)(2,1)} %param.18, bf16[64,8,5,128]{3,2,1,0:T(8,128)(2,1)S(1)} %bitcast.69), kind=kOutput, calls=%fused_computation.5 | convolution fusion | flops 3358064640 | bytes 12451840 | tf_op jit(solution)/shard_map/dot_general | solution.py:203
  233.2 50.3 %reduce-scatter.2.cloned.1.call-done = bf16[512,1280]{1,0:T(8,128)(2,1)} async-done(((bf16[512,5120]{1,0:T(8,128)(2,1)}), bf16[512,1280]{1,0:T(8,128)(2,1)}) %reduce-scatter.2.cloned.1.call-update) | async-done | bytes 1310736 | tf_op jit(solution)/shard_map/reduce_scatter | solution.py:204
  283.6 3.6 %fusion.1 = bf16[512,1280]{1,0:T(8,128)(2,1)} fusion(f32[6,1280]{1,0:T(8,128)S(1)} %fusion.19, bf16[512,1280]{1,0:T(8,128)(2,1)} %reduce-scatter.2.cloned.1.call-done, s32[512]{0:T(512)S(1)} %eq.97), kind=kOutput, calls=%fused_computation.10 | convolution fusion | flops 49155072 | bytes 2654208 | tf_op jit(solution)/shard_map/dot_general | solution.py:212
  (105 shorter events, 11.9 us)
Async XLA Ops:
  6.5 225.3 %copy-start = (f32[50,1280]{1,0:T(8,128)S(1)}, f32[50,1280]{1,0:T(8,128)}, u32[]{:S(2)}) copy-start(f32[50,1280]{1,0:T(8,128)} %param.19) | copy-start | bytes 768004
  6.5 4.9 %copy-start.1 = (bf16[512,640]{1,0:T(8,128)(2,1)S(1)}, bf16[512,640]{1,0:T(8,128)(2,1)}, u32[]{:S(2)}) copy-start(bf16[512,640]{1,0:T(8,128)(2,1)} %param.11) | copy-start | bytes 1966084
  6.5 277.0 %reduce-scatter.2.cloned.1.call-start = ((), (), s32[]{:S(2)}) async-start(), calls=%async_computation.2 | async-start | bytes 6553600 | tf_op jit(solution)/shard_map/reduce_scatter | solution.py:204
  7.3 31.6 %collective-permute-start = (s32[1,2,512]{2,1,0:T(2,128)S(1)}, s32[1,2,512]{2,1,0:T(2,128)S(1)}, u32[]{:S(2)}, u32[]{:S(2)}) collective-permute-start(s32[1,2,512]{2,1,0:T(2,128)S(1)} %add_bitcast_fusion), channel_id=1, source_target_pairs={{0,4},{4,8},{8,12},{12,16},{16,20},{20,24},{24,28},{28,32},{32,36}... | collective-permute-start | bytes 12296 | tf_op jit(solution)/shard_map/ppermute | solution.py:88
  9.8 2.1 copy-start.2
  11.2 10.0 %copy-start.6 = (f32[640]{0:T(1024)S(1)}, f32[640]{0:T(1024)}, u32[]{:S(2)}) copy-start(f32[640]{0:T(1024)} %param.14) | copy-start | bytes 7684
  11.7 9.7 %copy-start.7 = (f32[640]{0:T(1024)S(1)}, f32[640]{0:T(1024)}, u32[]{:S(2)}) copy-start(f32[640]{0:T(1024)} %param.13) | copy-start | bytes 7684
  22.0 66.8 %copy-start.4 = (s32[512]{0:T(512)S(1)}, s32[512]{0:T(512)}, u32[]{:S(2)}) copy-start(s32[512]{0:T(512)} %param.16) | copy-start | bytes 6148
  22.0 66.8 %copy-start.5 = (s32[512]{0:T(512)S(1)}, s32[512]{0:T(512)}, u32[]{:S(2)}) copy-start(s32[512]{0:T(512)} %param.15) | copy-start | bytes 6148
  22.3 75.7 %collective-permute-start.4 = (bf16[3,512,128]{2,1,0:T(8,128)(2,1)S(1)}, bf16[3,512,128]{2,1,0:T(8,128)(2,1)S(1)}, u32[]{:S(2)}, u32[]{:S(2)}) collective-permute-start(bf16[3,512,128]{2,1,0:T(8,128)(2,1)S(1)} %bitcast.72), channel_id=1, source_target_pairs={{0,0},{20,4},{40,8},{60,12},{16,16},{36,20},{56,24},{12,28},{32,32... | collective-permute-start | bytes 1179656 | tf_op jit(solution)/shard_map/ppermute | solution.py:141
  23.2 74.8 %collective-permute-start.5 = (bf16[3,512,128]{2,1,0:T(8,128)(2,1)S(1)}, bf16[3,512,128]{2,1,0:T(8,128)(2,1)S(1)}, u32[]{:S(2)}, u32[]{:S(2)}) collective-permute-start(bf16[3,512,128]{2,1,0:T(8,128)(2,1)S(1)} %bitcast.73), channel_id=1, source_target_pairs={{4,0},{24,4},{44,8},{0,12},{20,16},{40,20},{60,24},{16,28},{36,32}... | collective-permute-start | bytes 1179656 | tf_op jit(solution)/shard_map/ppermute | solution.py:141
  31.5 66.5 %collective-permute-start.6 = (bf16[3,512,128]{2,1,0:T(8,128)(2,1)S(1)}, bf16[3,512,128]{2,1,0:T(8,128)(2,1)S(1)}, u32[]{:S(2)}, u32[]{:S(2)}) collective-permute-start(bf16[3,512,128]{2,1,0:T(8,128)(2,1)S(1)} %bitcast.74), channel_id=1, source_target_pairs={{8,0},{28,4},{48,8},{4,12},{24,16},{44,20},{0,24},{20,28},{40,32},... | collective-permute-start | bytes 1179656 | tf_op jit(solution)/shard_map/ppermute | solution.py:141
  37.9 60.1 %collective-permute-start.7 = (bf16[3,512,128]{2,1,0:T(8,128)(2,1)}, bf16[3,512,128]{2,1,0:T(8,128)(2,1)S(1)}, u32[]{:S(2)}, u32[]{:S(2)}) collective-permute-start(bf16[3,512,128]{2,1,0:T(8,128)(2,1)} %bitcast.75), channel_id=1, source_target_pairs={{12,0},{32,4},{52,8},{8,12},{28,16},{48,20},{4,24},{24,28},{44,32}... | collective-permute-start | bytes 1179656 | tf_op jit(solution)/shard_map/ppermute | solution.py:141
  38.3 0.6 copy-start.8
  38.9 32.1 %collective-permute-start.1 = (s32[2,2,512]{2,1,0:T(2,128)S(1)}, s32[2,2,512]{2,1,0:T(2,128)S(1)}, u32[]{:S(2)}, u32[]{:S(2)}) collective-permute-start(s32[2,2,512]{2,1,0:T(2,128)S(1)} %pad_add_fusion.2), channel_id=1, source_target_pairs={{0,8},{4,12},{8,16},{12,20},{16,24},{20,28},{24,32},{28,36},{32,40... | collective-permute-start | bytes 24584 | tf_op jit(solution)/shard_map/ppermute | solution.py:88
  71.0 8.9 %collective-permute-start.2 = (s32[4,2,512]{2,1,0:T(2,128)S(1)}, s32[4,2,512]{2,1,0:T(2,128)S(1)}, u32[]{:S(2)}, u32[]{:S(2)}) collective-permute-start(s32[4,2,512]{2,1,0:T(2,128)S(1)} %pad_add_fusion.1), channel_id=1, source_target_pairs={{0,16},{4,20},{8,24},{12,28},{16,32},{20,36},{24,40},{28,44},{32,4... | collective-permute-start | bytes 49160 | tf_op jit(solution)/shard_map/ppermute | solution.py:88
  80.5 6.3 %collective-permute-start.3 = (s32[8,2,512]{2,1,0:T(2,128)}, s32[8,2,512]{2,1,0:T(2,128)S(1)}, u32[]{:S(2)}, u32[]{:S(2)}) collective-permute-start(s32[8,2,512]{2,1,0:T(2,128)} %pad_add_fusion), channel_id=1, source_target_pairs={{0,32},{4,36},{8,40},{12,44},{16,48},{20,52},{24,56},{28,60},{32,0... | collective-permute-start | bytes 98312 | tf_op jit(solution)/shard_map/ppermute | solution.py:88
  86.8 22.0 %collective-permute-start.8 = (bf16[3,512,128]{2,1,0:T(8,128)(2,1)}, bf16[3,512,128]{2,1,0:T(8,128)(2,1)S(1)}, u32[]{:S(2)}, u32[]{:S(2)}) collective-permute-start(bf16[3,512,128]{2,1,0:T(8,128)(2,1)} %bitcast.76), channel_id=1, source_target_pairs={{16,0},{36,4},{56,8},{12,12},{32,16},{52,20},{8,24},{28,28},{48,32... | collective-permute-start | bytes 1179656 | tf_op jit(solution)/shard_map/ppermute | solution.py:141
  89.0 5.2 %copy-start.3 = (s32[16,1,512]{2,1,0:T(1,128)}, s32[16,1,512]{2,1,0:T(1,128)S(1)}, u32[]{:S(2)}) copy-start(s32[16,1,512]{2,1,0:T(1,128)S(1)} %get-tuple-element.19.ks_ref) | copy-start | bytes 98308
  92.4 0.9 copy-start.11
  94.2 3.2 %copy-start.9 = (s32[45]{0:T(128)S(1)}, s32[45]{0:T(128)}, u32[]{:S(2)}) copy-start(s32[45]{0:T(128)} %copy-done.8) | copy-start | bytes 544
  94.2 3.2 %copy-start.10 = (s32[45]{0:T(128)S(1)}, s32[45]{0:T(128)}, u32[]{:S(2)}) copy-start(s32[45]{0:T(128)} %eq.92) | copy-start | bytes 544
  94.2 3.2 %copy-start.13 = (pred[45]{0:T(512)(128)(4,1)S(1)}, pred[45]{0:T(512)(128)(4,1)}, u32[]{:S(2)}) copy-start(pred[45]{0:T(512)(128)(4,1)} %and.170) | copy-start | bytes 139
  109.1 23.2 %collective-permute-start.9 = (bf16[2,4,512,128]{3,2,1,0:T(8,128)(2,1)S(1)}, bf16[2,4,512,128]{3,2,1,0:T(8,128)(2,1)S(1)}, u32[]{:S(2)}, u32[]{:S(2)}) collective-permute-start(bf16[2,4,512,128]{3,2,1,0:T(8,128)(2,1)S(1)} %get-tuple-element.16), channel_id=1, source_target_pairs={{0,4},{4,8},{8,12},{12,16},{16,20},{20,24},{24,28},{28,32},{32,36}... | collective-permute-start | bytes 3145736 | tf_op jit(solution)/shard_map/ppermute | solution.py:145
  110.4 25.7 %collective-permute-start.10 = (bf16[2,4,512,128]{3,2,1,0:T(8,128)(2,1)S(1)}, bf16[2,4,512,128]{3,2,1,0:T(8,128)(2,1)S(1)}, u32[]{:S(2)}, u32[]{:S(2)}) collective-permute-start(bf16[2,4,512,128]{3,2,1,0:T(8,128)(2,1)S(1)} %get-tuple-element.17), channel_id=1, source_target_pairs={{4,0},{8,4},{12,8},{16,12},{20,16},{24,20},{28,24},{32,28},{36,32}... | collective-permute-start | bytes 3145736 | tf_op jit(solution)/shard_map/ppermute | solution.py:148
  231.7 0.7 copy-start.12
Sparse Core Ops, SparseCore 0:
  231.9 51.6 reduce-scatter.1

commit v3 on v2

--- a/solution.py
+++ b/solution.py
@@ -14,17 +14,21 @@
 
 def flash_kernel(
     need_ref, qp_ref, kt_ref, kp_ref,
-    q_ref, k_ref, v_ref, qs_ref, ks_ref,
-    o_ref, m_scr, l_scr, acc_scr, *, offsets, score_scale
+    q_ref, k_ref, v_ref, qs_ref, ks_ref, m_in, l_in, acc_in,
+    *refs, offsets, score_scale, last
 ):
+    if last:
+        o_ref, m_scr, l_scr, acc_scr = refs
+    else:
+        m_scr, l_scr, acc_scr = refs
     j = pl.program_id(0)
     o = pl.program_id(1)
 
     @pl.when(o == 0)
     def _():
-        m_scr[...] = jnp.full_like(m_scr, -1e30)
-        l_scr[...] = jnp.zeros_like(l_scr)
-        acc_scr[...] = jnp.zeros_like(acc_scr)
+        m_scr[0] = m_in[0]
+        l_scr[0] = l_in[0]
+        acc_scr[0] = acc_in[0]
 
     @pl.when(need_ref[j * offsets + o] != 0)
     def _():
@@ -35,50 +39,72 @@
         ) * score_scale
         mask = qs_ref[0] == ks_ref[0]
         s = jnp.where(mask, s, -1e30)
-        m_prev = m_scr[...]
+        m_prev = m_scr[0]
         m_new = jnp.maximum(m_prev, jnp.max(s, axis=1, keepdims=True))
         alpha = jnp.exp(m_prev - m_new)
         p = jnp.where(mask, jnp.exp(s - m_new), 0.0)
-        l_scr[...] = alpha * l_scr[...] + jnp.sum(p, axis=1, keepdims=True)
-        acc_scr[...] = alpha * acc_scr[...] + jnp.dot(
+        l_scr[0] = alpha * l_scr[0] + jnp.sum(p, axis=1, keepdims=True)
+        acc_scr[0] = alpha * acc_scr[0] + jnp.dot(
             p.astype(jnp.bfloat16), v_ref[0], preferred_element_type=jnp.float32
         )
-        m_scr[...] = m_new
-
-    @pl.when(o == offsets - 1)
-    def _():
-        o_ref[0] = (acc_scr[...] / l_scr[...]).astype(o_ref.dtype)
-
-
-def flash(need, qp, kt, kp, q_tiles, k_tiles, v_tiles, seg_rows, seg_cols, score_scale):
+        m_scr[0] = m_new
+
+    if last:
+        @pl.when(o == offsets - 1)
+        def _():
+            o_ref[0] = (acc_scr[0] / l_scr[0]).astype(o_ref.dtype)
+
+
+def flash(need, qp, kt, kp, q_tiles, k_tiles, v_tiles, seg_rows, seg_cols, carry, score_scale, last, work):
     slots, rows, width = q_tiles.shape
     offsets = 2 * REACH + 1
-    kern = functools.partial(flash_kernel, offsets=offsets, score_scale=score_scale)
+    kern = functools.partial(flash_kernel, offsets=offsets, score_scale=score_scale, last=last)
+    tile = pl.BlockSpec((1, rows, width), lambda j, o, nd, qp, kt, kp: (j, 0, 0))
+    column = pl.BlockSpec((1, rows, 1), lambda j, o, nd, qp, kt, kp: (j, 0, 0))
+    carry_specs = [column, column, tile]
+    carry_shapes = [
+        jax.ShapeDtypeStruct((slots, rows, 1), jnp.float32),
+        jax.ShapeDtypeStruct((slots, rows, 1), jnp.float32),
+        jax.ShapeDtypeStruct((slots, rows, width), jnp.float32),
+    ]
+    if last:
+        out_specs = tile
+        out_shape = jax.ShapeDtypeStruct((slots, rows, width), jnp.bfloat16)
+        scratch = [
+            pltpu.VMEM((1, rows, 1), jnp.float32),
+            pltpu.VMEM((1, rows, 1), jnp.float32),
+            pltpu.VMEM((1, rows, width), jnp.float32),
+        ]
+    else:
+        out_specs = carry_specs
+        out_shape = carry_shapes
+        scratch = []
     grid_spec = pltpu.PrefetchScalarGridSpec(
         num_scalar_prefetch=4,
         grid=(slots, offsets),
         in_specs=[
-            pl.BlockSpec((1, rows, width), lambda j, o, nd, qp, kt, kp: (j, 0, 0)),
+            tile,
             pl.BlockSpec((1, rows, width), lambda j, o, nd, qp, kt, kp: (kt[j * offsets + o], 0, 0)),
             pl.BlockSpec((1, rows, width), lambda j, o, nd, qp, kt, kp: (kt[j * offsets + o], 0, 0)),
             pl.BlockSpec((1, rows, 1), lambda j, o, nd, qp, kt, kp: (qp[j], 0, 0)),
             pl.BlockSpec((1, 1, rows), lambda j, o, nd, qp, kt, kp: (kp[j * offsets + o], 0, 0)),
-        ],
-        out_specs=pl.BlockSpec((1, rows, width), lambda j, o, nd, qp, kt, kp: (j, 0, 0)),
-        scratch_shapes=[
-            pltpu.VMEM((rows, 1), jnp.float32),
-            pltpu.VMEM((rows, 1), jnp.float32),
-            pltpu.VMEM((rows, width), jnp.float32),
-        ],
+        ] + carry_specs,
+        out_specs=out_specs,
+        scratch_shapes=scratch,
     )
     return pl.pallas_call(
         kern,
         grid_spec=grid_spec,
-        out_shape=jax.ShapeDtypeStruct((slots, rows, width), jnp.bfloat16),
+        out_shape=out_shape,
         compiler_params=pltpu.CompilerParams(
             dimension_semantics=("arbitrary", "arbitrary")
         ),
-    )(need, qp, kt, kp, q_tiles, k_tiles, v_tiles, seg_rows, seg_cols)
+        cost_estimate=pl.CostEstimate(
+            flops=work * rows * rows * width * 4,
+            transcendentals=work * rows * rows,
+            bytes_accessed=work * rows * width * 4,
+        ),
+    )(need, qp, kt, kp, q_tiles, k_tiles, v_tiles, seg_rows, seg_cols, *carry)
 
 
 def doubling_gather(piece, me, size):
@@ -164,17 +190,30 @@
     p_k = t_kc % ctx_size
     same_head = (t_kc // ctx_size) == (t_q // ctx_size)
     meet = (seg_lo[p_q] <= seg_hi[p_k]) & (seg_lo[p_k] <= seg_hi[p_q])
-    need = (valid & same_head & meet).astype(jnp.int32).reshape(-1)
     kt = (jj + oo + REACH).astype(jnp.int32).reshape(-1)
     qp = p_q[:, 0].astype(jnp.int32)
     kp = p_k.astype(jnp.int32).reshape(-1)
 
+    kt_own = jj + oo
+    is_own = (kt_own >= 0) & (kt_own < slots)
+    need_all = valid & same_head & meet
+    need_own = (need_all & is_own).astype(jnp.int32).reshape(-1)
+    need_far = (need_all & ~is_own).astype(jnp.int32).reshape(-1)
+    kt_near = jnp.clip(kt_own, 0, slots - 1).astype(jnp.int32).reshape(-1)
+    seg_rows = seg_blocks.reshape(ctx_size, row_count, 1)
+    seg_cols = seg_blocks.reshape(ctx_size, 1, row_count)
+    carry = (
+        jnp.full((slots, row_count, 1), -1e30, jnp.float32),
+        jnp.zeros((slots, row_count, 1), jnp.float32),
+        jnp.zeros((slots, row_count, HD), jnp.float32),
+    )
+    carry = flash(
+        need_own, qp, kt_near, kp, own[0], own[1], own[2], seg_rows, seg_cols, carry,
+        score_scale, False, 15,
+    )
     attended = flash(
-        need, qp, kt, kp,
-        own[0], kv_all[0], kv_all[1],
-        seg_blocks.reshape(ctx_size, row_count, 1),
-        seg_blocks.reshape(ctx_size, 1, row_count),
-        score_scale,
+        need_far, qp, kt, kp, own[0], kv_all[0], kv_all[1], seg_rows, seg_cols, carry,
+        score_scale, True, 15,
     )
 
     slot_count = row_count // ctx_size
@@ -187,9 +226,6 @@
         "jsr,jrd->jsd", chooser, attended, preferred_element_type=jnp.float32
     ).astype(jnp.bfloat16)
     placed = placed.reshape(slots, ctx_size, slot_count, HD).transpose(1, 0, 2, 3)
-    got = lax.all_to_all(placed, "ctx", split_axis=0, concat_axis=0, tiled=True)
-    got = got.reshape(head_count, ctx_size, slot_count, HD).transpose(1, 2, 0, 3)
-    owned_attended = got.reshape(row_count, row_width)
 
     wanted = (
         me * row_count
@@ -198,23 +234,33 @@
     )
     owned_video = jnp.sum(
         jnp.where(dest_blocks[:, None, :] == wanted, seg_blocks[:, None, :], 0), axis=2
-    ).reshape(row_count)
-
-    head_terms = jnp.dot(owned_attended, out_weight, preferred_element_type=jnp.float32)
-    mixed_rows = lax.psum_scatter(
-        head_terms.astype(jnp.bfloat16), "head", scatter_dimension=1, tiled=True
-    ).astype(jnp.float32)
+    )
     video_gates = jnp.dot(
         jax.nn.one_hot(timestep, gate_table.shape[0], dtype=jnp.float32),
         gate_table,
         precision=lax.Precision.HIGHEST,
     )
-    token_gates = jnp.dot(
-        jax.nn.one_hot(owned_video, timestep.shape[0], dtype=jnp.float32),
-        video_gates,
-        precision=lax.Precision.HIGHEST,
-    )
-    return (mixed_rows * token_gates).astype(jnp.bfloat16)
+    halves = 2
+    part = slot_count // halves
+    results = []
+    for half in range(halves):
+        piece = placed[:, :, half * part:(half + 1) * part]
+        got = lax.all_to_all(piece, "ctx", split_axis=0, concat_axis=0, tiled=True)
+        got = got.reshape(head_count, ctx_size, part, HD).transpose(1, 2, 0, 3)
+        owned_attended = got.reshape(ctx_size * part, row_width)
+        head_terms = jnp.dot(owned_attended, out_weight, preferred_element_type=jnp.float32)
+        mixed_rows = lax.psum_scatter(
+            head_terms.astype(jnp.bfloat16), "head", scatter_dimension=1, tiled=True
+        ).astype(jnp.float32)
+        videos = owned_video[:, half * part:(half + 1) * part].reshape(-1)
+        token_gates = jnp.dot(
+            jax.nn.one_hot(videos, timestep.shape[0], dtype=jnp.float32),
+            video_gates,
+            precision=lax.Precision.HIGHEST,
+        )
+        gated = (mixed_rows * token_gates).astype(jnp.bfloat16)
+        results.append(gated.reshape(ctx_size, part, -1))
+    return jnp.concatenate(results, axis=1).reshape(row_count, -1)
 
 
 def solution(mesh):

time: 295 us -> 316 us (1.071)
  Pallas kernels: 44.8 us -> 72.5 us
  waiting for transfers between devices: 124 us -> 97.2 us
  local copies, waits for them, and re-layouts: 18.8 us -> 25.8 us
  matrix products: 14.8 us -> 19.2 us
  blocking collectives: 46 us -> 50.2 us
  other arithmetic: 6.39 us -> 10.3 us
    pallas_call x1 -> x2, Pallas kernels: 44.8 us -> 72.5 us  [flash(): pl.pallas_call(kern, grid_spec=grid_spec, out_shape=out_shape, compiler_p...]
    ppermute x1, waiting for transfers between devices: 19.1 us -> 0.01 us  [local(): lax.ppermute(kv_own[:, slots - REACH:], 'ctx', [(e, e + 1) for e in range...]
    dot_general x1 -> x2, matrix products: 8.85 us -> 13.3 us  [local(): jnp.dot(owned_attended, out_weight, preferred_element_type=jnp.float32)]
    all_to_all x1 -> x2, blocking collectives: 37 us -> 41.2 us  [local(): got = lax.all_to_all(piece, 'ctx', split_axis=0, concat_axis=0, tiled=True)]
    ppermute x1, waiting for transfers between devices: 3.86 us -> 0.01 us  [local(): lax.ppermute(kv_own[:, :REACH], 'ctx', [(e, e - 1) for e in range(1, ctx_...]
    broadcast_in_dim x0 -> x3, local copies, waits for them, and re-layouts: none -> 3.45 us  [the longest x1 1.16 us: local(): jnp.zeros((slots, row_count, HD), jnp.float32)]
    reduce_scatter x1 -> x2, waiting for transfers between devices: 50.3 us -> 47.8 us  [local(): lax.psum_scatter(head_terms.astype(jnp.bfloat16), 'head', scatter_dimensi...]
  transfers between devices with their start and end apart: 12 -> 13, of which waited for: 6 -> 5; matrix products, arithmetic and copies ran while one was open for 7% -> 12% of each run, Pallas kernels for 0% -> 13%
where the time goes in v3:
time: 316 us; the launch traced here: 314 us
  waiting for transfers between devices  97.2 us (31%)
  Pallas kernels  72.5 us (23%)
  blocking collectives  50.2 us (16%)
  local copies, waits for them, and re-layouts  25.8 us (8%)
  starting transfers between devices  25.1 us (8%)
  matrix products  19.2 us (6%)
  between operations  13.9 us (4%)
  other arithmetic  10.3 us (3%)
    pallas_call x2, Pallas kernels, flash(): pl.pallas_call(kern, grid_spec=grid_spec, out_shape=out_shape, compiler_p...  72.5 us
    reduce_scatter x2, waiting for transfers between devices, local(): lax.psum_scatter(head_terms.astype(jnp.bfloat16), 'head', scatter_dimensi...  47.8 us
    all_to_all x2, blocking collectives, local(): got = lax.all_to_all(piece, 'ctx', split_axis=0, concat_axis=0, tiled=True)  41.2 us
    ppermute x4, waiting for transfers between devices, doubling_gather(): lax.ppermute(held, 'ctx', [(e, (e + shift) % size) for e in range(size)])  39.1 us
    ppermute x5, starting transfers between devices, local(): own.append(lax.ppermute(piece, 'ctx', perm))  16.2 us
    dot_general x2, matrix products, local(): jnp.dot(owned_attended, out_weight, preferred_element_type=jnp.float32)  13.3 us
    ppermute x5, waiting for transfers between devices, local(): own.append(lax.ppermute(piece, 'ctx', perm))  10.3 us
    psum x1, blocking collectives, local(): lax.psum((jnp.sum(query_float * query_float, axis=1), jnp.sum(key_float *...  9.03 us
  transfers between devices with their start and end apart: 13, of which 5 were waited for; matrix products, arithmetic and copies ran while one was open for 12% of the time, Pallas kernels for 13%

profile of v3, /device:TPU:1, one launch (start us, length us, event | category | flops | bytes accessed | tf_op | source)
XLA Modules:
  0.0 314.3 jit_solution(12333964704283428126)
XLA Ops:
  7.3 2.5 collective-permute-start
  9.8 1.4 copy.29
  12.2 9.0 %all-reduce = (f32[512]{0:T(512)S(1)}, f32[512]{0:T(512)S(1)}) all-reduce(f32[512]{0:T(512)S(1)} %fusion.8, f32[512]{0:T(512)S(1)} %fusion.5), channel_id=1, replica_groups=mesh['batch'=4,'ctx'=16,'head'=4] {'head'}, use_global_device_ids=true, to_apply=%region_3.4 | all-reduce | flops 1024 | bytes 8192 | tf_op jit(solution)/shard_map/psum | solution.py:147
  23.2 8.1 %collective-permute-start.5 = (bf16[3,512,128]{2,1,0:T(8,128)(2,1)S(1)}, bf16[3,512,128]{2,1,0:T(8,128)(2,1)S(1)}, u32[]{:S(2)}, u32[]{:S(2)}) collective-permute-start(bf16[3,512,128]{2,1,0:T(8,128)(2,1)S(1)} %bitcast.94), channel_id=1, source_target_pairs={{4,0},{24,4},{44,8},{0,12},{20,16},{40,20},{60,24},{16,28},{36,32}... | collective-permute-start | bytes 1179656 | tf_op jit(solution)/shard_map/ppermute | solution.py:167
  31.5 5.5 %collective-permute-start.6 = (bf16[3,512,128]{2,1,0:T(8,128)(2,1)S(1)}, bf16[3,512,128]{2,1,0:T(8,128)(2,1)S(1)}, u32[]{:S(2)}, u32[]{:S(2)}) collective-permute-start(bf16[3,512,128]{2,1,0:T(8,128)(2,1)S(1)} %bitcast.95), channel_id=1, source_target_pairs={{8,0},{28,4},{48,8},{4,12},{24,16},{44,20},{0,24},{20,28},{40,32},... | collective-permute-start | bytes 1179656 | tf_op jit(solution)/shard_map/ppermute | solution.py:167
  39.7 31.3 %collective-permute-done.1 = s32[2,2,512]{2,1,0:T(2,128)S(1)} collective-permute-done((s32[2,2,512]{2,1,0:T(2,128)S(1)}, s32[2,2,512]{2,1,0:T(2,128)S(1)}, u32[]{:S(2)}, u32[]{:S(2)}) %collective-permute-start.1) | collective-permute-done | bytes 8224 | tf_op jit(solution)/shard_map/ppermute | solution.py:114
  72.2 7.7 %collective-permute-done.2 = s32[4,2,512]{2,1,0:T(2,128)S(1)} collective-permute-done((s32[4,2,512]{2,1,0:T(2,128)S(1)}, s32[4,2,512]{2,1,0:T(2,128)S(1)}, u32[]{:S(2)}, u32[]{:S(2)}) %collective-permute-start.2) | collective-permute-done | bytes 16416 | tf_op jit(solution)/shard_map/ppermute | solution.py:114
  79.9 2.9 collective-permute-start.3
  83.4 1.3 and.196
  84.8 1.2 and.206
  89.5 1.9 collective-permute-start.8
  92.5 1.2 gather_fusion.1
  95.6 2.6 copy.38.qs_ref
  100.1 10.3 %collective-permute-done.8 = bf16[3,512,128]{2,1,0:T(8,128)(2,1)S(1)} collective-permute-done((bf16[3,512,128]{2,1,0:T(8,128)(2,1)}, bf16[3,512,128]{2,1,0:T(8,128)(2,1)S(1)}, u32[]{:S(2)}, u32[]{:S(2)}) %collective-permute-start.8) | collective-permute-done | bytes 393248 | tf_op jit(solution)/shard_map/ppermute | solution.py:167
  110.3 1.6 pad_maximum_fusion.6
  111.9 1.3 collective-permute-start.9
  113.3 1.5 collective-permute-start.10
  115.1 1.3 slice_bitcast_fusion.2
  119.9 40.8 %shard_map.100 = (f32[5,512,1]{2,1,0:T(8,128)}, f32[5,512,1]{2,1,0:T(8,128)}, f32[5,512,128]{2,1,0:T(8,128)}) custom-call(s32[45]{0:T(128)} %get-tuple-element.15.need_ref, s32[5]{0:T(128)} %get-tuple-element.40.qp_ref, s32[45]{0:T(128)} %min.26.kt_ref, s32[45]{0:T(128)} %and_select_fusion.kp_ref, bf16[5,512,128]{2,1,0:T(8,128)(2,1)} %get-tuple-element.21.q_ref, ...), custom_call_target="tpu_custom_call" | custom-call | flops 2013265920 | bytes 3932160 | tf_op jit(solution)/shard_map/pallas_call | solution.py:95
  160.7 1.5 pad_maximum_fusion
  162.2 2.0 slice_bitcast_fusion
  164.1 31.8 %shard_map.101 = bf16[5,512,128]{2,1,0:T(8,128)(2,1)} custom-call(s32[45]{0:T(128)} %and_convert_fusion.1.need_ref, s32[5]{0:T(128)} %get-tuple-element.40.qp_ref, s32[45]{0:T(128)} %add.377.kt_ref, s32[45]{0:T(128)} %and_select_fusion.kp_ref, bf16[5,512,128]{2,1,0:T(8,128)(2,1)} %get-tuple-element.21.q_ref, bf16[13,512,128]{2,1,0:T(8,128)(2,1)} %get-tuple-element.18.k_ref, ...), custom_call_target="tpu_custom_call" | custom-call | flops 2013265920 | bytes 3932160 | tf_op jit(solution)/shard_map/pallas_call | solution.py:95
  195.9 2.0 fusion.4
  198.1 24.6 %all_to_all.10 = bf16[16,5,16,128]{3,2,1,0:T(8,128)(2,1)S(1)} all-to-all(bf16[16,5,16,128]{3,2,1,0:T(8,128)(2,1)S(1)} %get-tuple-element.29), channel_id=1, replica_groups=mesh['batch'=4,'ctx'=16,'head'=4] {'ctx'}, dimensions={0} | all-to-all | bytes 655360 | tf_op jit(solution)/shard_map/all_to_all | solution.py:248
  222.9 6.6 %convolution_convert_fusion.1 = bf16[256,5120]{1,0:T(8,128)(2,1)} fusion(bf16[640,5120]{1,0:T(8,128)(2,1)} %param.18, bf16[32,8,5,128]{3,2,1,0:T(8,128)(2,1)S(1)} %bitcast.91), kind=kOutput, calls=%fused_computation.6 | convolution fusion | flops 1679032320 | bytes 9502720 | tf_op jit(solution)/shard_map/dot_general | solution.py:251
  229.6 16.6 %all_to_all.11 = bf16[16,5,16,128]{3,2,1,0:T(8,128)(2,1)S(1)} all-to-all(bf16[16,5,16,128]{3,2,1,0:T(8,128)(2,1)S(1)} %get-tuple-element.30), channel_id=1, replica_groups=mesh['batch'=4,'ctx'=16,'head'=4] {'ctx'}, dimensions={0} | all-to-all | bytes 655360 | tf_op jit(solution)/shard_map/all_to_all | solution.py:248
  246.5 6.6 %convolution_convert_fusion = bf16[256,5120]{1,0:T(8,128)(2,1)} fusion(bf16[640,5120]{1,0:T(8,128)(2,1)} %param.18, bf16[32,8,5,128]{3,2,1,0:T(8,128)(2,1)S(1)} %bitcast.92), kind=kOutput, calls=%fused_computation.5 | convolution fusion | flops 1679032320 | bytes 9502720 | tf_op jit(solution)/shard_map/dot_general | solution.py:251
  254.8 10.7 %reduce-scatter.3.cloned.1.call-done = bf16[256,1280]{1,0:T(8,128)(2,1)} async-done(((bf16[256,5120]{1,0:T(8,128)(2,1)}), bf16[256,1280]{1,0:T(8,128)(2,1)}) %reduce-scatter.3.cloned.1.call-update) | async-done | bytes 655376 | tf_op jit(solution)/shard_map/reduce_scatter | solution.py:252
  265.6 1.8 fusion.2
  267.4 37.1 %reduce-scatter.5.cloned.1.call-done = bf16[256,1280]{1,0:T(8,128)(2,1)} async-done(((bf16[256,5120]{1,0:T(8,128)(2,1)}), bf16[256,1280]{1,0:T(8,128)(2,1)}) %reduce-scatter.5.cloned.1.call-update) | async-done | bytes 655376 | tf_op jit(solution)/shard_map/reduce_scatter | solution.py:252
  304.4 1.8 fusion.3
  306.2 1.2 pad_maximum_fusion.2
  (125 shorter events, 22.5 us)
Async XLA Ops:
  6.5 246.7 %copy-start = (f32[50,1280]{1,0:T(8,128)S(1)}, f32[50,1280]{1,0:T(8,128)}, u32[]{:S(2)}) copy-start(f32[50,1280]{1,0:T(8,128)} %param.19) | copy-start | bytes 768004
  6.5 4.9 %copy-start.2 = (bf16[512,640]{1,0:T(8,128)(2,1)S(1)}, bf16[512,640]{1,0:T(8,128)(2,1)}, u32[]{:S(2)}) copy-start(bf16[512,640]{1,0:T(8,128)(2,1)} %param.11) | copy-start | bytes 1966084
  6.5 259.0 %reduce-scatter.3.cloned.1.call-start = ((), (), s32[]{:S(2)}) async-start(), calls=%async_computation.4 | async-start | bytes 3276800 | tf_op jit(solution)/shard_map/reduce_scatter | solution.py:252
  7.3 32.2 %collective-permute-start = (s32[1,2,512]{2,1,0:T(2,128)S(1)}, s32[1,2,512]{2,1,0:T(2,128)S(1)}, u32[]{:S(2)}, u32[]{:S(2)}) collective-permute-start(s32[1,2,512]{2,1,0:T(2,128)S(1)} %add_bitcast_fusion), channel_id=1, source_target_pairs={{0,4},{4,8},{8,12},{12,16},{16,20},{20,24},{24,28},{28,32},{32,36}... | collective-permute-start | bytes 12296 | tf_op jit(solution)/shard_map/ppermute | solution.py:114
  9.8 2.1 copy-start.3
  11.2 10.0 %copy-start.6 = (f32[640]{0:T(1024)S(1)}, f32[640]{0:T(1024)}, u32[]{:S(2)}) copy-start(f32[640]{0:T(1024)} %param.14) | copy-start | bytes 7684
  11.7 9.7 %copy-start.7 = (f32[640]{0:T(1024)S(1)}, f32[640]{0:T(1024)}, u32[]{:S(2)}) copy-start(f32[640]{0:T(1024)} %param.13) | copy-start | bytes 7684
  22.0 69.5 %copy-start.4 = (s32[512]{0:T(512)S(1)}, s32[512]{0:T(512)}, u32[]{:S(2)}) copy-start(s32[512]{0:T(512)} %param.16) | copy-start | bytes 6148
  22.0 69.5 %copy-start.5 = (s32[512]{0:T(512)S(1)}, s32[512]{0:T(512)}, u32[]{:S(2)}) copy-start(s32[512]{0:T(512)} %param.15) | copy-start | bytes 6148
  22.3 77.7 %collective-permute-start.4 = (bf16[3,512,128]{2,1,0:T(8,128)(2,1)S(1)}, bf16[3,512,128]{2,1,0:T(8,128)(2,1)S(1)}, u32[]{:S(2)}, u32[]{:S(2)}) collective-permute-start(bf16[3,512,128]{2,1,0:T(8,128)(2,1)S(1)} %bitcast.93), channel_id=1, source_target_pairs={{0,0},{20,4},{40,8},{60,12},{16,16},{36,20},{56,24},{12,28},{32,32... | collective-permute-start | bytes 1179656 | tf_op jit(solution)/shard_map/ppermute | solution.py:167
  23.2 76.8 %collective-permute-start.5 = (bf16[3,512,128]{2,1,0:T(8,128)(2,1)S(1)}, bf16[3,512,128]{2,1,0:T(8,128)(2,1)S(1)}, u32[]{:S(2)}, u32[]{:S(2)}) collective-permute-start(bf16[3,512,128]{2,1,0:T(8,128)(2,1)S(1)} %bitcast.94), channel_id=1, source_target_pairs={{4,0},{24,4},{44,8},{0,12},{20,16},{40,20},{60,24},{16,28},{36,32}... | collective-permute-start | bytes 1179656 | tf_op jit(solution)/shard_map/ppermute | solution.py:167
  31.5 68.5 %collective-permute-start.6 = (bf16[3,512,128]{2,1,0:T(8,128)(2,1)S(1)}, bf16[3,512,128]{2,1,0:T(8,128)(2,1)S(1)}, u32[]{:S(2)}, u32[]{:S(2)}) collective-permute-start(bf16[3,512,128]{2,1,0:T(8,128)(2,1)S(1)} %bitcast.95), channel_id=1, source_target_pairs={{8,0},{28,4},{48,8},{4,12},{24,16},{44,20},{0,24},{20,28},{40,32},... | collective-permute-start | bytes 1179656 | tf_op jit(solution)/shard_map/ppermute | solution.py:167
  37.9 62.1 %collective-permute-start.7 = (bf16[3,512,128]{2,1,0:T(8,128)(2,1)}, bf16[3,512,128]{2,1,0:T(8,128)(2,1)S(1)}, u32[]{:S(2)}, u32[]{:S(2)}) collective-permute-start(bf16[3,512,128]{2,1,0:T(8,128)(2,1)} %bitcast.96), channel_id=1, source_target_pairs={{12,0},{32,4},{52,8},{8,12},{28,16},{48,20},{4,24},{24,28},{44,32}... | collective-permute-start | bytes 1179656 | tf_op jit(solution)/shard_map/ppermute | solution.py:167
  38.9 47.1 %copy-start.8 = (s32[45]{0:T(128)}, s32[45]{0:T(128)S(1)}, u32[]{:S(2)}) copy-start(s32[45]{0:T(128)S(1)} %min.22) | copy-start | bytes 544
  39.6 31.4 %collective-permute-start.1 = (s32[2,2,512]{2,1,0:T(2,128)S(1)}, s32[2,2,512]{2,1,0:T(2,128)S(1)}, u32[]{:S(2)}, u32[]{:S(2)}) collective-permute-start(s32[2,2,512]{2,1,0:T(2,128)S(1)} %pad_add_fusion.2), channel_id=1, source_target_pairs={{0,8},{4,12},{8,16},{12,20},{16,24},{20,28},{24,32},{28,36},{32,40... | collective-permute-start | bytes 24584 | tf_op jit(solution)/shard_map/ppermute | solution.py:114
  71.0 8.9 %collective-permute-start.2 = (s32[4,2,512]{2,1,0:T(2,128)S(1)}, s32[4,2,512]{2,1,0:T(2,128)S(1)}, u32[]{:S(2)}, u32[]{:S(2)}) collective-permute-start(s32[4,2,512]{2,1,0:T(2,128)S(1)} %pad_add_fusion.1), channel_id=1, source_target_pairs={{0,16},{4,20},{8,24},{12,28},{16,32},{20,36},{24,40},{28,44},{32,4... | collective-permute-start | bytes 49160 | tf_op jit(solution)/shard_map/ppermute | solution.py:114
  79.9 9.6 %collective-permute-start.3 = (s32[8,2,512]{2,1,0:T(2,128)S(1)}, s32[8,2,512]{2,1,0:T(2,128)S(1)}, u32[]{:S(2)}, u32[]{:S(2)}) collective-permute-start(s32[8,2,512]{2,1,0:T(2,128)S(1)} %pad_add_fusion), channel_id=1, source_target_pairs={{0,32},{4,36},{8,40},{12,44},{16,48},{20,52},{24,56},{28,60},{32,0... | collective-permute-start | bytes 98312 | tf_op jit(solution)/shard_map/ppermute | solution.py:114
  89.5 20.8 %collective-permute-start.8 = (bf16[3,512,128]{2,1,0:T(8,128)(2,1)}, bf16[3,512,128]{2,1,0:T(8,128)(2,1)S(1)}, u32[]{:S(2)}, u32[]{:S(2)}) collective-permute-start(bf16[3,512,128]{2,1,0:T(8,128)(2,1)} %bitcast.97), channel_id=1, source_target_pairs={{16,0},{36,4},{56,8},{12,12},{32,16},{52,20},{8,24},{28,28},{48,32... | collective-permute-start | bytes 1179656 | tf_op jit(solution)/shard_map/ppermute | solution.py:167
  91.7 3.9 %copy-start.1 = (s32[16,1,512]{2,1,0:T(1,128)}, s32[16,1,512]{2,1,0:T(1,128)S(1)}, u32[]{:S(2)}) copy-start(s32[16,1,512]{2,1,0:T(1,128)S(1)} %get-tuple-element.32.ks_ref) | copy-start | bytes 98308
  94.5 0.9 copy-start.11
  95.6 3.3 %copy-start.9 = (s32[45]{0:T(128)S(1)}, s32[45]{0:T(128)}, u32[]{:S(2)}) copy-start(s32[45]{0:T(128)} %copy-done.8) | copy-start | bytes 544
  95.6 3.4 %copy-start.10 = (s32[45]{0:T(128)S(1)}, s32[45]{0:T(128)}, u32[]{:S(2)}) copy-start(s32[45]{0:T(128)} %eq.108) | copy-start | bytes 544
  95.6 3.4 %copy-start.13 = (pred[45]{0:T(512)(128)(4,1)S(1)}, pred[45]{0:T(512)(128)(4,1)}, u32[]{:S(2)}) copy-start(pred[45]{0:T(512)(128)(4,1)} %and.206) | copy-start | bytes 139
  95.6 3.4 %copy-start.14 = (pred[45]{0:T(512)(128)(4,1)S(1)}, pred[45]{0:T(512)(128)(4,1)}, u32[]{:S(2)}) copy-start(pred[45]{0:T(512)(128)(4,1)} %and.196) | copy-start | bytes 139
  111.9 48.8 %collective-permute-start.9 = (bf16[2,4,512,128]{3,2,1,0:T(8,128)(2,1)}, bf16[2,4,512,128]{3,2,1,0:T(8,128)(2,1)S(1)}, u32[]{:S(2)}, u32[]{:S(2)}) collective-permute-start(bf16[2,4,512,128]{3,2,1,0:T(8,128)(2,1)} %get-tuple-element.27), channel_id=1, source_target_pairs={{0,4},{4,8},{8,12},{12,16},{16,20},{20,24},{24,28},{28,32},{32,36}... | collective-permute-start | bytes 3145736 | tf_op jit(solution)/shard_map/ppermute | solution.py:171
  113.3 47.4 %collective-permute-start.10 = (bf16[2,4,512,128]{3,2,1,0:T(8,128)(2,1)}, bf16[2,4,512,128]{3,2,1,0:T(8,128)(2,1)}, u32[]{:S(2)}, u32[]{:S(2)}) collective-permute-start(bf16[2,4,512,128]{3,2,1,0:T(8,128)(2,1)} %get-tuple-element.28), channel_id=1, source_target_pairs={{4,0},{8,4},{12,8},{16,12},{20,16},{24,20},{28,24},{32,28},{36,32}... | collective-permute-start | bytes 3145736 | tf_op jit(solution)/shard_map/ppermute | solution.py:174
  229.6 74.8 %reduce-scatter.5.cloned.1.call-start = ((), (), s32[]{:S(2)}) async-start(), calls=%async_computation.5 | async-start | bytes 3276800 | tf_op jit(solution)/shard_map/reduce_scatter | solution.py:252
  253.2 0.7 copy-start.12
Sparse Core Ops, SparseCore 0:
  229.7 35.8 reduce-scatter.2
  268.1 36.2 reduce-scatter.4

commit v4 on v1

--- a/solution.py
+++ b/solution.py
@@ -117,68 +117,120 @@
 
     qkv = jnp.stack([queries, normed_keys, value_rows]).reshape(3, row_count, head_count, HD)
     qkv = jnp.transpose(qkv, (0, 2, 1, 3))
+    meta = jnp.stack([segment, destination // 64, destination % 64]).astype(jnp.bfloat16)
+    meta = meta.reshape(-1, HD)
+    body_rows = 3 * row_count
+    pad = (-(body_rows + meta.shape[0])) % 16
 
     inverse = pow(slots, -1, ctx_size)
     own = []
+    own_meta = []
     for j in range(slots):
         target = lax.rem(inverse * (me - j + ctx_size), ctx_size)
         head = (slots * target + j) // ctx_size
         piece = lax.dynamic_index_in_dim(qkv, head, axis=1, keepdims=False)
+        piece = jnp.concatenate(
+            [piece.reshape(body_rows, HD), meta, jnp.zeros((pad, HD), jnp.bfloat16)], axis=0
+        )
         perm = [((slots * e + j) % ctx_size, e) for e in range(ctx_size)]
-        own.append(lax.ppermute(piece, "ctx", perm))
+        came = lax.ppermute(piece, "ctx", perm)
+        own.append(came[:body_rows].reshape(3, row_count, HD))
+        own_meta.append(came[body_rows:body_rows + meta.shape[0]].reshape(3, row_count))
     own = jnp.stack(own, axis=1)
+    own_meta = jnp.stack(own_meta, axis=1).astype(jnp.int32)
+    seg_own = own_meta[0]
+    dest_own = own_meta[1] * 64 + own_meta[2]
 
     kv_own = own[1:]
+    seg_own_b = seg_own.astype(jnp.bfloat16).reshape(slots, row_count // HD, HD)
+    halo_rows = 2 * REACH * row_count
+
+    def halo(kv_part, seg_part):
+        return jnp.concatenate(
+            [kv_part.reshape(halo_rows, HD), seg_part.reshape(REACH * row_count // HD, HD)], axis=0
+        )
+
     left = lax.ppermute(
-        kv_own[:, slots - REACH:], "ctx", [(e, e + 1) for e in range(ctx_size - 1)]
+        halo(kv_own[:, slots - REACH:], seg_own_b[slots - REACH:]),
+        "ctx",
+        [(e, e + 1) for e in range(ctx_size - 1)],
     )
     right = lax.ppermute(
-        kv_own[:, :REACH], "ctx", [(e, e - 1) for e in range(1, ctx_size)]
-    )
-    kv_all = jnp.concatenate([left, kv_own, right], axis=1)
-
-    seg_all = lax.all_gather(segment, "ctx", axis=0, tiled=True)
-    dest_all = lax.all_gather(destination, "ctx", axis=0, tiled=True)
-    seg_blocks = seg_all.reshape(ctx_size, row_count)
-    seg_lo = seg_blocks[:, 0]
-    seg_hi = seg_blocks[:, -1]
+        halo(kv_own[:, :REACH], seg_own_b[:REACH]),
+        "ctx",
+        [(e, e - 1) for e in range(1, ctx_size)],
+    )
+
+    def unpack(got):
+        kv_part = got[:halo_rows].reshape(2, REACH, row_count, HD)
+        seg_part = got[halo_rows:].reshape(REACH, row_count).astype(jnp.int32)
+        return kv_part, seg_part
+
+    left_kv, left_seg = unpack(left)
+    right_kv, right_seg = unpack(right)
+    kv_all = jnp.concatenate([left_kv, kv_own, right_kv], axis=1)
+    seg_keys = jnp.concatenate([left_seg, seg_own, right_seg], axis=0)
+    seg_lo = seg_keys[:, 0]
+    seg_hi = seg_keys[:, -1]
 
     offsets = 2 * REACH + 1
     jj = jnp.arange(slots, dtype=jnp.int32)[:, None]
     oo = jnp.arange(offsets, dtype=jnp.int32)[None, :] - REACH
     t_q = slots * me + jj
     t_k = t_q + oo
-    p_q = t_q % ctx_size
     valid = (t_k >= 0) & (t_k < tiles)
     t_kc = jnp.clip(t_k, 0, tiles - 1)
-    p_k = t_kc % ctx_size
     same_head = (t_kc // ctx_size) == (t_q // ctx_size)
-    meet = (seg_lo[p_q] <= seg_hi[p_k]) & (seg_lo[p_k] <= seg_hi[p_q])
-    need = (valid & same_head & meet).astype(jnp.int32).reshape(-1)
-    kt = (jj + oo + REACH).astype(jnp.int32).reshape(-1)
-    qp = p_q[:, 0].astype(jnp.int32)
-    kp = p_k.astype(jnp.int32).reshape(-1)
+    q_index = jj + REACH
+    k_index = jj + oo + REACH
+    meet = (seg_lo[q_index] <= seg_hi[k_index]) & (seg_lo[k_index] <= seg_hi[q_index])
+    need_b = (valid & same_head & meet).reshape(-1)
+    need = need_b.astype(jnp.int32)
+    steps = jnp.arange(need.shape[0], dtype=jnp.int32)
+    latest = lax.cummax(jnp.where(need_b, steps, -1), axis=0)
+    source = jnp.where(latest < 0, jnp.argmax(need_b).astype(jnp.int32), latest)
+    kt = k_index.astype(jnp.int32).reshape(-1)[source]
+    qp = q_index[:, 0].astype(jnp.int32)
+    kp = kt
 
     attended = flash(
         need, qp, kt, kp,
         own[0], kv_all[0], kv_all[1],
-        seg_blocks.reshape(ctx_size, row_count, 1),
-        seg_blocks.reshape(ctx_size, 1, row_count),
+        seg_keys.reshape(-1, row_count, 1),
+        seg_keys.reshape(-1, 1, row_count),
         score_scale,
     )
 
     slot_count = row_count // ctx_size
-    dest_blocks = dest_all.reshape(ctx_size, row_count)
-    dest_mine = dest_blocks[qp]
-    place = (dest_mine // row_count) * slot_count + dest_mine % slot_count
-    placed = jnp.zeros_like(attended).at[jj, place].set(attended)
+    place = (dest_own // row_count) * slot_count + dest_own % slot_count
+    chooser = (
+        place[:, None, :] == jnp.arange(row_count, dtype=jnp.int32)[None, :, None]
+    ).astype(jnp.bfloat16)
+    placed = jnp.einsum(
+        "jsr,jrd->jsd", chooser, attended, preferred_element_type=jnp.float32
+    ).astype(jnp.bfloat16)
+    placed_seg = jnp.einsum(
+        "jsr,jr->js", chooser, seg_own.astype(jnp.bfloat16), preferred_element_type=jnp.float32
+    ).astype(jnp.bfloat16)
     placed = placed.reshape(slots, ctx_size, slot_count, HD).transpose(1, 0, 2, 3)
-    got = lax.all_to_all(placed, "ctx", split_axis=0, concat_axis=0, tiled=True)
-    got = got.reshape(head_count, ctx_size, slot_count, HD).transpose(1, 2, 0, 3)
-    owned_attended = got.reshape(row_count, row_width)
-
-    owned_video_all = jnp.zeros_like(seg_all).at[dest_all].set(seg_all)
-    owned_video = lax.dynamic_slice_in_dim(owned_video_all, me * row_count, row_count)
+    placed = placed.reshape(ctx_size, slots * slot_count, HD)
+    placed_seg = placed_seg.reshape(slots, ctx_size, slot_count).transpose(1, 0, 2)
+    seg_width = slots * slot_count
+    seg_rows_n = -(-seg_width // HD)
+    placed_seg = jnp.pad(
+        placed_seg.reshape(ctx_size, seg_width), ((0, 0), (0, seg_rows_n * HD - seg_width))
+    ).reshape(ctx_size, seg_rows_n, HD)
+    extra = (-(seg_width + seg_rows_n)) % 16
+    payload = jnp.concatenate(
+        [placed, placed_seg, jnp.zeros((ctx_size, extra, HD), jnp.bfloat16)], axis=1
+    )
+    got = lax.all_to_all(payload, "ctx", split_axis=0, concat_axis=0, tiled=True)
+    got_att = got[:, :seg_width].reshape(tiles, slot_count, HD)
+    got_att = got_att.reshape(head_count, ctx_size, slot_count, HD).transpose(1, 2, 0, 3)
+    owned_attended = got_att.reshape(row_count, row_width)
+    got_seg = got[:, seg_width:seg_width + seg_rows_n].reshape(ctx_size, seg_rows_n * HD)
+    got_seg = got_seg[:, :seg_width].reshape(tiles, slot_count)
+    owned_video = got_seg[:ctx_size].reshape(row_count).astype(jnp.int32)
 
     head_terms = jnp.dot(owned_attended, out_weight, preferred_element_type=jnp.float32)
     mixed_rows = lax.psum_scatter(

time: 333 us -> 292 us (0.88)
  blocking collectives: 127 us -> 44.9 us
  waiting for transfers between devices: 51 us -> 109 us
  local copies, waits for them, and re-layouts: 54.6 us -> 31 us
  other arithmetic: 3.89 us -> 7.66 us
    all_gather x2 -> x0, blocking collectives: 87.4 us -> none  [the longest x1 58.7 us: local(): seg_all = lax.all_gather(segment, 'ctx', axis=0, tiled=True)]
    ppermute x7, waiting for transfers between devices: 13 us -> 59.1 us  [the longest x5 40.6 us: local(): came = lax.ppermute(piece, 'ctx', perm)]
    scatter x1 -> x0, local copies, waits for them, and re-layouts: 30.7 us -> none  [local(): owned_video_all = jnp.zeros_like(seg_all).at[dest_all].set(seg_all)]
    reduce_scatter x1, waiting for transfers between devices: 38 us -> 50.3 us  [local(): lax.psum_scatter(head_terms.astype(jnp.bfloat16), 'head', scatter_dimensi...]
    slice x1 -> x17, local copies, waits for them, and re-layouts: 0.17 us -> 10.6 us  [the longest x5 5.4 us: local(): own.append(came[:body_rows].reshape(3, row_count, HD))]
    unnamed x33 -> x46, local copies, waits for them, and re-layouts: 9.75 us -> 3.56 us
    all_to_all x1, blocking collectives: 30 us -> 35.3 us  [local(): lax.all_to_all(payload, 'ctx', split_axis=0, concat_axis=0, tiled=True)]
    another operation x7 -> x17, local copies, waits for them, and re-layouts: 5.71 us -> 1.92 us  [the longest x1 3 us: local(): seg_blocks.reshape(ctx_size, row_count, 1)]
  transfers between devices with their start and end apart: 8 -> 8, of which waited for: 3 -> 6; matrix products, arithmetic and copies ran while one was open for 13% -> 4% of each run, Pallas kernels for 0% -> 0%
where the time goes in v4:
time: 292 us; the launch traced here: 291 us
  waiting for transfers between devices  109 us (37%)
  blocking collectives  44.9 us (15%)
  Pallas kernels  42.6 us (15%)
  local copies, waits for them, and re-layouts  31 us (11%)
  starting transfers between devices  26.1 us (9%)
  matrix products  15.7 us (5%)
  between operations  14.1 us (5%)
  other arithmetic  7.66 us (3%)
    reduce_scatter x1, waiting for transfers between devices, local(): lax.psum_scatter(head_terms.astype(jnp.bfloat16), 'head', scatter_dimensi...  50.3 us
    pallas_call x1, Pallas kernels, flash(): pl.pallas_call(kern, grid_spec=grid_spec, out_shape=jax.ShapeDtypeStruct(...  42.6 us
    ppermute x5, waiting for transfers between devices, local(): came = lax.ppermute(piece, 'ctx', perm)  40.6 us
    all_to_all x1, blocking collectives, local(): lax.all_to_all(payload, 'ctx', split_axis=0, concat_axis=0, tiled=True)  35.3 us
    ppermute x5, starting transfers between devices, local(): came = lax.ppermute(piece, 'ctx', perm)  19.8 us
    ppermute x1, waiting for transfers between devices, local(): lax.ppermute(halo(kv_own[:, :REACH], seg_own_b[:REACH]), 'ctx', [(e, e -...  15.3 us
    psum x1, blocking collectives, local(): lax.psum((jnp.sum(query_float * query_float, axis=1), jnp.sum(key_float *...  9.55 us
    dot_general x1, matrix products, local(): jnp.dot(owned_attended, out_weight, preferred_element_type=jnp.float32)  8.83 us
  transfers between devices with their start and end apart: 8, of which 6 were waited for; matrix products, arithmetic and copies ran while one was open for 4% of the time, Pallas kernels for 0%

profile of v4, /device:TPU:1, one launch (start us, length us, event | category | flops | bytes accessed | tf_op | source)
XLA Modules:
  0.0 291.4 jit_solution(10272407833120668669)
XLA Ops:
  6.7 1.4 copy.21
  9.1 9.6 %all-reduce.1 = (f32[512]{0:T(512)S(1)}, f32[512]{0:T(512)S(1)}) all-reduce(f32[512]{0:T(512)S(1)} %fusion.9, f32[512]{0:T(512)S(1)} %fusion.6), channel_id=1, replica_groups=mesh['batch'=4,'ctx'=16,'head'=4] {'head'}, use_global_device_ids=true, to_apply=%region_3.0 | all-reduce | flops 1024 | bytes 8192 | tf_op jit(solution)/shard_map/psum | solution.py:108
  20.2 1.4 collective-permute-start
  22.1 9.1 %collective-permute-start.1 = (bf16[1552,128]{1,0:T(8,128)(2,1)S(1)}, bf16[1552,128]{1,0:T(8,128)(2,1)}, u32[]{:S(2)}, u32[]{:S(2)}) collective-permute-start(bf16[1552,128]{1,0:T(8,128)(2,1)S(1)} %concatenate.34), channel_id=1, source_target_pairs={{4,0},{24,4},{44,8},{0,12},{20,16},{40,20},{60,24},{16,28},{36,32}... | collective-permute-start | bytes 1191944 | tf_op jit(solution)/shard_map/ppermute | solution.py:136
  31.6 4.9 %collective-permute-start.2 = (bf16[1552,128]{1,0:T(8,128)(2,1)S(1)}, bf16[1552,128]{1,0:T(8,128)(2,1)}, u32[]{:S(2)}, u32[]{:S(2)}) collective-permute-start(bf16[1552,128]{1,0:T(8,128)(2,1)S(1)} %concatenate.35), channel_id=1, source_target_pairs={{8,0},{28,4},{48,8},{4,12},{24,16},{44,20},{0,24},{20,28},{40,32},... | collective-permute-start | bytes 1191944 | tf_op jit(solution)/shard_map/ppermute | solution.py:136
  37.4 4.3 %collective-permute-start.4 = (bf16[1552,128]{1,0:T(8,128)(2,1)S(1)}, bf16[1552,128]{1,0:T(8,128)(2,1)}, u32[]{:S(2)}, u32[]{:S(2)}) collective-permute-start(bf16[1552,128]{1,0:T(8,128)(2,1)S(1)} %concatenate.37), channel_id=1, source_target_pairs={{16,0},{36,4},{56,8},{12,12},{32,16},{52,20},{8,24},{28,28},{48,32... | collective-permute-start | bytes 1191944 | tf_op jit(solution)/shard_map/ppermute | solution.py:136
  46.2 19.2 %collective-permute-done.1 = bf16[1552,128]{1,0:T(8,128)(2,1)} collective-permute-done((bf16[1552,128]{1,0:T(8,128)(2,1)S(1)}, bf16[1552,128]{1,0:T(8,128)(2,1)}, u32[]{:S(2)}, u32[]{:S(2)}) %collective-permute-start.1) | collective-permute-done | bytes 397344 | tf_op jit(solution)/shard_map/ppermute | solution.py:136
  66.8 15.1 %collective-permute-done.3 = bf16[1552,128]{1,0:T(8,128)(2,1)} collective-permute-done((bf16[1552,128]{1,0:T(8,128)(2,1)S(1)}, bf16[1552,128]{1,0:T(8,128)(2,1)}, u32[]{:S(2)}, u32[]{:S(2)}) %collective-permute-start.3) | collective-permute-done | bytes 397344 | tf_op jit(solution)/shard_map/ppermute | solution.py:136
  82.6 6.2 %collective-permute-done.4 = bf16[1552,128]{1,0:T(8,128)(2,1)} collective-permute-done((bf16[1552,128]{1,0:T(8,128)(2,1)S(1)}, bf16[1552,128]{1,0:T(8,128)(2,1)}, u32[]{:S(2)}, u32[]{:S(2)}) %collective-permute-start.4) | collective-permute-done | bytes 397344 | tf_op jit(solution)/shard_map/ppermute | solution.py:136
  89.7 1.0 slice.150
  90.7 1.0 slice.149
  91.7 1.0 slice.148
  92.8 1.2 slice.147
  94.0 1.2 slice.154
  95.9 1.0 pad_maximum_fusion.3
  96.9 1.3 collective-permute-start.6
  98.2 1.1 pad_maximum_fusion.2
  99.3 0.9 fusion
  100.5 5.0 %collective-permute-start.5 = (bf16[4112,128]{1,0:T(8,128)(2,1)}, bf16[4112,128]{1,0:T(8,128)(2,1)}, u32[]{:S(2)}, u32[]{:S(2)}) collective-permute-start(bf16[4112,128]{1,0:T(8,128)(2,1)} %pad_maximum_fusion.2), channel_id=1, source_target_pairs={{0,4},{4,8},{8,12},{12,16},{16,20},{20,24},{24,28},{28,32},{32,36}... | collective-permute-start | bytes 3158024 | tf_op jit(solution)/shard_map/ppermute | solution.py:153
  105.8 0.9 slice_bitcast_fusion.2.q_ref
  106.7 15.3 %collective-permute-done.6 = bf16[4112,128]{1,0:T(8,128)(2,1)S(1)} collective-permute-done((bf16[4112,128]{1,0:T(8,128)(2,1)}, bf16[4112,128]{1,0:T(8,128)(2,1)S(1)}, u32[]{:S(2)}, u32[]{:S(2)}) %collective-permute-start.6) | collective-permute-done | bytes 1052704 | tf_op jit(solution)/shard_map/ppermute | solution.py:158
  122.0 3.3 %collective-permute-done.5 = bf16[4112,128]{1,0:T(8,128)(2,1)} collective-permute-done((bf16[4112,128]{1,0:T(8,128)(2,1)}, bf16[4112,128]{1,0:T(8,128)(2,1)}, u32[]{:S(2)}, u32[]{:S(2)}) %collective-permute-start.5) | collective-permute-done | bytes 1052704 | tf_op jit(solution)/shard_map/ppermute | solution.py:153
  132.3 1.4 slice.160
  134.3 2.0 slice_bitcast_fusion
  136.3 2.3 copy.39.qs_ref
  138.6 1.4 gather_fusion.4
  139.9 42.6 %shard_map.100 = bf16[5,512,128]{2,1,0:T(8,128)(2,1)} custom-call(s32[45]{0:T(128)} %get-tuple-element.11.need_ref, s32[5]{0:T(128)} %iota_add_fusion.2.qp_ref, s32[45]{0:T(128)} %gather_fusion.4, s32[45]{0:T(128)} %gather_fusion.4, bf16[5,512,128]{2,1,0:T(8,128)(2,1)} %slice_bitcast_fusion.2.q_ref, bf16[13,512,128]{2,1,0:T(8,128)(2,1)} %get-tuple-element.14.k_ref, ...), custom_call_target="tpu_custom_call" | custom-call | tf_op jit(solution)/shard_map/pallas_call | solution.py:74
  182.5 2.0 fusion.5
  184.8 35.3 %all_to_all.5 = bf16[16,176,128]{2,1,0:T(8,128)(2,1)S(1)} all-to-all(bf16[16,176,128]{2,1,0:T(8,128)(2,1)S(1)} %maximum_maximum_fusion), channel_id=1, replica_groups=mesh['batch'=4,'ctx'=16,'head'=4] {'ctx'}, dimensions={0} | all-to-all | bytes 1441792 | tf_op jit(solution)/shard_map/all_to_all | solution.py:227
  220.7 8.8 %convolution_convert_fusion = bf16[512,5120]{1,0:T(8,128)(2,1)} fusion(bf16[640,5120]{1,0:T(8,128)(2,1)} %param.18, bf16[64,8,5,128]{3,2,1,0:T(8,128)(2,1)S(1)} %bitcast.86), kind=kOutput, calls=%fused_computation.5 | convolution fusion | flops 3358064640 | bytes 12451840 | tf_op jit(solution)/shard_map/dot_general | solution.py:235
  230.6 50.3 %reduce-scatter.2.cloned.1.call-done = bf16[512,1280]{1,0:T(8,128)(2,1)} async-done(((bf16[512,5120]{1,0:T(8,128)(2,1)}), bf16[512,1280]{1,0:T(8,128)(2,1)}) %reduce-scatter.2.cloned.1.call-update) | async-done | bytes 1310736 | tf_op jit(solution)/shard_map/reduce_scatter | solution.py:236
  280.9 3.6 %fusion.2 = bf16[512,1280]{1,0:T(8,128)(2,1)} fusion(f32[6,1280]{1,0:T(8,128)S(1)} %fusion.26, bf16[512,1280]{1,0:T(8,128)(2,1)} %reduce-scatter.2.cloned.1.call-done, s32[512]{0:T(512)S(1)} %reshape.482), kind=kOutput, calls=%fused_computation.11 | convolution fusion | flops 49155072 | bytes 2654208 | tf_op jit(solution)/shard_map/dot_general | solution.py:244
  (154 shorter events, 22.1 us)
Async XLA Ops:
  6.5 223.0 %copy-start = (f32[50,1280]{1,0:T(8,128)S(1)}, f32[50,1280]{1,0:T(8,128)}, u32[]{:S(2)}) copy-start(f32[50,1280]{1,0:T(8,128)} %param.19) | copy-start | bytes 768004
  6.5 1.6 copy-start.8
  6.5 2.1 copy-start.9
  6.5 274.4 %reduce-scatter.2.cloned.1.call-start = ((), (), s32[]{:S(2)}) async-start(), calls=%async_computation.2 | async-start | bytes 6553600 | tf_op jit(solution)/shard_map/reduce_scatter | solution.py:236
  8.1 10.5 %copy-start.10 = (f32[640]{0:T(1024)S(1)}, f32[640]{0:T(1024)}, u32[]{:S(2)}) copy-start(f32[640]{0:T(1024)} %param.14) | copy-start | bytes 7684
  8.4 10.4 %copy-start.11 = (f32[640]{0:T(1024)S(1)}, f32[640]{0:T(1024)}, u32[]{:S(2)}) copy-start(f32[640]{0:T(1024)} %param.13) | copy-start | bytes 7684
  19.3 0.7 copy-start.13
  19.3 0.7 copy-start.12
  20.2 25.2 %collective-permute-start = (bf16[1552,128]{1,0:T(8,128)(2,1)S(1)}, bf16[1552,128]{1,0:T(8,128)(2,1)}, u32[]{:S(2)}, u32[]{:S(2)}) collective-permute-start(bf16[1552,128]{1,0:T(8,128)(2,1)S(1)} %concatenate.33), channel_id=1, source_target_pairs={{0,0},{20,4},{40,8},{60,12},{16,16},{36,20},{56,24},{12,28},{32,32... | collective-permute-start | bytes 1191944 | tf_op jit(solution)/shard_map/ppermute | solution.py:136
  22.1 43.3 %collective-permute-start.1 = (bf16[1552,128]{1,0:T(8,128)(2,1)S(1)}, bf16[1552,128]{1,0:T(8,128)(2,1)}, u32[]{:S(2)}, u32[]{:S(2)}) collective-permute-start(bf16[1552,128]{1,0:T(8,128)(2,1)S(1)} %concatenate.34), channel_id=1, source_target_pairs={{4,0},{24,4},{44,8},{0,12},{20,16},{40,20},{60,24},{16,28},{36,32}... | collective-permute-start | bytes 1191944 | tf_op jit(solution)/shard_map/ppermute | solution.py:136
  31.6 34.5 %collective-permute-start.2 = (bf16[1552,128]{1,0:T(8,128)(2,1)S(1)}, bf16[1552,128]{1,0:T(8,128)(2,1)}, u32[]{:S(2)}, u32[]{:S(2)}) collective-permute-start(bf16[1552,128]{1,0:T(8,128)(2,1)S(1)} %concatenate.35), channel_id=1, source_target_pairs={{8,0},{28,4},{48,8},{4,12},{24,16},{44,20},{0,24},{20,28},{40,32},... | collective-permute-start | bytes 1191944 | tf_op jit(solution)/shard_map/ppermute | solution.py:136
  36.9 45.0 %collective-permute-start.3 = (bf16[1552,128]{1,0:T(8,128)(2,1)S(1)}, bf16[1552,128]{1,0:T(8,128)(2,1)}, u32[]{:S(2)}, u32[]{:S(2)}) collective-permute-start(bf16[1552,128]{1,0:T(8,128)(2,1)S(1)} %concatenate.36), channel_id=1, source_target_pairs={{12,0},{32,4},{52,8},{8,12},{28,16},{48,20},{4,24},{24,28},{44,32}... | collective-permute-start | bytes 1191944 | tf_op jit(solution)/shard_map/ppermute | solution.py:136
  37.4 51.4 %collective-permute-start.4 = (bf16[1552,128]{1,0:T(8,128)(2,1)S(1)}, bf16[1552,128]{1,0:T(8,128)(2,1)}, u32[]{:S(2)}, u32[]{:S(2)}) collective-permute-start(bf16[1552,128]{1,0:T(8,128)(2,1)S(1)} %concatenate.37), channel_id=1, source_target_pairs={{16,0},{36,4},{56,8},{12,12},{32,16},{52,20},{8,24},{28,28},{48,32... | collective-permute-start | bytes 1191944 | tf_op jit(solution)/shard_map/ppermute | solution.py:136
  92.8 2.6 copy-start.2
  93.9 1.4 copy-start.4
  95.1 0.8 copy-start.6
  96.9 25.1 %collective-permute-start.6 = (bf16[4112,128]{1,0:T(8,128)(2,1)}, bf16[4112,128]{1,0:T(8,128)(2,1)S(1)}, u32[]{:S(2)}, u32[]{:S(2)}) collective-permute-start(bf16[4112,128]{1,0:T(8,128)(2,1)} %pad_maximum_fusion.3), channel_id=1, source_target_pairs={{4,0},{8,4},{12,8},{16,12},{20,16},{24,20},{28,24},{32,28},{36,32}... | collective-permute-start | bytes 3158024 | tf_op jit(solution)/shard_map/ppermute | solution.py:158
  99.3 6.2 %copy-start.7 = (bf16[1536,128]{1,0:T(8,128)(2,1)S(1)}, bf16[1536,128]{1,0:T(8,128)(2,1)}, u32[]{:S(2)}) copy-start(bf16[1536,128]{1,0:T(8,128)(2,1)} %copy-done.6) | copy-start | bytes 1179652
  99.3 6.2 %copy-start.5 = (bf16[1536,128]{1,0:T(8,128)(2,1)S(1)}, bf16[1536,128]{1,0:T(8,128)(2,1)}, u32[]{:S(2)}) copy-start(bf16[1536,128]{1,0:T(8,128)(2,1)} %copy-done.4) | copy-start | bytes 1179652
  99.3 6.3 %copy-start.3 = (bf16[1536,128]{1,0:T(8,128)(2,1)S(1)}, bf16[1536,128]{1,0:T(8,128)(2,1)}, u32[]{:S(2)}) copy-start(bf16[1536,128]{1,0:T(8,128)(2,1)} %copy-done.2) | copy-start | bytes 1179652
  100.5 24.8 %collective-permute-start.5 = (bf16[4112,128]{1,0:T(8,128)(2,1)}, bf16[4112,128]{1,0:T(8,128)(2,1)}, u32[]{:S(2)}, u32[]{:S(2)}) collective-permute-start(bf16[4112,128]{1,0:T(8,128)(2,1)} %pad_maximum_fusion.2), channel_id=1, source_target_pairs={{0,4},{4,8},{8,12},{12,16},{16,20},{20,24},{24,28},{28,32},{32,36}... | collective-permute-start | bytes 3158024 | tf_op jit(solution)/shard_map/ppermute | solution.py:153
  122.0 10.3 %copy-start.1 = (bf16[4112,128]{1,0:T(8,128)(2,1)}, bf16[4112,128]{1,0:T(8,128)(2,1)S(1)}, u32[]{:S(2)}) copy-start(bf16[4112,128]{1,0:T(8,128)(2,1)S(1)} %collective-permute-done.6) | copy-start | bytes 3158020
  126.9 3.1 %copy-start.14 = (s32[45]{0:T(128)S(1)}, s32[45]{0:T(128)}, u32[]{:S(2)}) copy-start(s32[45]{0:T(128)} %eq.85) | copy-start | bytes 544
  126.9 3.1 %copy-start.15 = (s32[45]{0:T(128)S(1)}, s32[45]{0:T(128)}, u32[]{:S(2)}) copy-start(s32[45]{0:T(128)} %min.14) | copy-start | bytes 544
  126.9 3.1 %copy-start.18 = (pred[45]{0:T(512)(128)(4,1)S(1)}, pred[45]{0:T(512)(128)(4,1)}, u32[]{:S(2)}) copy-start(pred[45]{0:T(512)(128)(4,1)} %and.172) | copy-start | bytes 139
  132.3 1.5 slice-start
  182.5 2.1 copy-start.16
  229.5 0.7 copy-start.17
Sparse Core Ops, SparseCore 0:
  229.6 51.2 reduce-scatter.1

commit v5 on v2

--- a/solution.py
+++ b/solution.py
@@ -164,10 +164,14 @@
     p_k = t_kc % ctx_size
     same_head = (t_kc // ctx_size) == (t_q // ctx_size)
     meet = (seg_lo[p_q] <= seg_hi[p_k]) & (seg_lo[p_k] <= seg_hi[p_q])
-    need = (valid & same_head & meet).astype(jnp.int32).reshape(-1)
-    kt = (jj + oo + REACH).astype(jnp.int32).reshape(-1)
+    need_b = (valid & same_head & meet).reshape(-1)
+    need = need_b.astype(jnp.int32)
+    steps = jnp.arange(need.shape[0], dtype=jnp.int32)
+    latest = lax.cummax(jnp.where(need_b, steps, -1), axis=0)
+    source = jnp.where(latest < 0, jnp.argmax(need_b).astype(jnp.int32), latest)
+    kt = (jj + oo + REACH).astype(jnp.int32).reshape(-1)[source]
     qp = p_q[:, 0].astype(jnp.int32)
-    kp = p_k.astype(jnp.int32).reshape(-1)
+    kp = p_k.astype(jnp.int32).reshape(-1)[source]
 
     attended = flash(
         need, qp, kt, kp,

time: 295 us -> 293 us (level)
  waiting for transfers between devices: 124 us -> 110 us
  Pallas kernels: 44.8 us -> 35.7 us
  blocking collectives: 46 us -> 54.6 us
  local copies, waits for them, and re-layouts: 18.8 us -> 25.6 us
  other arithmetic: 6.39 us -> 12.4 us
    ppermute x5, waiting for transfers between devices: 10.8 us -> 1.18 us  [local(): own.append(lax.ppermute(piece, 'ctx', perm))]
    pallas_call x1, Pallas kernels: 44.8 us -> 35.7 us  [flash(): pl.pallas_call(kern, grid_spec=grid_spec, out_shape=jax.ShapeDtypeStruct(...]
    all_to_all x1, blocking collectives: 37 us -> 45.6 us  [local(): got = lax.all_to_all(placed, 'ctx', split_axis=0, concat_axis=0, tiled=True)]
    ppermute x1, waiting for transfers between devices: 19.1 us -> 14.3 us  [local(): lax.ppermute(kv_own[:, slots - REACH:], 'ctx', [(e, e + 1) for e in range...]
  transfers between devices with their start and end apart: 12 -> 12, of which waited for: 6 -> 6; matrix products, arithmetic and copies ran while one was open for 7% -> 11% of each run, Pallas kernels for 0% -> 0%
where the time goes in v5:
time: 293 us; the launch traced here: 292 us
  waiting for transfers between devices  110 us (38%)
  blocking collectives  54.6 us (19%)
  Pallas kernels  35.7 us (12%)
  local copies, waits for them, and re-layouts  25.6 us (9%)
  starting transfers between devices  25.1 us (9%)
  matrix products  14.8 us (5%)
  between operations  13.8 us (5%)
  other arithmetic  12.4 us (4%)
    reduce_scatter x1, waiting for transfers between devices, local(): lax.psum_scatter(head_terms.astype(jnp.bfloat16), 'head', scatter_dimensi...  51.8 us
    all_to_all x1, blocking collectives, local(): got = lax.all_to_all(placed, 'ctx', split_axis=0, concat_axis=0, tiled=True)  45.6 us
    ppermute x4, waiting for transfers between devices, doubling_gather(): lax.ppermute(held, 'ctx', [(e, (e + shift) % size) for e in range(size)])  38.8 us
    pallas_call x1, Pallas kernels, flash(): pl.pallas_call(kern, grid_spec=grid_spec, out_shape=jax.ShapeDtypeStruct(...  35.7 us
    ppermute x5, starting transfers between devices, local(): own.append(lax.ppermute(piece, 'ctx', perm))  16.3 us
    ppermute x1, waiting for transfers between devices, local(): lax.ppermute(kv_own[:, slots - REACH:], 'ctx', [(e, e + 1) for e in range...  14.3 us
    psum x1, blocking collectives, local(): lax.psum((jnp.sum(query_float * query_float, axis=1), jnp.sum(key_float *...  9.03 us
    dot_general x1, matrix products, local(): jnp.dot(owned_attended, out_weight, preferred_element_type=jnp.float32)  8.85 us
  transfers between devices with their start and end apart: 12, of which 6 were waited for; matrix products, arithmetic and copies ran while one was open for 11% of the time, Pallas kernels for 0%

profile of v5, /device:TPU:1, one launch (start us, length us, event | category | flops | bytes accessed | tf_op | source)
XLA Modules:
  0.0 292.0 jit_solution(7906996401895502503)
XLA Ops:
  7.3 2.5 collective-permute-start
  9.8 1.4 copy.47
  12.2 9.0 %all-reduce = (f32[512]{0:T(512)S(1)}, f32[512]{0:T(512)S(1)}) all-reduce(f32[512]{0:T(512)S(1)} %fusion.7, f32[512]{0:T(512)S(1)} %fusion.4), channel_id=1, replica_groups=mesh['batch'=4,'ctx'=16,'head'=4] {'head'}, use_global_device_ids=true, to_apply=%region_5.6 | all-reduce | flops 1024 | bytes 8192 | tf_op jit(solution)/shard_map/psum | solution.py:121
  23.3 8.1 %collective-permute-start.5 = (bf16[3,512,128]{2,1,0:T(8,128)(2,1)S(1)}, bf16[3,512,128]{2,1,0:T(8,128)(2,1)S(1)}, u32[]{:S(2)}, u32[]{:S(2)}) collective-permute-start(bf16[3,512,128]{2,1,0:T(8,128)(2,1)S(1)} %bitcast.73), channel_id=1, source_target_pairs={{4,0},{24,4},{44,8},{0,12},{20,16},{40,20},{60,24},{16,28},{36,32}... | collective-permute-start | bytes 1179656 | tf_op jit(solution)/shard_map/ppermute | solution.py:141
  31.6 5.5 %collective-permute-start.6 = (bf16[3,512,128]{2,1,0:T(8,128)(2,1)S(1)}, bf16[3,512,128]{2,1,0:T(8,128)(2,1)S(1)}, u32[]{:S(2)}, u32[]{:S(2)}) collective-permute-start(bf16[3,512,128]{2,1,0:T(8,128)(2,1)S(1)} %bitcast.74), channel_id=1, source_target_pairs={{8,0},{28,4},{48,8},{4,12},{24,16},{44,20},{0,24},{20,28},{40,32},... | collective-permute-start | bytes 1179656 | tf_op jit(solution)/shard_map/ppermute | solution.py:141
  40.7 30.4 %collective-permute-done.1 = s32[2,2,512]{2,1,0:T(2,128)S(1)} collective-permute-done((s32[2,2,512]{2,1,0:T(2,128)S(1)}, s32[2,2,512]{2,1,0:T(2,128)S(1)}, u32[]{:S(2)}, u32[]{:S(2)}) %collective-permute-start.1) | collective-permute-done | bytes 8224 | tf_op jit(solution)/shard_map/ppermute | solution.py:88
  71.7 8.3 %collective-permute-done.2 = s32[4,2,512]{2,1,0:T(2,128)S(1)} collective-permute-done((s32[4,2,512]{2,1,0:T(2,128)S(1)}, s32[4,2,512]{2,1,0:T(2,128)S(1)}, u32[]{:S(2)}, u32[]{:S(2)}) %collective-permute-start.2) | collective-permute-done | bytes 16416 | tf_op jit(solution)/shard_map/ppermute | solution.py:88
  80.0 2.9 %collective-permute-start.3 = (s32[8,2,512]{2,1,0:T(2,128)S(1)}, s32[8,2,512]{2,1,0:T(2,128)S(1)}, u32[]{:S(2)}, u32[]{:S(2)}) collective-permute-start(s32[8,2,512]{2,1,0:T(2,128)S(1)} %pad_add_fusion), channel_id=1, source_target_pairs={{0,32},{4,36},{8,40},{12,44},{16,48},{20,52},{24,56},{28,60},{32,0... | collective-permute-start | bytes 98312 | tf_op jit(solution)/shard_map/ppermute | solution.py:88
  83.5 1.2 and.226
  84.8 1.4 and.247
  89.8 1.9 collective-permute-start.8
  92.1 1.3 gather_fusion.4
  93.5 1.3 gather_fusion.1
  97.3 1.2 fusion.30
  99.2 1.4 iota_select_fusion
  100.6 1.4 reduce-window.4
  102.0 1.5 fusion.15
  103.5 1.3 gather_fusion.6
  104.8 1.3 gather_fusion.5
  106.1 2.6 copy.55.qs_ref
  109.4 1.2 collective-permute-done.8
  110.8 1.4 collective-permute-start.9
  112.2 1.5 collective-permute-start.10
  114.9 14.3 %collective-permute-done.9 = bf16[2,4,512,128]{3,2,1,0:T(8,128)(2,1)S(1)} collective-permute-done((bf16[2,4,512,128]{3,2,1,0:T(8,128)(2,1)S(1)}, bf16[2,4,512,128]{3,2,1,0:T(8,128)(2,1)S(1)}, u32[]{:S(2)}, u32[]{:S(2)}) %collective-permute-start.9) | collective-permute-done | bytes 1048608 | tf_op jit(solution)/shard_map/ppermute | solution.py:145
  129.2 3.9 %collective-permute-done.10 = bf16[2,4,512,128]{3,2,1,0:T(8,128)(2,1)S(1)} collective-permute-done((bf16[2,4,512,128]{3,2,1,0:T(8,128)(2,1)S(1)}, bf16[2,4,512,128]{3,2,1,0:T(8,128)(2,1)S(1)}, u32[]{:S(2)}, u32[]{:S(2)}) %collective-permute-start.10) | collective-permute-done | bytes 1048608 | tf_op jit(solution)/shard_map/ppermute | solution.py:148
  133.5 2.0 slice_bitcast_fusion
  135.5 35.7 %shard_map.100 = bf16[5,512,128]{2,1,0:T(8,128)(2,1)} custom-call(s32[45]{0:T(128)} %get-tuple-element.11.need_ref, s32[5]{0:T(128)} %and_select_fusion.1.qp_ref, s32[45]{0:T(128)} %gather_fusion.5, s32[45]{0:T(128)} %gather_fusion.6, bf16[5,512,128]{2,1,0:T(8,128)(2,1)} %slice_bitcast_fusion.2.q_ref, bf16[13,512,128]{2,1,0:T(8,128)(2,1)} %get-tuple-element.14.k_ref, ...), custom_call_target="tpu_custom_call" | custom-call | tf_op jit(solution)/shard_map/pallas_call | solution.py:74
  171.2 2.0 fusion.3
  173.3 45.6 %all_to_all.5 = bf16[16,5,32,128]{3,2,1,0:T(8,128)(2,1)S(1)} all-to-all(bf16[16,5,32,128]{3,2,1,0:T(8,128)(2,1)S(1)} %bitcast.59), channel_id=1, replica_groups=mesh['batch'=4,'ctx'=16,'head'=4] {'ctx'}, dimensions={0} | all-to-all | bytes 1310720 | tf_op jit(solution)/shard_map/all_to_all | solution.py:194
  219.4 8.9 %convolution_convert_fusion = bf16[512,5120]{1,0:T(8,128)(2,1)} fusion(bf16[640,5120]{1,0:T(8,128)(2,1)} %param.18, bf16[64,8,5,128]{3,2,1,0:T(8,128)(2,1)S(1)} %bitcast.69), kind=kOutput, calls=%fused_computation.7 | convolution fusion | flops 3358064640 | bytes 12451840 | tf_op jit(solution)/shard_map/dot_general | solution.py:207
  229.7 51.8 %reduce-scatter.2.cloned.1.call-done = bf16[512,1280]{1,0:T(8,128)(2,1)} async-done(((bf16[512,5120]{1,0:T(8,128)(2,1)}), bf16[512,1280]{1,0:T(8,128)(2,1)}) %reduce-scatter.2.cloned.1.call-update) | async-done | bytes 1310736 | tf_op jit(solution)/shard_map/reduce_scatter | solution.py:208
  281.5 3.6 %fusion.1 = bf16[512,1280]{1,0:T(8,128)(2,1)} fusion(f32[6,1280]{1,0:T(8,128)S(1)} %fusion.23, bf16[512,1280]{1,0:T(8,128)(2,1)} %reduce-scatter.2.cloned.1.call-done, s32[512]{0:T(512)S(1)} %eq.112), kind=kOutput, calls=%fused_computation.12 | convolution fusion | flops 49155072 | bytes 2654208 | tf_op jit(solution)/shard_map/dot_general | solution.py:216
  (108 shorter events, 20.5 us)
Async XLA Ops:
  6.5 221.8 %copy-start = (f32[50,1280]{1,0:T(8,128)S(1)}, f32[50,1280]{1,0:T(8,128)}, u32[]{:S(2)}) copy-start(f32[50,1280]{1,0:T(8,128)} %param.19) | copy-start | bytes 768004
  6.5 4.9 %copy-start.1 = (bf16[512,640]{1,0:T(8,128)(2,1)S(1)}, bf16[512,640]{1,0:T(8,128)(2,1)}, u32[]{:S(2)}) copy-start(bf16[512,640]{1,0:T(8,128)(2,1)} %param.11) | copy-start | bytes 1966084
  6.5 275.0 %reduce-scatter.2.cloned.1.call-start = ((), (), s32[]{:S(2)}) async-start(), calls=%async_computation.2 | async-start | bytes 6553600 | tf_op jit(solution)/shard_map/reduce_scatter | solution.py:208
  7.3 32.7 %collective-permute-start = (s32[1,2,512]{2,1,0:T(2,128)S(1)}, s32[1,2,512]{2,1,0:T(2,128)S(1)}, u32[]{:S(2)}, u32[]{:S(2)}) collective-permute-start(s32[1,2,512]{2,1,0:T(2,128)S(1)} %add_bitcast_fusion), channel_id=1, source_target_pairs={{0,4},{4,8},{8,12},{12,16},{16,20},{20,24},{24,28},{28,32},{32,36}... | collective-permute-start | bytes 12296 | tf_op jit(solution)/shard_map/ppermute | solution.py:88
  9.8 2.1 copy-start.2
  11.2 10.0 %copy-start.6 = (f32[640]{0:T(1024)S(1)}, f32[640]{0:T(1024)}, u32[]{:S(2)}) copy-start(f32[640]{0:T(1024)} %param.14) | copy-start | bytes 7684
  11.7 9.7 %copy-start.7 = (f32[640]{0:T(1024)S(1)}, f32[640]{0:T(1024)}, u32[]{:S(2)}) copy-start(f32[640]{0:T(1024)} %param.13) | copy-start | bytes 7684
  22.3 69.5 %copy-start.4 = (s32[512]{0:T(512)S(1)}, s32[512]{0:T(512)}, u32[]{:S(2)}) copy-start(s32[512]{0:T(512)} %param.16) | copy-start | bytes 6148
  22.3 69.5 %copy-start.5 = (s32[512]{0:T(512)S(1)}, s32[512]{0:T(512)}, u32[]{:S(2)}) copy-start(s32[512]{0:T(512)} %param.15) | copy-start | bytes 6148
  22.3 87.1 %collective-permute-start.4 = (bf16[3,512,128]{2,1,0:T(8,128)(2,1)S(1)}, bf16[3,512,128]{2,1,0:T(8,128)(2,1)S(1)}, u32[]{:S(2)}, u32[]{:S(2)}) collective-permute-start(bf16[3,512,128]{2,1,0:T(8,128)(2,1)S(1)} %bitcast.72), channel_id=1, source_target_pairs={{0,0},{20,4},{40,8},{60,12},{16,16},{36,20},{56,24},{12,28},{32,32... | collective-permute-start | bytes 1179656 | tf_op jit(solution)/shard_map/ppermute | solution.py:141
  23.3 86.0 %collective-permute-start.5 = (bf16[3,512,128]{2,1,0:T(8,128)(2,1)S(1)}, bf16[3,512,128]{2,1,0:T(8,128)(2,1)S(1)}, u32[]{:S(2)}, u32[]{:S(2)}) collective-permute-start(bf16[3,512,128]{2,1,0:T(8,128)(2,1)S(1)} %bitcast.73), channel_id=1, source_target_pairs={{4,0},{24,4},{44,8},{0,12},{20,16},{40,20},{60,24},{16,28},{36,32}... | collective-permute-start | bytes 1179656 | tf_op jit(solution)/shard_map/ppermute | solution.py:141
  31.6 77.7 %collective-permute-start.6 = (bf16[3,512,128]{2,1,0:T(8,128)(2,1)S(1)}, bf16[3,512,128]{2,1,0:T(8,128)(2,1)S(1)}, u32[]{:S(2)}, u32[]{:S(2)}) collective-permute-start(bf16[3,512,128]{2,1,0:T(8,128)(2,1)S(1)} %bitcast.74), channel_id=1, source_target_pairs={{8,0},{28,4},{48,8},{4,12},{24,16},{44,20},{0,24},{20,28},{40,32},... | collective-permute-start | bytes 1179656 | tf_op jit(solution)/shard_map/ppermute | solution.py:141
  38.1 71.3 %collective-permute-start.7 = (bf16[3,512,128]{2,1,0:T(8,128)(2,1)}, bf16[3,512,128]{2,1,0:T(8,128)(2,1)S(1)}, u32[]{:S(2)}, u32[]{:S(2)}) collective-permute-start(bf16[3,512,128]{2,1,0:T(8,128)(2,1)} %bitcast.75), channel_id=1, source_target_pairs={{12,0},{32,4},{52,8},{8,12},{28,16},{48,20},{4,24},{24,28},{44,32}... | collective-permute-start | bytes 1179656 | tf_op jit(solution)/shard_map/ppermute | solution.py:141
  39.5 0.5 copy-start.8
  40.0 31.1 %collective-permute-start.1 = (s32[2,2,512]{2,1,0:T(2,128)S(1)}, s32[2,2,512]{2,1,0:T(2,128)S(1)}, u32[]{:S(2)}, u32[]{:S(2)}) collective-permute-start(s32[2,2,512]{2,1,0:T(2,128)S(1)} %pad_add_fusion.2), channel_id=1, source_target_pairs={{0,8},{4,12},{8,16},{12,20},{16,24},{20,28},{24,32},{28,36},{32,40... | collective-permute-start | bytes 24584 | tf_op jit(solution)/shard_map/ppermute | solution.py:88
  71.1 8.9 %collective-permute-start.2 = (s32[4,2,512]{2,1,0:T(2,128)S(1)}, s32[4,2,512]{2,1,0:T(2,128)S(1)}, u32[]{:S(2)}, u32[]{:S(2)}) collective-permute-start(s32[4,2,512]{2,1,0:T(2,128)S(1)} %pad_add_fusion.1), channel_id=1, source_target_pairs={{0,16},{4,20},{8,24},{12,28},{16,32},{20,36},{24,40},{28,44},{32,4... | collective-permute-start | bytes 49160 | tf_op jit(solution)/shard_map/ppermute | solution.py:88
  80.0 9.8 %collective-permute-start.3 = (s32[8,2,512]{2,1,0:T(2,128)S(1)}, s32[8,2,512]{2,1,0:T(2,128)S(1)}, u32[]{:S(2)}, u32[]{:S(2)}) collective-permute-start(s32[8,2,512]{2,1,0:T(2,128)S(1)} %pad_add_fusion), channel_id=1, source_target_pairs={{0,32},{4,36},{8,40},{12,44},{16,48},{20,52},{24,56},{28,60},{32,0... | collective-permute-start | bytes 98312 | tf_op jit(solution)/shard_map/ppermute | solution.py:88
  89.8 20.8 %collective-permute-start.8 = (bf16[3,512,128]{2,1,0:T(8,128)(2,1)}, bf16[3,512,128]{2,1,0:T(8,128)(2,1)S(1)}, u32[]{:S(2)}, u32[]{:S(2)}) collective-permute-start(bf16[3,512,128]{2,1,0:T(8,128)(2,1)} %bitcast.76), channel_id=1, source_target_pairs={{16,0},{36,4},{56,8},{12,12},{32,16},{52,20},{8,24},{28,28},{48,32... | collective-permute-start | bytes 1179656 | tf_op jit(solution)/shard_map/ppermute | solution.py:141
  91.9 14.1 %copy-start.3 = (s32[16,1,512]{2,1,0:T(1,128)}, s32[16,1,512]{2,1,0:T(1,128)S(1)}, u32[]{:S(2)}) copy-start(s32[16,1,512]{2,1,0:T(1,128)S(1)} %get-tuple-element.23.ks_ref) | copy-start | bytes 98308
  110.8 18.4 %collective-permute-start.9 = (bf16[2,4,512,128]{3,2,1,0:T(8,128)(2,1)S(1)}, bf16[2,4,512,128]{3,2,1,0:T(8,128)(2,1)S(1)}, u32[]{:S(2)}, u32[]{:S(2)}) collective-permute-start(bf16[2,4,512,128]{3,2,1,0:T(8,128)(2,1)S(1)} %get-tuple-element.20), channel_id=1, source_target_pairs={{0,4},{4,8},{8,12},{12,16},{16,20},{20,24},{24,28},{28,32},{32,36}... | collective-permute-start | bytes 3145736 | tf_op jit(solution)/shard_map/ppermute | solution.py:145
  112.2 21.0 %collective-permute-start.10 = (bf16[2,4,512,128]{3,2,1,0:T(8,128)(2,1)S(1)}, bf16[2,4,512,128]{3,2,1,0:T(8,128)(2,1)S(1)}, u32[]{:S(2)}, u32[]{:S(2)}) collective-permute-start(bf16[2,4,512,128]{3,2,1,0:T(8,128)(2,1)S(1)} %get-tuple-element.21), channel_id=1, source_target_pairs={{4,0},{8,4},{12,8},{16,12},{20,16},{24,20},{28,24},{32,28},{36,32}... | collective-permute-start | bytes 3145736 | tf_op jit(solution)/shard_map/ppermute | solution.py:148
  228.2 0.7 copy-start.9
Sparse Core Ops, SparseCore 0:
  228.4 53.0 reduce-scatter.1

commit v6 on v5

--- a/solution.py
+++ b/solution.py
@@ -89,6 +89,59 @@
         held = jnp.concatenate([came, held], axis=0)
         shift *= 2
     return jnp.roll(held, me + 1, axis=0)
+
+
+def relay_kernel(src_ref, dst_ref, send_sem, recv_sem, *, slots, size, inverse):
+    me = lax.axis_index("ctx")
+    barrier = pltpu.get_barrier_semaphore()
+    for step in range(1, size):
+        pl.semaphore_signal(
+            barrier, inc=1, device_id={"ctx": lax.rem(me + step, size)},
+            device_id_type=pl.DeviceIdType.MESH,
+        )
+    pl.semaphore_wait(barrier, size - 1)
+    copies = []
+    for j in range(slots):
+        target = lax.rem(inverse * (me - j + size), size)
+        head = (slots * target + j) // size
+        remote = pltpu.make_async_remote_copy(
+            src_ref.at[head], dst_ref.at[j], send_sem.at[j], recv_sem.at[j],
+            device_id={"ctx": target}, device_id_type=pl.DeviceIdType.MESH,
+        )
+        here = pltpu.make_async_copy(src_ref.at[head], dst_ref.at[j], recv_sem.at[j])
+        is_self = target == me
+
+        @pl.when(is_self)
+        def _():
+            here.start()
+
+        @pl.when(jnp.logical_not(is_self))
+        def _():
+            remote.start()
+
+        copies.append((remote, here, is_self))
+    for remote, here, is_self in copies:
+        @pl.when(is_self)
+        def _():
+            here.wait()
+
+        @pl.when(jnp.logical_not(is_self))
+        def _():
+            remote.wait_send()
+            remote.wait_recv()
+
+
+def relay(tiles, slots, size):
+    inverse = pow(slots, -1, size)
+    kern = functools.partial(relay_kernel, slots=slots, size=size, inverse=inverse)
+    return pl.pallas_call(
+        kern,
+        out_shape=jax.ShapeDtypeStruct((slots,) + tiles.shape[1:], tiles.dtype),
+        in_specs=[pl.BlockSpec(memory_space=pl.ANY)],
+        out_specs=pl.BlockSpec(memory_space=pl.ANY),
+        scratch_shapes=[pltpu.SemaphoreType.DMA((slots,)), pltpu.SemaphoreType.DMA((slots,))],
+        compiler_params=pltpu.CompilerParams(collective_id=0, has_side_effects=True),
+    )(tiles)
 
 
 def local(
@@ -131,15 +184,8 @@
     qkv = jnp.stack([queries, normed_keys, value_rows]).reshape(3, row_count, head_count, HD)
     qkv = jnp.transpose(qkv, (0, 2, 1, 3))
 
-    inverse = pow(slots, -1, ctx_size)
-    own = []
-    for j in range(slots):
-        target = lax.rem(inverse * (me - j + ctx_size), ctx_size)
-        head = (slots * target + j) // ctx_size
-        piece = lax.dynamic_index_in_dim(qkv, head, axis=1, keepdims=False)
-        perm = [((slots * e + j) % ctx_size, e) for e in range(ctx_size)]
-        own.append(lax.ppermute(piece, "ctx", perm))
-    own = jnp.stack(own, axis=1)
+    came = relay(jnp.transpose(qkv, (1, 0, 2, 3)), slots, ctx_size)
+    own = jnp.transpose(came, (1, 0, 2, 3))
 
     kv_own = own[1:]
     left = lax.ppermute(

time: 293 us -> 294 us (level)
  Pallas kernels: 35.7 us -> 102 us
  waiting for transfers between devices: 110 us -> 86.9 us
  blocking collectives: 54.6 us -> 35.2 us
  starting transfers between devices: 25.1 us -> 11.3 us
  other arithmetic: 12.4 us -> 8.14 us
  local copies, waits for them, and re-layouts: 25.6 us -> 21.6 us
    pallas_call x0 -> x1, Pallas kernels: none -> 63.4 us  [relay(): pl.pallas_call(kern, out_shape=jax.ShapeDtypeStruct((slots,) + tiles.shap...]
    all_to_all x1, blocking collectives: 45.6 us -> 26.2 us  [local(): got = lax.all_to_all(placed, 'ctx', split_axis=0, concat_axis=0, tiled=True)]
    ppermute x5 -> x0, starting transfers between devices: 16.3 us -> none  [local(): own.append(lax.ppermute(piece, 'ctx', perm))]
    ppermute x4, waiting for transfers between devices: 38.8 us -> 23.5 us  [doubling_gather(): lax.ppermute(held, 'ctx', [(e, (e + shift) % size) for e in range(size)])]
    ppermute x1, waiting for transfers between devices: 14.3 us -> 0.01 us  [local(): lax.ppermute(kv_own[:, slots - REACH:], 'ctx', [(e, e + 1) for e in range...]
    reduce_scatter x1, waiting for transfers between devices: 51.8 us -> 63.3 us  [local(): lax.psum_scatter(head_terms.astype(jnp.bfloat16), 'head', scatter_dimensi...]
    ppermute x1, waiting for transfers between devices: 3.9 us -> 0.01 us  [local(): lax.ppermute(kv_own[:, :REACH], 'ctx', [(e, e - 1) for e in range(1, ctx_...]
    pallas_call x1, Pallas kernels: 35.7 us -> 38.8 us  [flash(): pl.pallas_call(kern, grid_spec=grid_spec, out_shape=jax.ShapeDtypeStruct(...]
  transfers between devices with their start and end apart: 12 -> 7, of which waited for: 6 -> 4; matrix products, arithmetic and copies ran while one was open for 11% -> 8% of each run, Pallas kernels for 0% -> 22%
where the time goes in v6:
time: 294 us
  Pallas kernels  102 us (35%)
  waiting for transfers between devices  86.9 us (30%)
  blocking collectives  35.2 us (12%)
  local copies, waits for them, and re-layouts  21.6 us (7%)
  matrix products  14.8 us (5%)
  between operations  13.7 us (5%)
  starting transfers between devices  11.3 us (4%)
  other arithmetic  8.14 us (3%)
    pallas_call x1, Pallas kernels, relay(): pl.pallas_call(kern, out_shape=jax.ShapeDtypeStruct((slots,) + tiles.shap...  63.4 us
    reduce_scatter x1, waiting for transfers between devices, local(): lax.psum_scatter(head_terms.astype(jnp.bfloat16), 'head', scatter_dimensi...  63.3 us
    pallas_call x1, Pallas kernels, flash(): pl.pallas_call(kern, grid_spec=grid_spec, out_shape=jax.ShapeDtypeStruct(...  38.8 us
    all_to_all x1, blocking collectives, local(): got = lax.all_to_all(placed, 'ctx', split_axis=0, concat_axis=0, tiled=True)  26.2 us
    ppermute x4, waiting for transfers between devices, doubling_gather(): lax.ppermute(held, 'ctx', [(e, (e + shift) % size) for e in range(size)])  23.5 us
    psum x1, blocking collectives, local(): lax.psum((jnp.sum(query_float * query_float, axis=1), jnp.sum(key_float *...  9.02 us
    dot_general x1, matrix products, local(): jnp.dot(owned_attended, out_weight, preferred_element_type=jnp.float32)  8.85 us
    ppermute x4, starting transfers between devices, doubling_gather(): lax.ppermute(held, 'ctx', [(e, (e + shift) % size) for e in range(size)])  8.62 us
  transfers between devices with their start and end apart: 7, of which 4 were waited for; matrix products, arithmetic and copies ran while one was open for 8% of the time, Pallas kernels for 22%

profile of v6, /device:TPU:1, one launch (start us, length us, event | category | flops | bytes accessed | tf_op | source)
XLA Modules:
  0.0 293.7 jit_solution(6934554118671968767)
XLA Ops:
  6.5 0.8 add_bitcast_fusion
  7.3 2.5 collective-permute-start
  9.9 1.3 copy.44
  11.9 9.0 %all-reduce = (f32[512]{0:T(512)S(1)}, f32[512]{0:T(512)S(1)}) all-reduce(f32[512]{0:T(512)S(1)} %fusion.7, f32[512]{0:T(512)S(1)} %fusion.4), channel_id=1, replica_groups=mesh['batch'=4,'ctx'=16,'head'=4] {'head'}, use_global_device_ids=true, to_apply=%region_5.6 | all-reduce | flops 1024 | bytes 8192 | tf_op jit(solution)/shard_map/psum | solution.py:174
  22.7 1.5 maximum_bitcast_fusion.src_ref
  24.2 63.4 %shard_map.100 = bf16[5,3,512,128]{3,2,1,0:T(8,128)(2,1)} custom-call(bf16[5,3,512,128]{3,2,1,0:T(8,128)(2,1)} %maximum_bitcast_fusion.src_ref), custom_call_target="tpu_custom_call" | custom-call | tf_op jit(solution)/shard_map/pallas_call | solution.py:137
  87.6 1.7 copy.65
  89.3 1.7 fusion.31
  91.0 1.3 collective-permute-start.4
  92.4 1.3 collective-permute-start.5
  94.0 0.9 slice_bitcast_fusion.2.q_ref
  95.0 1.2 collective-permute-start.1
  96.3 17.2 %collective-permute-done.1 = s32[2,2,512]{2,1,0:T(2,128)S(1)} collective-permute-done((s32[2,2,512]{2,1,0:T(2,128)S(1)}, s32[2,2,512]{2,1,0:T(2,128)S(1)}, u32[]{:S(2)}, u32[]{:S(2)}) %collective-permute-start.1) | collective-permute-done | bytes 8224 | tf_op jit(solution)/shard_map/ppermute | solution.py:88
  113.5 4.1 %collective-permute-start.2 = (s32[4,2,512]{2,1,0:T(2,128)S(1)}, s32[4,2,512]{2,1,0:T(2,128)S(1)}, u32[]{:S(2)}, u32[]{:S(2)}) collective-permute-start(s32[4,2,512]{2,1,0:T(2,128)S(1)} %pad_add_fusion.1), channel_id=1, source_target_pairs={{0,16},{4,20},{8,24},{12,28},{16,32},{20,36},{24,40},{28,44},{32,4... | collective-permute-start | bytes 49160 | tf_op jit(solution)/shard_map/ppermute | solution.py:88
  117.6 5.1 %collective-permute-done.2 = s32[4,2,512]{2,1,0:T(2,128)S(1)} collective-permute-done((s32[4,2,512]{2,1,0:T(2,128)S(1)}, s32[4,2,512]{2,1,0:T(2,128)S(1)}, u32[]{:S(2)}, u32[]{:S(2)}) %collective-permute-start.2) | collective-permute-done | bytes 16416 | tf_op jit(solution)/shard_map/ppermute | solution.py:88
  122.7 0.8 collective-permute-start.3
  124.5 1.2 slice.60
  125.8 1.2 collective-permute-done.3
  128.7 0.8 gather_fusion.3
  129.5 0.8 gather_fusion.2
  131.3 0.7 iota_reduce_fusion
  132.8 1.3 gather_fusion.6
  134.1 1.3 gather_fusion.5
  135.4 2.6 copy.51.qs_ref
  138.6 1.5 pad_maximum_fusion
  140.1 2.0 slice_bitcast_fusion
  142.1 38.8 %shard_map.101 = bf16[5,512,128]{2,1,0:T(8,128)(2,1)} custom-call(s32[45]{0:T(128)} %get-tuple-element.11.need_ref, s32[5]{0:T(128)} %get-tuple-element.23.qp_ref, s32[45]{0:T(128)} %gather_fusion.5, s32[45]{0:T(128)} %gather_fusion.6, bf16[5,512,128]{2,1,0:T(8,128)(2,1)} %slice_bitcast_fusion.2.q_ref, bf16[13,512,128]{2,1,0:T(8,128)(2,1)} %get-tuple-element.14.k_ref, ...), custom_call_target="tpu_custom_call" | custom-call | tf_op jit(solution)/shard_map/pallas_call | solution.py:74
  180.8 2.0 fusion.3
  182.9 26.2 %all_to_all.5 = bf16[16,5,32,128]{3,2,1,0:T(8,128)(2,1)S(1)} all-to-all(bf16[16,5,32,128]{3,2,1,0:T(8,128)(2,1)S(1)} %bitcast.54), channel_id=1, replica_groups=mesh['batch'=4,'ctx'=16,'head'=4] {'ctx'}, dimensions={0} | all-to-all | bytes 1310720 | tf_op jit(solution)/shard_map/all_to_all | solution.py:240
  209.6 8.9 %convolution_convert_fusion = bf16[512,5120]{1,0:T(8,128)(2,1)} fusion(bf16[640,5120]{1,0:T(8,128)(2,1)} %param.18, bf16[64,8,5,128]{3,2,1,0:T(8,128)(2,1)S(1)} %bitcast.57), kind=kOutput, calls=%fused_computation.7 | convolution fusion | flops 3358064640 | bytes 12451840 | tf_op jit(solution)/shard_map/dot_general | solution.py:253
  220.0 63.3 %reduce-scatter.2.cloned.1.call-done = bf16[512,1280]{1,0:T(8,128)(2,1)} async-done(((bf16[512,5120]{1,0:T(8,128)(2,1)}), bf16[512,1280]{1,0:T(8,128)(2,1)}) %reduce-scatter.2.cloned.1.call-update) | async-done | bytes 1310736 | tf_op jit(solution)/shard_map/reduce_scatter | solution.py:254
  283.3 3.6 %fusion.1 = bf16[512,1280]{1,0:T(8,128)(2,1)} fusion(f32[6,1280]{1,0:T(8,128)S(1)} %fusion.23, bf16[512,1280]{1,0:T(8,128)(2,1)} %reduce-scatter.2.cloned.1.call-done, s32[512]{0:T(512)S(1)} %eq.112), kind=kOutput, calls=%fused_computation.12 | convolution fusion | flops 49155072 | bytes 2654208 | tf_op jit(solution)/shard_map/dot_general | solution.py:262
  (92 shorter events, 10.0 us)
Async XLA Ops:
  6.5 212.1 %copy-start = (f32[50,1280]{1,0:T(8,128)S(1)}, f32[50,1280]{1,0:T(8,128)}, u32[]{:S(2)}) copy-start(f32[50,1280]{1,0:T(8,128)} %param.19) | copy-start | bytes 768004
  6.5 4.9 %copy-start.2 = (bf16[512,640]{1,0:T(8,128)(2,1)S(1)}, bf16[512,640]{1,0:T(8,128)(2,1)}, u32[]{:S(2)}) copy-start(bf16[512,640]{1,0:T(8,128)(2,1)} %param.11) | copy-start | bytes 1966084
  6.5 276.7 %reduce-scatter.2.cloned.1.call-start = ((), (), s32[]{:S(2)}) async-start(), calls=%async_computation.2 | async-start | bytes 6553600 | tf_op jit(solution)/shard_map/reduce_scatter | solution.py:254
  7.3 13.6 %copy-start.7 = (f32[640]{0:T(1024)S(1)}, f32[640]{0:T(1024)}, u32[]{:S(2)}) copy-start(f32[640]{0:T(1024)} %param.14) | copy-start | bytes 7684
  7.3 87.7 %collective-permute-start = (s32[1,2,512]{2,1,0:T(2,128)S(1)}, s32[1,2,512]{2,1,0:T(2,128)S(1)}, u32[]{:S(2)}, u32[]{:S(2)}) collective-permute-start(s32[1,2,512]{2,1,0:T(2,128)S(1)} %add_bitcast_fusion), channel_id=1, source_target_pairs={{0,4},{4,8},{8,12},{12,16},{16,20},{20,24},{24,28},{28,32},{32,36}... | collective-permute-start | bytes 12296 | tf_op jit(solution)/shard_map/ppermute | solution.py:88
  11.7 9.7 %copy-start.8 = (f32[640]{0:T(1024)S(1)}, f32[640]{0:T(1024)}, u32[]{:S(2)}) copy-start(f32[640]{0:T(1024)} %param.13) | copy-start | bytes 7684
  21.1 1.1 copy-start.3
  91.0 47.5 %collective-permute-start.4 = (bf16[2,4,512,128]{3,2,1,0:T(8,128)(2,1)}, bf16[2,4,512,128]{3,2,1,0:T(8,128)(2,1)S(1)}, u32[]{:S(2)}, u32[]{:S(2)}) collective-permute-start(bf16[2,4,512,128]{3,2,1,0:T(8,128)(2,1)} %get-tuple-element.15), channel_id=1, source_target_pairs={{0,4},{4,8},{8,12},{12,16},{16,20},{20,24},{24,28},{28,32},{32,36}... | collective-permute-start | bytes 3145736 | tf_op jit(solution)/shard_map/ppermute | solution.py:191
  92.4 46.2 %collective-permute-start.5 = (bf16[2,4,512,128]{3,2,1,0:T(8,128)(2,1)}, bf16[2,4,512,128]{3,2,1,0:T(8,128)(2,1)}, u32[]{:S(2)}, u32[]{:S(2)}) collective-permute-start(bf16[2,4,512,128]{3,2,1,0:T(8,128)(2,1)} %get-tuple-element.16), channel_id=1, source_target_pairs={{4,0},{8,4},{12,8},{16,12},{20,16},{24,20},{28,24},{32,28},{36,32}... | collective-permute-start | bytes 3145736 | tf_op jit(solution)/shard_map/ppermute | solution.py:194
  93.9 33.1 %copy-start.5 = (s32[512]{0:T(512)S(1)}, s32[512]{0:T(512)}, u32[]{:S(2)}) copy-start(s32[512]{0:T(512)} %param.16) | copy-start | bytes 6148
  94.0 33.1 %copy-start.6 = (s32[512]{0:T(512)S(1)}, s32[512]{0:T(512)}, u32[]{:S(2)}) copy-start(s32[512]{0:T(512)} %param.15) | copy-start | bytes 6148
  95.0 18.4 %collective-permute-start.1 = (s32[2,2,512]{2,1,0:T(2,128)S(1)}, s32[2,2,512]{2,1,0:T(2,128)S(1)}, u32[]{:S(2)}, u32[]{:S(2)}) collective-permute-start(s32[2,2,512]{2,1,0:T(2,128)S(1)} %pad_add_fusion.2), channel_id=1, source_target_pairs={{0,8},{4,12},{8,16},{12,20},{16,24},{20,28},{24,32},{28,36},{32,40... | collective-permute-start | bytes 24584 | tf_op jit(solution)/shard_map/ppermute | solution.py:88
  113.5 9.2 %collective-permute-start.2 = (s32[4,2,512]{2,1,0:T(2,128)S(1)}, s32[4,2,512]{2,1,0:T(2,128)S(1)}, u32[]{:S(2)}, u32[]{:S(2)}) collective-permute-start(s32[4,2,512]{2,1,0:T(2,128)S(1)} %pad_add_fusion.1), channel_id=1, source_target_pairs={{0,16},{4,20},{8,24},{12,28},{16,32},{20,36},{24,40},{28,44},{32,4... | collective-permute-start | bytes 49160 | tf_op jit(solution)/shard_map/ppermute | solution.py:88
  122.7 4.3 %collective-permute-start.3 = (s32[8,2,512]{2,1,0:T(2,128)S(1)}, s32[8,2,512]{2,1,0:T(2,128)S(1)}, u32[]{:S(2)}, u32[]{:S(2)}) collective-permute-start(s32[8,2,512]{2,1,0:T(2,128)S(1)} %pad_add_fusion), channel_id=1, source_target_pairs={{0,32},{4,36},{8,40},{12,44},{16,48},{20,52},{24,56},{28,60},{32,0... | collective-permute-start | bytes 98312 | tf_op jit(solution)/shard_map/ppermute | solution.py:88
  127.2 8.2 %copy-start.4 = (s32[16,1,512]{2,1,0:T(1,128)}, s32[16,1,512]{2,1,0:T(1,128)S(1)}, u32[]{:S(2)}) copy-start(s32[16,1,512]{2,1,0:T(1,128)S(1)} %get-tuple-element.18.ks_ref) | copy-start | bytes 98308
  135.4 3.2 %copy-start.1 = (bf16[2,5,512,128]{3,2,1,0:T(8,128)(2,1)S(1)}, bf16[2,5,512,128]{3,2,1,0:T(8,128)(2,1)}, u32[]{:S(2)}) copy-start(bf16[2,5,512,128]{3,2,1,0:T(8,128)(2,1)} %slice.60) | copy-start | bytes 3932164
  218.5 0.7 copy-start.9
Sparse Core Ops, SparseCore 0:
  218.6 64.5 reduce-scatter.1

commit v7 on v4

--- a/solution.py
+++ b/solution.py
@@ -79,6 +79,59 @@
             dimension_semantics=("arbitrary", "arbitrary")
         ),
     )(need, qp, kt, kp, q_tiles, k_tiles, v_tiles, seg_rows, seg_cols)
+
+
+def relay_kernel(src_ref, dst_ref, send_sem, recv_sem, *, slots, size, inverse):
+    me = lax.axis_index("ctx")
+    barrier = pltpu.get_barrier_semaphore()
+    for step in range(1, size):
+        pl.semaphore_signal(
+            barrier, inc=1, device_id={"ctx": lax.rem(me + step, size)},
+            device_id_type=pl.DeviceIdType.MESH,
+        )
+    pl.semaphore_wait(barrier, size - 1)
+    copies = []
+    for j in range(slots):
+        target = lax.rem(inverse * (me - j + size), size)
+        head = (slots * target + j) // size
+        remote = pltpu.make_async_remote_copy(
+            src_ref.at[head], dst_ref.at[j], send_sem.at[j], recv_sem.at[j],
+            device_id={"ctx": target}, device_id_type=pl.DeviceIdType.MESH,
+        )
+        here = pltpu.make_async_copy(src_ref.at[head], dst_ref.at[j], recv_sem.at[j])
+        is_self = target == me
+
+        @pl.when(is_self)
+        def _():
+            here.start()
+
+        @pl.when(jnp.logical_not(is_self))
+        def _():
+            remote.start()
+
+        copies.append((remote, here, is_self))
+    for remote, here, is_self in copies:
+        @pl.when(is_self)
+        def _():
+            here.wait()
+
+        @pl.when(jnp.logical_not(is_self))
+        def _():
+            remote.wait_send()
+            remote.wait_recv()
+
+
+def relay(tiles, slots, size):
+    inverse = pow(slots, -1, size)
+    kern = functools.partial(relay_kernel, slots=slots, size=size, inverse=inverse)
+    return pl.pallas_call(
+        kern,
+        out_shape=jax.ShapeDtypeStruct((slots,) + tiles.shape[1:], tiles.dtype),
+        in_specs=[pl.BlockSpec(memory_space=pl.ANY)],
+        out_specs=pl.BlockSpec(memory_space=pl.ANY),
+        scratch_shapes=[pltpu.SemaphoreType.DMA((slots,)), pltpu.SemaphoreType.DMA((slots,))],
+        compiler_params=pltpu.CompilerParams(collective_id=0, has_side_effects=True),
+    )(tiles)
 
 
 def local(
@@ -122,22 +175,19 @@
     body_rows = 3 * row_count
     pad = (-(body_rows + meta.shape[0])) % 16
 
-    inverse = pow(slots, -1, ctx_size)
-    own = []
-    own_meta = []
-    for j in range(slots):
-        target = lax.rem(inverse * (me - j + ctx_size), ctx_size)
-        head = (slots * target + j) // ctx_size
-        piece = lax.dynamic_index_in_dim(qkv, head, axis=1, keepdims=False)
-        piece = jnp.concatenate(
-            [piece.reshape(body_rows, HD), meta, jnp.zeros((pad, HD), jnp.bfloat16)], axis=0
-        )
-        perm = [((slots * e + j) % ctx_size, e) for e in range(ctx_size)]
-        came = lax.ppermute(piece, "ctx", perm)
-        own.append(came[:body_rows].reshape(3, row_count, HD))
-        own_meta.append(came[body_rows:body_rows + meta.shape[0]].reshape(3, row_count))
-    own = jnp.stack(own, axis=1)
-    own_meta = jnp.stack(own_meta, axis=1).astype(jnp.int32)
+    meta_rows = meta.shape[0]
+    sendable = jnp.concatenate(
+        [
+            jnp.transpose(qkv, (1, 0, 2, 3)).reshape(head_count, body_rows, HD),
+            jnp.broadcast_to(meta[None], (head_count, meta_rows, HD)),
+            jnp.zeros((head_count, pad, HD), jnp.bfloat16),
+        ],
+        axis=1,
+    )
+    came = relay(sendable, slots, ctx_size)
+    own = came[:, :body_rows].reshape(slots, 3, row_count, HD).transpose(1, 0, 2, 3)
+    own_meta = came[:, body_rows:body_rows + meta_rows].reshape(slots, 3, row_count)
+    own_meta = own_meta.transpose(1, 0, 2).astype(jnp.int32)
     seg_own = own_meta[0]
     dest_own = own_meta[1] * 64 + own_meta[2]
 

time: 292 us -> 306 us (1.048)
  Pallas kernels: 42.6 us -> 111 us
  waiting for transfers between devices: 109 us -> 69.2 us
  starting transfers between devices: 26.1 us -> 5.32 us
  local copies, waits for them, and re-layouts: 31 us -> 35.7 us
    pallas_call x0 -> x1, Pallas kernels: none -> 68.7 us  [relay(): pl.pallas_call(kern, out_shape=jax.ShapeDtypeStruct((slots,) + tiles.shap...]
    ppermute x5 -> x0, waiting for transfers between devices: 40.6 us -> none  [local(): came = lax.ppermute(piece, 'ctx', perm)]
    ppermute x5 -> x0, starting transfers between devices: 19.8 us -> none  [local(): came = lax.ppermute(piece, 'ctx', perm)]
    concatenate x5 -> x1, local copies, waits for them, and re-layouts: 0.94 us -> 10.9 us  [local(): jnp.concatenate([jnp.transpose(qkv, (1, 0, 2, 3)).reshape(head_count, bod...]
    slice x10 -> x2, local copies, waits for them, and re-layouts: 8.79 us -> 3.2 us  [the longest x1 2.95 us: local(): came[:, :body_rows].reshape(slots, 3, row_count, HD).transpose(1, 0, 2, 3)]
  transfers between devices with their start and end apart: 8 -> 3, of which waited for: 6 -> 3; matrix products, arithmetic and copies ran while one was open for 4% -> 2% of each run, Pallas kernels for 0% -> 0%
where the time goes in v7:
time: 306 us; the launch traced here: 305 us
  Pallas kernels  111 us (36%)
  waiting for transfers between devices  69.2 us (23%)
  blocking collectives  45.7 us (15%)
  local copies, waits for them, and re-layouts  35.7 us (12%)
  matrix products  15.7 us (5%)
  between operations  13.8 us (5%)
  other arithmetic  8.16 us (3%)
  starting transfers between devices  5.32 us (2%)
    pallas_call x1, Pallas kernels, relay(): pl.pallas_call(kern, out_shape=jax.ShapeDtypeStruct((slots,) + tiles.shap...  68.7 us
    reduce_scatter x1, waiting for transfers between devices, local(): lax.psum_scatter(head_terms.astype(jnp.bfloat16), 'head', scatter_dimensi...  52.7 us
    pallas_call x1, Pallas kernels, flash(): pl.pallas_call(kern, grid_spec=grid_spec, out_shape=jax.ShapeDtypeStruct(...  42.6 us
    all_to_all x1, blocking collectives, local(): lax.all_to_all(payload, 'ctx', split_axis=0, concat_axis=0, tiled=True)  36.2 us
    ppermute x1, waiting for transfers between devices, local(): lax.ppermute(halo(kv_own[:, :REACH], seg_own_b[:REACH]), 'ctx', [(e, e -...  15.2 us
    concatenate x1, local copies, waits for them, and re-layouts, local(): jnp.concatenate([jnp.transpose(qkv, (1, 0, 2, 3)).reshape(head_count, bod...  10.9 us
    psum x1, blocking collectives, local(): lax.psum((jnp.sum(query_float * query_float, axis=1), jnp.sum(key_float *...  9.55 us
    dot_general x1, matrix products, local(): jnp.dot(owned_attended, out_weight, preferred_element_type=jnp.float32)  8.85 us
  transfers between devices with their start and end apart: 3, of which 3 were waited for; matrix products, arithmetic and copies ran while one was open for 2% of the time, Pallas kernels for 0%

profile of v7, /device:TPU:1, one launch (start us, length us, event | category | flops | bytes accessed | tf_op | source)
XLA Modules:
  0.0 304.9 jit_solution(6450222220426412541)
XLA Ops:
  6.5 1.5 copy.24
  8.9 9.6 %all-reduce.1 = (f32[512]{0:T(512)S(1)}, f32[512]{0:T(512)S(1)}) all-reduce(f32[512]{0:T(512)S(1)} %fusion.9, f32[512]{0:T(512)S(1)} %fusion.6), channel_id=1, replica_groups=mesh['batch'=4,'ctx'=16,'head'=4] {'head'}, use_global_device_ids=true, to_apply=%region_3.0 | all-reduce | flops 1024 | bytes 8192 | tf_op jit(solution)/shard_map/psum | solution.py:161
  19.1 2.3 copy.25
  21.5 10.9 %concatenate.19.src_ref = bf16[5,1552,128]{2,1,0:T(8,128)(2,1)} concatenate(bf16[5,1536,128]{2,1,0:T(8,128)(2,1)} %bitcast.66, bf16[5,12,128]{2,1,0:T(8,128)(2,1)S(1)} %broadcast_in_dim.12, bf16[5,4,128]{2,1,0:T(4,128)(2,1)S(1)} %broadcast_in_dim.13), dimensions={1} | concatenate | bytes 3973120 | tf_op jit(solution)/shard_map/concatenate | solution.py:179
  32.4 68.7 %shard_map.100 = bf16[5,1552,128]{2,1,0:T(8,128)(2,1)} custom-call(bf16[5,1552,128]{2,1,0:T(8,128)(2,1)} %concatenate.19.src_ref), custom_call_target="tpu_custom_call" | custom-call | tf_op jit(solution)/shard_map/pallas_call | solution.py:127
  101.1 0.7 slice_convert_fusion
  101.9 3.0 slice.76
  104.9 1.7 copy.53
  106.8 1.1 pad_maximum_fusion.2
  107.9 1.3 collective-permute-start.1
  109.2 1.1 pad_maximum_fusion.1
  110.3 4.0 %collective-permute-start = (bf16[4112,128]{1,0:T(8,128)(2,1)}, bf16[4112,128]{1,0:T(8,128)(2,1)S(1)}, u32[]{:S(2)}, u32[]{:S(2)}) collective-permute-start(bf16[4112,128]{1,0:T(8,128)(2,1)} %pad_maximum_fusion.1), channel_id=1, source_target_pairs={{0,4},{4,8},{8,12},{12,16},{16,20},{20,24},{24,28},{28,32},{32,36}... | collective-permute-start | bytes 3158024 | tf_op jit(solution)/shard_map/ppermute | solution.py:203
  115.1 1.2 slice.119
  116.3 0.9 fusion
  118.3 0.9 slice_bitcast_fusion.2.q_ref
  119.2 15.2 %collective-permute-done.1 = bf16[4112,128]{1,0:T(8,128)(2,1)} collective-permute-done((bf16[4112,128]{1,0:T(8,128)(2,1)}, bf16[4112,128]{1,0:T(8,128)(2,1)}, u32[]{:S(2)}, u32[]{:S(2)}) %collective-permute-start.1) | collective-permute-done | bytes 1052704 | tf_op jit(solution)/shard_map/ppermute | solution.py:208
  134.4 0.7 slice_convert_fusion.2
  135.1 1.2 collective-permute-done
  136.6 0.8 gather_fusion.2
  137.4 0.8 gather_fusion.1
  141.0 0.7 iota_reduce_fusion
  141.8 0.7 fusion.17
  142.6 1.4 slice.120
  144.6 2.0 slice_bitcast_fusion
  146.6 2.3 copy.35.qs_ref
  148.9 1.2 gather_fusion.4
  150.2 42.6 %shard_map.101 = bf16[5,512,128]{2,1,0:T(8,128)(2,1)} custom-call(s32[45]{0:T(128)} %get-tuple-element.11.need_ref, s32[5]{0:T(128)} %iota_add_fusion.2.qp_ref, s32[45]{0:T(128)} %gather_fusion.4, s32[45]{0:T(128)} %gather_fusion.4, bf16[5,512,128]{2,1,0:T(8,128)(2,1)} %slice_bitcast_fusion.2.q_ref, bf16[13,512,128]{2,1,0:T(8,128)(2,1)} %get-tuple-element.14.k_ref, ...), custom_call_target="tpu_custom_call" | custom-call | tf_op jit(solution)/shard_map/pallas_call | solution.py:74
  192.7 2.0 fusion.5
  195.0 36.2 %all_to_all.5 = bf16[16,176,128]{2,1,0:T(8,128)(2,1)S(1)} all-to-all(bf16[16,176,128]{2,1,0:T(8,128)(2,1)S(1)} %maximum_maximum_fusion), channel_id=1, replica_groups=mesh['batch'=4,'ctx'=16,'head'=4] {'ctx'}, dimensions={0} | all-to-all | bytes 1441792 | tf_op jit(solution)/shard_map/all_to_all | solution.py:277
  231.7 8.9 %convolution_convert_fusion = bf16[512,5120]{1,0:T(8,128)(2,1)} fusion(bf16[640,5120]{1,0:T(8,128)(2,1)} %param.18, bf16[64,8,5,128]{3,2,1,0:T(8,128)(2,1)S(1)} %bitcast.76), kind=kOutput, calls=%fused_computation.5 | convolution fusion | flops 3358064640 | bytes 12451840 | tf_op jit(solution)/shard_map/dot_general | solution.py:285
  241.7 52.7 %reduce-scatter.2.cloned.1.call-done = bf16[512,1280]{1,0:T(8,128)(2,1)} async-done(((bf16[512,5120]{1,0:T(8,128)(2,1)}), bf16[512,1280]{1,0:T(8,128)(2,1)}) %reduce-scatter.2.cloned.1.call-update) | async-done | bytes 1310736 | tf_op jit(solution)/shard_map/reduce_scatter | solution.py:286
  294.4 3.6 %fusion.2 = bf16[512,1280]{1,0:T(8,128)(2,1)} fusion(f32[6,1280]{1,0:T(8,128)S(1)} %fusion.26, bf16[512,1280]{1,0:T(8,128)(2,1)} %reduce-scatter.2.cloned.1.call-done, s32[512]{0:T(512)S(1)} %reshape.461), kind=kOutput, calls=%fused_computation.11 | convolution fusion | flops 49155072 | bytes 2654208 | tf_op jit(solution)/shard_map/dot_general | solution.py:294
  (100 shorter events, 9.4 us)
Async XLA Ops:
  6.5 234.1 %copy-start = (f32[50,1280]{1,0:T(8,128)S(1)}, f32[50,1280]{1,0:T(8,128)}, u32[]{:S(2)}) copy-start(f32[50,1280]{1,0:T(8,128)} %param.19) | copy-start | bytes 768004
  6.5 1.5 copy-start.2
  6.5 1.9 copy-start.3
  6.5 287.9 %reduce-scatter.2.cloned.1.call-start = ((), (), s32[]{:S(2)}) async-start(), calls=%async_computation.2 | async-start | bytes 6553600 | tf_op jit(solution)/shard_map/reduce_scatter | solution.py:286
  8.0 10.5 %copy-start.4 = (f32[640]{0:T(1024)S(1)}, f32[640]{0:T(1024)}, u32[]{:S(2)}) copy-start(f32[640]{0:T(1024)} %param.14) | copy-start | bytes 7684
  8.5 10.2 %copy-start.5 = (f32[640]{0:T(1024)S(1)}, f32[640]{0:T(1024)}, u32[]{:S(2)}) copy-start(f32[640]{0:T(1024)} %param.13) | copy-start | bytes 7684
  19.1 2.3 copy-start.7
  19.1 2.3 copy-start.6
  107.9 26.5 %collective-permute-start.1 = (bf16[4112,128]{1,0:T(8,128)(2,1)}, bf16[4112,128]{1,0:T(8,128)(2,1)}, u32[]{:S(2)}, u32[]{:S(2)}) collective-permute-start(bf16[4112,128]{1,0:T(8,128)(2,1)} %pad_maximum_fusion.2), channel_id=1, source_target_pairs={{4,0},{8,4},{12,8},{16,12},{20,16},{24,20},{28,24},{32,28},{36,32}... | collective-permute-start | bytes 3158024 | tf_op jit(solution)/shard_map/ppermute | solution.py:208
  110.3 26.1 %collective-permute-start = (bf16[4112,128]{1,0:T(8,128)(2,1)}, bf16[4112,128]{1,0:T(8,128)(2,1)S(1)}, u32[]{:S(2)}, u32[]{:S(2)}) collective-permute-start(bf16[4112,128]{1,0:T(8,128)(2,1)} %pad_maximum_fusion.1), channel_id=1, source_target_pairs={{0,4},{4,8},{8,12},{12,16},{16,20},{20,24},{24,28},{28,32},{32,36}... | collective-permute-start | bytes 3158024 | tf_op jit(solution)/shard_map/ppermute | solution.py:203
  142.6 1.6 copy-start.1
  240.6 0.7 copy-start.8
Sparse Core Ops, SparseCore 0:
  240.7 53.6 reduce-scatter.1

commit v8 on v6

--- a/solution.py
+++ b/solution.py
@@ -81,17 +81,8 @@
     )(need, qp, kt, kp, q_tiles, k_tiles, v_tiles, seg_rows, seg_cols)
 
 
-def doubling_gather(piece, me, size):
-    held = piece[None]
-    shift = 1
-    while shift < size:
-        came = lax.ppermute(held, "ctx", [(e, (e + shift) % size) for e in range(size)])
-        held = jnp.concatenate([came, held], axis=0)
-        shift *= 2
-    return jnp.roll(held, me + 1, axis=0)
-
-
-def relay_kernel(src_ref, dst_ref, send_sem, recv_sem, *, slots, size, inverse):
+def relay_kernel(src_ref, mark_ref, dst_ref, marks_ref, send_sem, recv_sem, mark_send, mark_recv, self_sem,
+                 *, slots, size, inverse):
     me = lax.axis_index("ctx")
     barrier = pltpu.get_barrier_semaphore()
     for step in range(1, size):
@@ -120,6 +111,16 @@
             remote.start()
 
         copies.append((remote, here, is_self))
+    mark_copies = []
+    for step in range(1, size):
+        sent = pltpu.make_async_remote_copy(
+            mark_ref, marks_ref.at[me], mark_send.at[step - 1], mark_recv.at[step - 1],
+            device_id={"ctx": lax.rem(me + step, size)}, device_id_type=pl.DeviceIdType.MESH,
+        )
+        sent.start()
+        mark_copies.append(sent)
+    mine = pltpu.make_async_copy(mark_ref, marks_ref.at[me], self_sem.at[0])
+    mine.start()
     for remote, here, is_self in copies:
         @pl.when(is_self)
         def _():
@@ -130,18 +131,32 @@
             remote.wait_send()
             remote.wait_recv()
 
-
-def relay(tiles, slots, size):
+    for sent in mark_copies:
+        sent.wait_send()
+        sent.wait_recv()
+    mine.wait()
+
+
+def relay(tiles, marks, slots, size):
     inverse = pow(slots, -1, size)
     kern = functools.partial(relay_kernel, slots=slots, size=size, inverse=inverse)
     return pl.pallas_call(
         kern,
-        out_shape=jax.ShapeDtypeStruct((slots,) + tiles.shape[1:], tiles.dtype),
-        in_specs=[pl.BlockSpec(memory_space=pl.ANY)],
-        out_specs=pl.BlockSpec(memory_space=pl.ANY),
-        scratch_shapes=[pltpu.SemaphoreType.DMA((slots,)), pltpu.SemaphoreType.DMA((slots,))],
+        out_shape=(
+            jax.ShapeDtypeStruct((slots,) + tiles.shape[1:], tiles.dtype),
+            jax.ShapeDtypeStruct((size,) + marks.shape, marks.dtype),
+        ),
+        in_specs=[pl.BlockSpec(memory_space=pl.ANY), pl.BlockSpec(memory_space=pl.ANY)],
+        out_specs=(pl.BlockSpec(memory_space=pl.ANY), pl.BlockSpec(memory_space=pl.ANY)),
+        scratch_shapes=[
+            pltpu.SemaphoreType.DMA((slots,)),
+            pltpu.SemaphoreType.DMA((slots,)),
+            pltpu.SemaphoreType.DMA((size - 1,)),
+            pltpu.SemaphoreType.DMA((size - 1,)),
+            pltpu.SemaphoreType.DMA((1,)),
+        ],
         compiler_params=pltpu.CompilerParams(collective_id=0, has_side_effects=True),
-    )(tiles)
+    )(tiles, marks)
 
 
 def local(
@@ -166,9 +181,6 @@
     tiles = head_count * ctx_size
     slots = tiles // ctx_size
 
-    marks = doubling_gather(jnp.stack([segment, destination]), me, ctx_size)
-    seg_blocks = marks[:, 0]
-    dest_blocks = marks[:, 1]
     query_float = query_raw.astype(jnp.float32)
     key_float = key_raw.astype(jnp.float32)
     query_sum, key_sum = lax.psum(
@@ -184,7 +196,11 @@
     qkv = jnp.stack([queries, normed_keys, value_rows]).reshape(3, row_count, head_count, HD)
     qkv = jnp.transpose(qkv, (0, 2, 1, 3))
 
-    came = relay(jnp.transpose(qkv, (1, 0, 2, 3)), slots, ctx_size)
+    came, marks = relay(
+        jnp.transpose(qkv, (1, 0, 2, 3)), jnp.stack([segment, destination]), slots, ctx_size
+    )
+    seg_blocks = marks[:, 0]
+    dest_blocks = marks[:, 1]
     own = jnp.transpose(came, (1, 0, 2, 3))
 
     kv_own = own[1:]

time: 294 us -> 280 us (0.952)
  waiting for transfers between devices: 86.9 us -> 64.2 us
  Pallas kernels: 102 us -> 114 us
  starting transfers between devices: 11.3 us -> 5.01 us
    ppermute x4 -> x0, waiting for transfers between devices: 23.5 us -> none  [doubling_gather(): lax.ppermute(held, 'ctx', [(e, (e + shift) % size) for e in range(size)])]
    ppermute x4 -> x0, starting transfers between devices: 8.62 us -> none  [doubling_gather(): lax.ppermute(held, 'ctx', [(e, (e + shift) % size) for e in range(size)])]
    reduce_scatter x1, waiting for transfers between devices: 63.3 us -> 56 us  [local(): lax.psum_scatter(head_terms.astype(jnp.bfloat16), 'head', scatter_dimensi...]
    pallas_call x1, Pallas kernels: 63.4 us -> 69.5 us  [relay(): pl.pallas_call(kern, out_shape=(jax.ShapeDtypeStruct((slots,) + tiles.sha...]
    pallas_call x1, Pallas kernels: 38.8 us -> 44.7 us  [flash(): pl.pallas_call(kern, grid_spec=grid_spec, out_shape=jax.ShapeDtypeStruct(...]
    ppermute x1, waiting for transfers between devices: 0.01 us -> 4.39 us  [local(): lax.ppermute(kv_own[:, slots - REACH:], 'ctx', [(e, e + 1) for e in range...]
    ppermute x1, waiting for transfers between devices: 0.01 us -> 3.88 us  [local(): lax.ppermute(kv_own[:, :REACH], 'ctx', [(e, e - 1) for e in range(1, ctx_...]
  transfers between devices with their start and end apart: 7 -> 3, of which waited for: 4 -> 3; matrix products, arithmetic and copies ran while one was open for 8% -> 6% of each run, Pallas kernels for 22% -> 0%
where the time goes in v8:
time: 280 us
  Pallas kernels  114 us (41%)
  waiting for transfers between devices  64.2 us (23%)
  blocking collectives  37.1 us (13%)
  local copies, waits for them, and re-layouts  22.9 us (8%)
  matrix products  14.8 us (5%)
  between operations  13.7 us (5%)
  other arithmetic  8.03 us (3%)
  starting transfers between devices  5.01 us (2%)
    pallas_call x1, Pallas kernels, relay(): pl.pallas_call(kern, out_shape=(jax.ShapeDtypeStruct((slots,) + tiles.sha...  69.5 us
    reduce_scatter x1, waiting for transfers between devices, local(): lax.psum_scatter(head_terms.astype(jnp.bfloat16), 'head', scatter_dimensi...  56 us
    pallas_call x1, Pallas kernels, flash(): pl.pallas_call(kern, grid_spec=grid_spec, out_shape=jax.ShapeDtypeStruct(...  44.7 us
    all_to_all x1, blocking collectives, local(): got = lax.all_to_all(placed, 'ctx', split_axis=0, concat_axis=0, tiled=True)  27.5 us
    psum x1, blocking collectives, local(): lax.psum((jnp.sum(query_float * query_float, axis=1), jnp.sum(key_float *...  9.55 us
    dot_general x1, matrix products, local(): jnp.dot(owned_attended, out_weight, preferred_element_type=jnp.float32)  8.85 us
  transfers between devices with their start and end apart: 3, of which 3 were waited for; matrix products, arithmetic and copies ran while one was open for 6% of the time, Pallas kernels for 0%

profile of v8, /device:TPU:1, one launch (start us, length us, event | category | flops | bytes accessed | tf_op | source)
XLA Modules:
  0.0 279.8 jit_solution(2595956068829854080)
XLA Ops:
  6.5 1.4 copy.37
  8.6 9.6 %all-reduce = (f32[512]{0:T(512)S(1)}, f32[512]{0:T(512)S(1)}) all-reduce(f32[512]{0:T(512)S(1)} %fusion.7, f32[512]{0:T(512)S(1)} %fusion.4), channel_id=1, replica_groups=mesh['batch'=4,'ctx'=16,'head'=4] {'head'}, use_global_device_ids=true, to_apply=%region_3.0 | all-reduce | flops 1024 | bytes 8192 | tf_op jit(solution)/shard_map/psum | solution.py:186
  19.3 1.3 copy.39
  20.9 0.6 pad_add_fusion.mark_ref
  21.6 1.5 maximum_bitcast_fusion.src_ref
  23.0 69.5 %shard_map.100 = (bf16[5,3,512,128]{3,2,1,0:T(8,128)(2,1)}, s32[16,2,512]{2,1,0:T(2,128)}) custom-call(bf16[5,3,512,128]{3,2,1,0:T(8,128)(2,1)} %maximum_bitcast_fusion.src_ref, s32[2,512]{1,0:T(2,128)} %pad_add_fusion.mark_ref), custom_call_target="tpu_custom_call" | custom-call | tf_op jit(solution)/shard_map/pallas_call | solution.py:143
  92.5 1.7 copy.65
  94.2 1.7 fusion.31
  95.9 3.7 %collective-permute-start = (bf16[2,4,512,128]{3,2,1,0:T(8,128)(2,1)}, bf16[2,4,512,128]{3,2,1,0:T(8,128)(2,1)S(1)}, u32[]{:S(2)}, u32[]{:S(2)}) collective-permute-start(bf16[2,4,512,128]{3,2,1,0:T(8,128)(2,1)} %get-tuple-element.19), channel_id=1, source_target_pairs={{0,4},{4,8},{8,12},{12,16},{16,20},{20,24},{24,28},{28,32},{32,36}... | collective-permute-start | bytes 3145736 | tf_op jit(solution)/shard_map/ppermute | solution.py:207
  99.6 1.3 collective-permute-start.1
  102.4 1.0 fusion.32
  103.6 0.7 gather_fusion.4
  104.3 0.6 gather_fusion.1
  104.9 0.8 gather_fusion.3
  105.7 0.8 gather_fusion.2
  107.5 0.7 iota_reduce_fusion
  108.3 0.8 fusion.15
  109.1 1.2 slice.60
  110.3 1.3 gather_fusion.6
  111.7 1.3 gather_fusion.5
  112.9 2.6 copy.51.qs_ref
  116.2 0.9 slice_bitcast_fusion.2.q_ref
  117.0 4.4 %collective-permute-done = bf16[2,4,512,128]{3,2,1,0:T(8,128)(2,1)S(1)} collective-permute-done((bf16[2,4,512,128]{3,2,1,0:T(8,128)(2,1)}, bf16[2,4,512,128]{3,2,1,0:T(8,128)(2,1)S(1)}, u32[]{:S(2)}, u32[]{:S(2)}) %collective-permute-start) | collective-permute-done | bytes 1048608 | tf_op jit(solution)/shard_map/ppermute | solution.py:207
  121.4 3.9 %collective-permute-done.1 = bf16[2,4,512,128]{3,2,1,0:T(8,128)(2,1)} collective-permute-done((bf16[2,4,512,128]{3,2,1,0:T(8,128)(2,1)}, bf16[2,4,512,128]{3,2,1,0:T(8,128)(2,1)}, u32[]{:S(2)}, u32[]{:S(2)}) %collective-permute-start.1) | collective-permute-done | bytes 1048608 | tf_op jit(solution)/shard_map/ppermute | solution.py:210
  125.3 1.5 pad_maximum_fusion
  126.8 2.0 slice_bitcast_fusion
  128.8 44.7 %shard_map.101 = bf16[5,512,128]{2,1,0:T(8,128)(2,1)} custom-call(s32[45]{0:T(128)} %get-tuple-element.15.need_ref, s32[5]{0:T(128)} %get-tuple-element.28.qp_ref, s32[45]{0:T(128)} %gather_fusion.5, s32[45]{0:T(128)} %gather_fusion.6, bf16[5,512,128]{2,1,0:T(8,128)(2,1)} %slice_bitcast_fusion.2.q_ref, bf16[13,512,128]{2,1,0:T(8,128)(2,1)} %get-tuple-element.18.k_ref, ...), custom_call_target="tpu_custom_call" | custom-call | tf_op jit(solution)/shard_map/pallas_call | solution.py:74
  173.5 2.0 fusion.3
  175.6 27.5 %all_to_all.5 = bf16[16,5,32,128]{3,2,1,0:T(8,128)(2,1)S(1)} all-to-all(bf16[16,5,32,128]{3,2,1,0:T(8,128)(2,1)S(1)} %bitcast.51), channel_id=1, replica_groups=mesh['batch'=4,'ctx'=16,'head'=4] {'ctx'}, dimensions={0} | all-to-all | bytes 1310720 | tf_op jit(solution)/shard_map/all_to_all | solution.py:256
  203.6 8.9 %convolution_convert_fusion = bf16[512,5120]{1,0:T(8,128)(2,1)} fusion(bf16[640,5120]{1,0:T(8,128)(2,1)} %param.18, bf16[64,8,5,128]{3,2,1,0:T(8,128)(2,1)S(1)} %bitcast.56), kind=kOutput, calls=%fused_computation.7 | convolution fusion | flops 3358064640 | bytes 12451840 | tf_op jit(solution)/shard_map/dot_general | solution.py:269
  213.4 56.0 %reduce-scatter.2.cloned.1.call-done = bf16[512,1280]{1,0:T(8,128)(2,1)} async-done(((bf16[512,5120]{1,0:T(8,128)(2,1)}), bf16[512,1280]{1,0:T(8,128)(2,1)}) %reduce-scatter.2.cloned.1.call-update) | async-done | bytes 1310736 | tf_op jit(solution)/shard_map/reduce_scatter | solution.py:270
  269.3 3.6 %fusion.1 = bf16[512,1280]{1,0:T(8,128)(2,1)} fusion(f32[6,1280]{1,0:T(8,128)S(1)} %fusion.23, bf16[512,1280]{1,0:T(8,128)(2,1)} %reduce-scatter.2.cloned.1.call-done, s32[512]{0:T(512)S(1)} %eq.109), kind=kOutput, calls=%fused_computation.12 | convolution fusion | flops 49155072 | bytes 2654208 | tf_op jit(solution)/shard_map/dot_general | solution.py:278
  (71 shorter events, 6.9 us)
Async XLA Ops:
  6.5 206.6 %copy-start = (f32[50,1280]{1,0:T(8,128)S(1)}, f32[50,1280]{1,0:T(8,128)}, u32[]{:S(2)}) copy-start(f32[50,1280]{1,0:T(8,128)} %param.19) | copy-start | bytes 768004
  6.5 1.6 copy-start.2
  6.5 11.6 %copy-start.4 = (f32[640]{0:T(1024)S(1)}, f32[640]{0:T(1024)}, u32[]{:S(2)}) copy-start(f32[640]{0:T(1024)} %param.14) | copy-start | bytes 7684
  6.5 262.8 %reduce-scatter.2.cloned.1.call-start = ((), (), s32[]{:S(2)}) async-start(), calls=%async_computation.2 | async-start | bytes 6553600 | tf_op jit(solution)/shard_map/reduce_scatter | solution.py:270
  8.4 10.3 %copy-start.5 = (f32[640]{0:T(1024)S(1)}, f32[640]{0:T(1024)}, u32[]{:S(2)}) copy-start(f32[640]{0:T(1024)} %param.13) | copy-start | bytes 7684
  18.9 2.0 copy-start.6
  18.9 2.0 copy-start.7
  95.9 25.5 %collective-permute-start = (bf16[2,4,512,128]{3,2,1,0:T(8,128)(2,1)}, bf16[2,4,512,128]{3,2,1,0:T(8,128)(2,1)S(1)}, u32[]{:S(2)}, u32[]{:S(2)}) collective-permute-start(bf16[2,4,512,128]{3,2,1,0:T(8,128)(2,1)} %get-tuple-element.19), channel_id=1, source_target_pairs={{0,4},{4,8},{8,12},{12,16},{16,20},{20,24},{24,28},{28,32},{32,36}... | collective-permute-start | bytes 3145736 | tf_op jit(solution)/shard_map/ppermute | solution.py:207
  99.6 25.7 %collective-permute-start.1 = (bf16[2,4,512,128]{3,2,1,0:T(8,128)(2,1)}, bf16[2,4,512,128]{3,2,1,0:T(8,128)(2,1)}, u32[]{:S(2)}, u32[]{:S(2)}) collective-permute-start(bf16[2,4,512,128]{3,2,1,0:T(8,128)(2,1)} %get-tuple-element.20), channel_id=1, source_target_pairs={{4,0},{8,4},{12,8},{16,12},{20,16},{24,20},{28,24},{32,28},{36,32}... | collective-permute-start | bytes 3145736 | tf_op jit(solution)/shard_map/ppermute | solution.py:210
  103.4 2.3 copy-start.3
  116.1 9.2 %copy-start.1 = (bf16[2,5,512,128]{3,2,1,0:T(8,128)(2,1)S(1)}, bf16[2,5,512,128]{3,2,1,0:T(8,128)(2,1)}, u32[]{:S(2)}) copy-start(bf16[2,5,512,128]{3,2,1,0:T(8,128)(2,1)} %slice.60) | copy-start | bytes 3932164
  212.4 0.7 copy-start.8
Sparse Core Ops, SparseCore 0:
  212.6 56.7 reduce-scatter.1

commit v9 on v8

--- a/solution.py
+++ b/solution.py
@@ -81,8 +81,9 @@
     )(need, qp, kt, kp, q_tiles, k_tiles, v_tiles, seg_rows, seg_cols)
 
 
-def relay_kernel(src_ref, mark_ref, dst_ref, marks_ref, send_sem, recv_sem, mark_send, mark_recv, self_sem,
-                 *, slots, size, inverse):
+def relay_kernel(src_ref, mark_ref, dst_ref, marks_ref, left_ref, right_ref,
+                 send_sem, recv_sem, mark_send, mark_recv, self_sem, halo_send, halo_recv,
+                 *, slots, size, inverse, reach):
     me = lax.axis_index("ctx")
     barrier = pltpu.get_barrier_semaphore()
     for step in range(1, size):
@@ -136,24 +137,66 @@
         sent.wait_recv()
     mine.wait()
 
+    ahead = []
+    for i in range(reach):
+        to_next = pltpu.make_async_remote_copy(
+            dst_ref.at[slots - reach + i, pl.ds(1, 2)], left_ref.at[i], halo_send.at[i], halo_recv.at[i],
+            device_id={"ctx": jnp.minimum(me + 1, size - 1)}, device_id_type=pl.DeviceIdType.MESH,
+        )
+        to_prev = pltpu.make_async_remote_copy(
+            dst_ref.at[i, pl.ds(1, 2)], right_ref.at[i], halo_send.at[reach + i], halo_recv.at[reach + i],
+            device_id={"ctx": jnp.maximum(me - 1, 0)}, device_id_type=pl.DeviceIdType.MESH,
+        )
+
+        @pl.when(me < size - 1)
+        def _():
+            to_next.start()
+
+        @pl.when(me > 0)
+        def _():
+            to_prev.start()
+
+        ahead.append((to_next, to_prev))
+    for to_next, to_prev in ahead:
+        @pl.when(me < size - 1)
+        def _():
+            to_next.wait_send()
+
+        @pl.when(me > 0)
+        def _():
+            to_next.wait_recv()
+
+        @pl.when(me > 0)
+        def _():
+            to_prev.wait_send()
+
+        @pl.when(me < size - 1)
+        def _():
+            to_prev.wait_recv()
+
 
 def relay(tiles, marks, slots, size):
     inverse = pow(slots, -1, size)
-    kern = functools.partial(relay_kernel, slots=slots, size=size, inverse=inverse)
+    kern = functools.partial(relay_kernel, slots=slots, size=size, inverse=inverse, reach=REACH)
+    halo_shape = jax.ShapeDtypeStruct((REACH, 2) + tiles.shape[2:], tiles.dtype)
     return pl.pallas_call(
         kern,
         out_shape=(
             jax.ShapeDtypeStruct((slots,) + tiles.shape[1:], tiles.dtype),
             jax.ShapeDtypeStruct((size,) + marks.shape, marks.dtype),
+            halo_shape,
+            halo_shape,
         ),
         in_specs=[pl.BlockSpec(memory_space=pl.ANY), pl.BlockSpec(memory_space=pl.ANY)],
-        out_specs=(pl.BlockSpec(memory_space=pl.ANY), pl.BlockSpec(memory_space=pl.ANY)),
+        out_specs=tuple(pl.BlockSpec(memory_space=pl.ANY) for _ in range(4)),
         scratch_shapes=[
             pltpu.SemaphoreType.DMA((slots,)),
             pltpu.SemaphoreType.DMA((slots,)),
             pltpu.SemaphoreType.DMA((size - 1,)),
             pltpu.SemaphoreType.DMA((size - 1,)),
             pltpu.SemaphoreType.DMA((1,)),
+            pltpu.SemaphoreType.DMA((2 * REACH,)),
+            pltpu.SemaphoreType.DMA((2 * REACH,)),
         ],
         compiler_params=pltpu.CompilerParams(collective_id=0, has_side_effects=True),
     )(tiles, marks)
@@ -196,7 +239,7 @@
     qkv = jnp.stack([queries, normed_keys, value_rows]).reshape(3, row_count, head_count, HD)
     qkv = jnp.transpose(qkv, (0, 2, 1, 3))
 
-    came, marks = relay(
+    came, marks, left_got, right_got = relay(
         jnp.transpose(qkv, (1, 0, 2, 3)), jnp.stack([segment, destination]), slots, ctx_size
     )
     seg_blocks = marks[:, 0]
@@ -204,12 +247,8 @@
     own = jnp.transpose(came, (1, 0, 2, 3))
 
     kv_own = own[1:]
-    left = lax.ppermute(
-        kv_own[:, slots - REACH:], "ctx", [(e, e + 1) for e in range(ctx_size - 1)]
-    )
-    right = lax.ppermute(
-        kv_own[:, :REACH], "ctx", [(e, e - 1) for e in range(1, ctx_size)]
-    )
+    left = jnp.transpose(left_got, (1, 0, 2, 3))
+    right = jnp.transpose(right_got, (1, 0, 2, 3))
     kv_all = jnp.concatenate([left, kv_own, right], axis=1)
 
     seg_lo = seg_blocks[:, 0]

time: 280 us -> 287 us (1.025)
  Pallas kernels: 114 us -> 134 us
  waiting for transfers between devices: 64.2 us -> 49.8 us
  blocking collectives: 37.1 us -> 47.1 us
  starting transfers between devices: 5.01 us -> 0.01 us
    pallas_call x1, Pallas kernels: 69.5 us -> 94.3 us  [relay(): pl.pallas_call(kern, out_shape=(jax.ShapeDtypeStruct((slots,) + tiles.sha...]
    all_to_all x1, blocking collectives: 27.5 us -> 37.6 us  [local(): got = lax.all_to_all(placed, 'ctx', split_axis=0, concat_axis=0, tiled=True)]
    ppermute x2 -> x0, waiting for transfers between devices: 8.26 us -> none  [the longest x1 4.39 us: local(): lax.ppermute(kv_own[:, slots - REACH:], 'ctx', [(e, e + 1) for e in range...]
    reduce_scatter x1, waiting for transfers between devices: 56 us -> 49.8 us  [local(): lax.psum_scatter(head_terms.astype(jnp.bfloat16), 'head', scatter_dimensi...]
    ppermute x2 -> x0, starting transfers between devices: 5.01 us -> none  [the longest x1 3.72 us: local(): lax.ppermute(kv_own[:, slots - REACH:], 'ctx', [(e, e + 1) for e in range...]
    pallas_call x1, Pallas kernels: 44.7 us -> 40 us  [flash(): pl.pallas_call(kern, grid_spec=grid_spec, out_shape=jax.ShapeDtypeStruct(...]
  transfers between devices with their start and end apart: 3 -> 1, of which waited for: 3 -> 1; matrix products, arithmetic and copies ran while one was open for 6% -> 0% of each run, Pallas kernels for 0% -> 0%
where the time goes in v9:
time: 287 us
  Pallas kernels  134 us (47%)
  waiting for transfers between devices  49.8 us (17%)
  blocking collectives  47.1 us (16%)
  local copies, waits for them, and re-layouts  20.2 us (7%)
  matrix products  14.8 us (5%)
  between operations  13.7 us (5%)
  other arithmetic  6.89 us (2%)
    pallas_call x1, Pallas kernels, relay(): pl.pallas_call(kern, out_shape=(jax.ShapeDtypeStruct((slots,) + tiles.sha...  94.3 us
    reduce_scatter x1, waiting for transfers between devices, local(): lax.psum_scatter(head_terms.astype(jnp.bfloat16), 'head', scatter_dimensi...  49.8 us
    pallas_call x1, Pallas kernels, flash(): pl.pallas_call(kern, grid_spec=grid_spec, out_shape=jax.ShapeDtypeStruct(...  40 us
    all_to_all x1, blocking collectives, local(): got = lax.all_to_all(placed, 'ctx', split_axis=0, concat_axis=0, tiled=True)  37.6 us
    psum x1, blocking collectives, local(): lax.psum((jnp.sum(query_float * query_float, axis=1), jnp.sum(key_float *...  9.55 us
    dot_general x1, matrix products, local(): jnp.dot(owned_attended, out_weight, preferred_element_type=jnp.float32)  8.85 us
  transfers between devices with their start and end apart: 1, of which 1 were waited for; matrix products, arithmetic and copies ran while one was open for 0% of the time, Pallas kernels for 0%

profile of v9, /device:TPU:1, one launch (start us, length us, event | category | flops | bytes accessed | tf_op | source)
XLA Modules:
  0.0 286.8 jit_solution(11819700264797027099)
XLA Ops:
  6.6 0.6 and_select_fusion.1
  8.1 1.3 copy.41
  10.1 9.6 %all-reduce = (f32[512]{0:T(512)S(1)}, f32[512]{0:T(512)S(1)}) all-reduce(f32[512]{0:T(512)S(1)} %fusion.7, f32[512]{0:T(512)S(1)} %fusion.4), channel_id=1, replica_groups=mesh['batch'=4,'ctx'=16,'head'=4] {'head'}, use_global_device_ids=true, to_apply=%region_3.0 | all-reduce | flops 1024 | bytes 8192 | tf_op jit(solution)/shard_map/psum | solution.py:229
  20.7 1.3 copy.43
  22.4 0.6 pad_add_fusion.mark_ref
  23.0 1.5 maximum_bitcast_fusion.src_ref
  24.5 94.3 %shard_map.100 = (bf16[5,3,512,128]{3,2,1,0:T(8,128)(2,1)}, s32[16,2,512]{2,1,0:T(2,128)}, bf16[4,2,512,128]{3,2,1,0:T(8,128)(2,1)}, bf16[4,2,512,128]{3,2,1,0:T(8,128)(2,1)}) custom-call(bf16[5,3,512,128]{3,2,1,0:T(8,128)(2,1)} %maximum_bitcast_fusion.src_ref, s32[2,512]{1,0:T(2,128)} %pad_add_fusion.mark_ref), custom_call_target="tpu_custom_call" | custom-call | tf_op jit(solution)/shard_map/pallas_call | solution.py:182
  118.8 1.0 fusion.31
  120.0 0.7 gather_fusion.4
  120.7 0.6 gather_fusion.1
  121.3 0.8 gather_fusion.3
  122.1 0.8 gather_fusion.2
  123.3 0.3 copy-done.1
  123.8 0.9 slice_bitcast_fusion.2.q_ref
  124.9 0.6 gather_fusion
  125.5 0.5 fusion.30
  126.0 0.7 iota_reduce_fusion
  126.8 0.7 fusion.15
  127.6 1.3 gather_fusion.6
  128.9 1.3 gather_fusion.5
  130.2 1.3 copy.75
  131.5 0.4 pad_maximum_fusion
  132.0 2.0 slice_bitcast_fusion
  134.0 2.6 copy.57.qs_ref
  136.6 40.0 %shard_map.101 = bf16[5,512,128]{2,1,0:T(8,128)(2,1)} custom-call(s32[45]{0:T(128)} %get-tuple-element.19.need_ref, s32[5]{0:T(128)} %get-tuple-element.30.qp_ref, s32[45]{0:T(128)} %gather_fusion.5, s32[45]{0:T(128)} %gather_fusion.6, bf16[5,512,128]{2,1,0:T(8,128)(2,1)} %slice_bitcast_fusion.2.q_ref, bf16[13,512,128]{2,1,0:T(8,128)(2,1)} %get-tuple-element.22.k_ref, ...), custom_call_target="tpu_custom_call" | custom-call | tf_op jit(solution)/shard_map/pallas_call | solution.py:74
  176.6 2.0 fusion.3
  178.7 37.6 %all_to_all.5 = bf16[16,5,32,128]{3,2,1,0:T(8,128)(2,1)S(1)} all-to-all(bf16[16,5,32,128]{3,2,1,0:T(8,128)(2,1)S(1)} %bitcast.58), channel_id=1, replica_groups=mesh['batch'=4,'ctx'=16,'head'=4] {'ctx'}, dimensions={0} | all-to-all | bytes 1310720 | tf_op jit(solution)/shard_map/all_to_all | solution.py:295
  216.3 0.5 copy.59
  216.7 8.9 %convolution_convert_fusion = bf16[512,5120]{1,0:T(8,128)(2,1)} fusion(bf16[640,5120]{1,0:T(8,128)(2,1)} %param.18, bf16[64,8,5,128]{3,2,1,0:T(8,128)(2,1)S(1)} %bitcast.63), kind=kOutput, calls=%fused_computation.7 | convolution fusion | flops 3358064640 | bytes 12451840 | tf_op jit(solution)/shard_map/dot_general | solution.py:308
  225.7 0.5 select_reduce_fusion
  226.5 49.8 %reduce-scatter.2.cloned.1.call-done = bf16[512,1280]{1,0:T(8,128)(2,1)} async-done(((bf16[512,5120]{1,0:T(8,128)(2,1)}), bf16[512,1280]{1,0:T(8,128)(2,1)}) %reduce-scatter.2.cloned.1.call-update) | async-done | bytes 1310736 | tf_op jit(solution)/shard_map/reduce_scatter | solution.py:309
  276.3 3.6 %fusion.1 = bf16[512,1280]{1,0:T(8,128)(2,1)} fusion(f32[6,1280]{1,0:T(8,128)S(1)} %fusion.23, bf16[512,1280]{1,0:T(8,128)(2,1)} %reduce-scatter.2.cloned.1.call-done, s32[512]{0:T(512)S(1)} %eq.109), kind=kOutput, calls=%fused_computation.12 | convolution fusion | flops 49155072 | bytes 2654208 | tf_op jit(solution)/shard_map/dot_general | solution.py:317
  (70 shorter events, 4.5 us)
Async XLA Ops:
  6.5 219.8 %copy-start = (f32[50,1280]{1,0:T(8,128)S(1)}, f32[50,1280]{1,0:T(8,128)}, u32[]{:S(2)}) copy-start(f32[50,1280]{1,0:T(8,128)} %param.19) | copy-start | bytes 768004
  6.5 3.1 %copy-start.3 = (bf16[512,640]{1,0:T(8,128)(2,1)S(1)}, bf16[512,640]{1,0:T(8,128)(2,1)}, u32[]{:S(2)}) copy-start(bf16[512,640]{1,0:T(8,128)(2,1)} %param.11) | copy-start | bytes 1966084
  6.5 269.8 %reduce-scatter.2.cloned.1.call-start = ((), (), s32[]{:S(2)}) async-start(), calls=%async_computation.2 | async-start | bytes 6553600 | tf_op jit(solution)/shard_map/reduce_scatter | solution.py:309
  8.1 11.6 %copy-start.5 = (f32[640]{0:T(1024)S(1)}, f32[640]{0:T(1024)}, u32[]{:S(2)}) copy-start(f32[640]{0:T(1024)} %param.14) | copy-start | bytes 7684
  9.9 10.3 %copy-start.6 = (f32[640]{0:T(1024)S(1)}, f32[640]{0:T(1024)}, u32[]{:S(2)}) copy-start(f32[640]{0:T(1024)} %param.13) | copy-start | bytes 7684
  20.4 2.0 copy-start.7
  20.4 2.0 copy-start.8
  119.8 2.3 copy-start.4
  122.1 1.5 copy-start.1
  124.8 6.7 %copy-start.2 = (bf16[4,2,512,128]{3,2,1,0:T(8,128)(2,1)S(1)}, bf16[4,2,512,128]{3,2,1,0:T(8,128)(2,1)}, u32[]{:S(2)}) copy-start(bf16[4,2,512,128]{3,2,1,0:T(8,128)(2,1)} %get-tuple-element.14) | copy-start | bytes 3145732
  225.6 0.7 copy-start.9
Sparse Core Ops, SparseCore 0:
  225.7 50.5 reduce-scatter.1

commit v10 on v8

--- a/solution.py
+++ b/solution.py
@@ -26,24 +26,34 @@
         l_scr[...] = jnp.zeros_like(l_scr)
         acc_scr[...] = jnp.zeros_like(acc_scr)
 
-    @pl.when(need_ref[j * offsets + o] != 0)
-    def _():
+    def step(masked):
         q = q_ref[0]
         k = k_ref[0]
         s = lax.dot_general(
             q, k, (((1,), (1,)), ((), ())), preferred_element_type=jnp.float32
         ) * score_scale
-        mask = qs_ref[0] == ks_ref[0]
-        s = jnp.where(mask, s, -1e30)
+        if masked:
+            mask = qs_ref[0] == ks_ref[0]
+            s = jnp.where(mask, s, -1e30)
         m_prev = m_scr[...]
         m_new = jnp.maximum(m_prev, jnp.max(s, axis=1, keepdims=True))
         alpha = jnp.exp(m_prev - m_new)
-        p = jnp.where(mask, jnp.exp(s - m_new), 0.0)
+        p = jnp.exp(s - m_new)
+        if masked:
+            p = jnp.where(mask, p, 0.0)
         l_scr[...] = alpha * l_scr[...] + jnp.sum(p, axis=1, keepdims=True)
         acc_scr[...] = alpha * acc_scr[...] + jnp.dot(
             p.astype(jnp.bfloat16), v_ref[0], preferred_element_type=jnp.float32
         )
         m_scr[...] = m_new
+
+    @pl.when(need_ref[j * offsets + o] == 1)
+    def _():
+        step(True)
+
+    @pl.when(need_ref[j * offsets + o] == 2)
+    def _():
+        step(False)
 
     @pl.when(o == offsets - 1)
     def _():
@@ -227,7 +237,10 @@
     same_head = (t_kc // ctx_size) == (t_q // ctx_size)
     meet = (seg_lo[p_q] <= seg_hi[p_k]) & (seg_lo[p_k] <= seg_hi[p_q])
     need_b = (valid & same_head & meet).reshape(-1)
-    need = need_b.astype(jnp.int32)
+    whole = (
+        (seg_lo[p_q] == seg_hi[p_q]) & (seg_lo[p_k] == seg_hi[p_k]) & (seg_lo[p_q] == seg_lo[p_k])
+    ).reshape(-1)
+    need = need_b.astype(jnp.int32) * (1 + whole.astype(jnp.int32))
     steps = jnp.arange(need.shape[0], dtype=jnp.int32)
     latest = lax.cummax(jnp.where(need_b, steps, -1), axis=0)
     source = jnp.where(latest < 0, jnp.argmax(need_b).astype(jnp.int32), latest)

time: 280 us -> 280 us (level)
  blocking collectives: 37.1 us -> 43.1 us
  waiting for transfers between devices: 64.2 us -> 59 us
    all_to_all x1, blocking collectives: 27.5 us -> 33.5 us  [local(): got = lax.all_to_all(placed, 'ctx', split_axis=0, concat_axis=0, tiled=True)]
    reduce_scatter x1, waiting for transfers between devices: 56 us -> 50.8 us  [local(): lax.psum_scatter(head_terms.astype(jnp.bfloat16), 'head', scatter_dimensi...]
where the time goes in v10:
time: 280 us; the launch traced here: 279 us
  Pallas kernels  113 us (40%)
  waiting for transfers between devices  59 us (21%)
  blocking collectives  43.1 us (15%)
  local copies, waits for them, and re-layouts  22.9 us (8%)
  matrix products  14.8 us (5%)
  between operations  13.7 us (5%)
  other arithmetic  7.99 us (3%)
  starting transfers between devices  5.01 us (2%)
    pallas_call x1, Pallas kernels, relay(): pl.pallas_call(kern, out_shape=(jax.ShapeDtypeStruct((slots,) + tiles.sha...  69.5 us
    reduce_scatter x1, waiting for transfers between devices, local(): lax.psum_scatter(head_terms.astype(jnp.bfloat16), 'head', scatter_dimensi...  50.8 us
    pallas_call x1, Pallas kernels, flash(): pl.pallas_call(kern, grid_spec=grid_spec, out_shape=jax.ShapeDtypeStruct(...  43.4 us
    all_to_all x1, blocking collectives, local(): got = lax.all_to_all(placed, 'ctx', split_axis=0, concat_axis=0, tiled=True)  33.5 us
    psum x1, blocking collectives, local(): lax.psum((jnp.sum(query_float * query_float, axis=1), jnp.sum(key_float *...  9.55 us
    dot_general x1, matrix products, local(): jnp.dot(owned_attended, out_weight, preferred_element_type=jnp.float32)  8.85 us
  transfers between devices with their start and end apart: 3, of which 3 were waited for; matrix products, arithmetic and copies ran while one was open for 6% of the time, Pallas kernels for 0%

profile of v10, /device:TPU:1, one launch (start us, length us, event | category | flops | bytes accessed | tf_op | source)
XLA Modules:
  0.0 279.4 jit_solution(9130429450788190790)
XLA Ops:
  6.5 1.4 copy.37
  8.6 9.6 %all-reduce = (f32[512]{0:T(512)S(1)}, f32[512]{0:T(512)S(1)}) all-reduce(f32[512]{0:T(512)S(1)} %fusion.7, f32[512]{0:T(512)S(1)} %fusion.4), channel_id=1, replica_groups=mesh['batch'=4,'ctx'=16,'head'=4] {'head'}, use_global_device_ids=true, to_apply=%region_3.0 | all-reduce | flops 1024 | bytes 8192 | tf_op jit(solution)/shard_map/psum | solution.py:196
  19.3 1.3 copy.39
  20.9 0.6 pad_add_fusion.mark_ref
  21.6 1.5 maximum_bitcast_fusion.src_ref
  23.0 69.5 %shard_map.100 = (bf16[5,3,512,128]{3,2,1,0:T(8,128)(2,1)}, s32[16,2,512]{2,1,0:T(2,128)}) custom-call(bf16[5,3,512,128]{3,2,1,0:T(8,128)(2,1)} %maximum_bitcast_fusion.src_ref, s32[2,512]{1,0:T(2,128)} %pad_add_fusion.mark_ref), custom_call_target="tpu_custom_call" | custom-call | tf_op jit(solution)/shard_map/pallas_call | solution.py:153
  92.5 1.7 copy.65
  94.2 1.7 fusion.30
  95.9 3.7 %collective-permute-start = (bf16[2,4,512,128]{3,2,1,0:T(8,128)(2,1)}, bf16[2,4,512,128]{3,2,1,0:T(8,128)(2,1)S(1)}, u32[]{:S(2)}, u32[]{:S(2)}) collective-permute-start(bf16[2,4,512,128]{3,2,1,0:T(8,128)(2,1)} %get-tuple-element.19), channel_id=1, source_target_pairs={{0,4},{4,8},{8,12},{12,16},{16,20},{20,24},{24,28},{28,32},{32,36}... | collective-permute-start | bytes 3145736 | tf_op jit(solution)/shard_map/ppermute | solution.py:217
  99.6 1.3 collective-permute-start.1
  102.4 1.0 fusion.31
  103.6 0.7 gather_fusion.1
  104.3 0.6 gather_fusion.4
  104.9 0.8 gather_fusion.2
  105.7 0.8 gather_fusion.3
  106.9 1.1 slice.60
  108.9 0.7 iota_reduce_fusion
  109.7 0.7 fusion.15
  110.4 1.3 gather_fusion.6
  111.7 1.3 gather_fusion.5
  113.0 2.6 copy.51.qs_ref
  116.2 0.9 slice_bitcast_fusion.2.q_ref
  117.1 4.4 %collective-permute-done = bf16[2,4,512,128]{3,2,1,0:T(8,128)(2,1)S(1)} collective-permute-done((bf16[2,4,512,128]{3,2,1,0:T(8,128)(2,1)}, bf16[2,4,512,128]{3,2,1,0:T(8,128)(2,1)S(1)}, u32[]{:S(2)}, u32[]{:S(2)}) %collective-permute-start) | collective-permute-done | bytes 1048608 | tf_op jit(solution)/shard_map/ppermute | solution.py:217
  121.4 3.9 %collective-permute-done.1 = bf16[2,4,512,128]{3,2,1,0:T(8,128)(2,1)} collective-permute-done((bf16[2,4,512,128]{3,2,1,0:T(8,128)(2,1)}, bf16[2,4,512,128]{3,2,1,0:T(8,128)(2,1)}, u32[]{:S(2)}, u32[]{:S(2)}) %collective-permute-start.1) | collective-permute-done | bytes 1048608 | tf_op jit(solution)/shard_map/ppermute | solution.py:220
  125.3 1.5 pad_maximum_fusion
  126.8 2.0 slice_bitcast_fusion
  128.8 43.4 %shard_map.101 = bf16[5,512,128]{2,1,0:T(8,128)(2,1)} custom-call(s32[45]{0:T(128)} %get-tuple-element.15.need_ref, s32[5]{0:T(128)} %get-tuple-element.29.qp_ref, s32[45]{0:T(128)} %gather_fusion.5, s32[45]{0:T(128)} %gather_fusion.6, bf16[5,512,128]{2,1,0:T(8,128)(2,1)} %slice_bitcast_fusion.2.q_ref, bf16[13,512,128]{2,1,0:T(8,128)(2,1)} %get-tuple-element.18.k_ref, ...), custom_call_target="tpu_custom_call" | custom-call | tf_op jit(solution)/shard_map/pallas_call | solution.py:84
  172.2 2.0 fusion.3
  174.3 33.5 %all_to_all.5 = bf16[16,5,32,128]{3,2,1,0:T(8,128)(2,1)S(1)} all-to-all(bf16[16,5,32,128]{3,2,1,0:T(8,128)(2,1)S(1)} %bitcast.51), channel_id=1, replica_groups=mesh['batch'=4,'ctx'=16,'head'=4] {'ctx'}, dimensions={0} | all-to-all | bytes 1310720 | tf_op jit(solution)/shard_map/all_to_all | solution.py:269
  208.3 8.9 %convolution_convert_fusion = bf16[512,5120]{1,0:T(8,128)(2,1)} fusion(bf16[640,5120]{1,0:T(8,128)(2,1)} %param.18, bf16[64,8,5,128]{3,2,1,0:T(8,128)(2,1)S(1)} %bitcast.56), kind=kOutput, calls=%fused_computation.7 | convolution fusion | flops 3358064640 | bytes 12451840 | tf_op jit(solution)/shard_map/dot_general | solution.py:282
  218.1 50.8 %reduce-scatter.2.cloned.1.call-done = bf16[512,1280]{1,0:T(8,128)(2,1)} async-done(((bf16[512,5120]{1,0:T(8,128)(2,1)}), bf16[512,1280]{1,0:T(8,128)(2,1)}) %reduce-scatter.2.cloned.1.call-update) | async-done | bytes 1310736 | tf_op jit(solution)/shard_map/reduce_scatter | solution.py:283
  268.9 3.6 %fusion.1 = bf16[512,1280]{1,0:T(8,128)(2,1)} fusion(f32[6,1280]{1,0:T(8,128)S(1)} %fusion.23, bf16[512,1280]{1,0:T(8,128)(2,1)} %reduce-scatter.2.cloned.1.call-done, s32[512]{0:T(512)S(1)} %eq.133), kind=kOutput, calls=%fused_computation.12 | convolution fusion | flops 49155072 | bytes 2654208 | tf_op jit(solution)/shard_map/dot_general | solution.py:291
  (73 shorter events, 7.0 us)
Async XLA Ops:
  6.5 211.4 %copy-start = (f32[50,1280]{1,0:T(8,128)S(1)}, f32[50,1280]{1,0:T(8,128)}, u32[]{:S(2)}) copy-start(f32[50,1280]{1,0:T(8,128)} %param.19) | copy-start | bytes 768004
  6.5 1.6 copy-start.2
  6.5 11.6 %copy-start.4 = (f32[640]{0:T(1024)S(1)}, f32[640]{0:T(1024)}, u32[]{:S(2)}) copy-start(f32[640]{0:T(1024)} %param.14) | copy-start | bytes 7684
  6.5 262.4 %reduce-scatter.2.cloned.1.call-start = ((), (), s32[]{:S(2)}) async-start(), calls=%async_computation.2 | async-start | bytes 6553600 | tf_op jit(solution)/shard_map/reduce_scatter | solution.py:283
  8.4 10.3 %copy-start.5 = (f32[640]{0:T(1024)S(1)}, f32[640]{0:T(1024)}, u32[]{:S(2)}) copy-start(f32[640]{0:T(1024)} %param.13) | copy-start | bytes 7684
  18.9 2.0 copy-start.6
  18.9 2.0 copy-start.7
  95.9 25.5 %collective-permute-start = (bf16[2,4,512,128]{3,2,1,0:T(8,128)(2,1)}, bf16[2,4,512,128]{3,2,1,0:T(8,128)(2,1)S(1)}, u32[]{:S(2)}, u32[]{:S(2)}) collective-permute-start(bf16[2,4,512,128]{3,2,1,0:T(8,128)(2,1)} %get-tuple-element.19), channel_id=1, source_target_pairs={{0,4},{4,8},{8,12},{12,16},{16,20},{20,24},{24,28},{28,32},{32,36}... | collective-permute-start | bytes 3145736 | tf_op jit(solution)/shard_map/ppermute | solution.py:217
  99.6 25.7 %collective-permute-start.1 = (bf16[2,4,512,128]{3,2,1,0:T(8,128)(2,1)}, bf16[2,4,512,128]{3,2,1,0:T(8,128)(2,1)}, u32[]{:S(2)}, u32[]{:S(2)}) collective-permute-start(bf16[2,4,512,128]{3,2,1,0:T(8,128)(2,1)} %get-tuple-element.20), channel_id=1, source_target_pairs={{4,0},{8,4},{12,8},{16,12},{20,16},{24,20},{28,24},{32,28},{36,32}... | collective-permute-start | bytes 3145736 | tf_op jit(solution)/shard_map/ppermute | solution.py:220
  103.4 2.3 copy-start.3
  116.1 9.2 %copy-start.1 = (bf16[2,5,512,128]{3,2,1,0:T(8,128)(2,1)S(1)}, bf16[2,5,512,128]{3,2,1,0:T(8,128)(2,1)}, u32[]{:S(2)}) copy-start(bf16[2,5,512,128]{3,2,1,0:T(8,128)(2,1)} %slice.60) | copy-start | bytes 3932164
  217.2 0.7 copy-start.8
Sparse Core Ops, SparseCore 0:
  217.3 51.5 reduce-scatter.1

commit v11 on v10

--- a/solution.py
+++ b/solution.py
@@ -38,7 +38,7 @@
         m_prev = m_scr[...]
         m_new = jnp.maximum(m_prev, jnp.max(s, axis=1, keepdims=True))
         alpha = jnp.exp(m_prev - m_new)
-        p = jnp.exp(s - m_new)
+        p = jnp.exp(s - m_new[:, :1])
         if masked:
             p = jnp.where(mask, p, 0.0)
         l_scr[...] = alpha * l_scr[...] + jnp.sum(p, axis=1, keepdims=True)
@@ -76,8 +76,8 @@
         ],
         out_specs=pl.BlockSpec((1, rows, width), lambda j, o, nd, qp, kt, kp: (j, 0, 0)),
         scratch_shapes=[
-            pltpu.VMEM((rows, 1), jnp.float32),
-            pltpu.VMEM((rows, 1), jnp.float32),
+            pltpu.VMEM((rows, width), jnp.float32),
+            pltpu.VMEM((rows, width), jnp.float32),
             pltpu.VMEM((rows, width), jnp.float32),
         ],
     )

time: 280 us -> 272 us (0.971)
  Pallas kernels: 113 us -> 106 us
  blocking collectives: 43.1 us -> 37.7 us
  waiting for transfers between devices: 59 us -> 63.3 us
    pallas_call x1, Pallas kernels: 43.4 us -> 36.5 us  [flash(): pl.pallas_call(kern, grid_spec=grid_spec, out_shape=jax.ShapeDtypeStruct(...]
    all_to_all x1, blocking collectives: 33.5 us -> 28.2 us  [local(): got = lax.all_to_all(placed, 'ctx', split_axis=0, concat_axis=0, tiled=True)]
    reduce_scatter x1, waiting for transfers between devices: 50.8 us -> 55 us  [local(): lax.psum_scatter(head_terms.astype(jnp.bfloat16), 'head', scatter_dimensi...]
where the time goes in v11:
time: 272 us; the launch traced here: 271 us
  Pallas kernels  106 us (39%)
  waiting for transfers between devices  63.3 us (23%)
  blocking collectives  37.7 us (14%)
  local copies, waits for them, and re-layouts  22.9 us (8%)
  matrix products  14.8 us (5%)
  between operations  13.7 us (5%)
  other arithmetic  7.99 us (3%)
  starting transfers between devices  5.01 us (2%)
    pallas_call x1, Pallas kernels, relay(): pl.pallas_call(kern, out_shape=(jax.ShapeDtypeStruct((slots,) + tiles.sha...  69.5 us
    reduce_scatter x1, waiting for transfers between devices, local(): lax.psum_scatter(head_terms.astype(jnp.bfloat16), 'head', scatter_dimensi...  55 us
    pallas_call x1, Pallas kernels, flash(): pl.pallas_call(kern, grid_spec=grid_spec, out_shape=jax.ShapeDtypeStruct(...  36.5 us
    all_to_all x1, blocking collectives, local(): got = lax.all_to_all(placed, 'ctx', split_axis=0, concat_axis=0, tiled=True)  28.2 us
    psum x1, blocking collectives, local(): lax.psum((jnp.sum(query_float * query_float, axis=1), jnp.sum(key_float *...  9.55 us
    dot_general x1, matrix products, local(): jnp.dot(owned_attended, out_weight, preferred_element_type=jnp.float32)  8.85 us
  transfers between devices with their start and end apart: 3, of which 3 were waited for; matrix products, arithmetic and copies ran while one was open for 6% of the time, Pallas kernels for 0%

profile of v11, /device:TPU:1, one launch (start us, length us, event | category | flops | bytes accessed | tf_op | source)
XLA Modules:
  0.0 271.4 jit_solution(16478577041306322229)
XLA Ops:
  6.5 1.4 copy.37
  8.6 9.6 %all-reduce = (f32[512]{0:T(512)S(1)}, f32[512]{0:T(512)S(1)}) all-reduce(f32[512]{0:T(512)S(1)} %fusion.7, f32[512]{0:T(512)S(1)} %fusion.4), channel_id=1, replica_groups=mesh['batch'=4,'ctx'=16,'head'=4] {'head'}, use_global_device_ids=true, to_apply=%region_3.0 | all-reduce | flops 1024 | bytes 8192 | tf_op jit(solution)/shard_map/psum | solution.py:196
  19.3 1.3 copy.39
  20.9 0.6 pad_add_fusion.mark_ref
  21.6 1.5 maximum_bitcast_fusion.src_ref
  23.0 69.5 %shard_map.100 = (bf16[5,3,512,128]{3,2,1,0:T(8,128)(2,1)}, s32[16,2,512]{2,1,0:T(2,128)}) custom-call(bf16[5,3,512,128]{3,2,1,0:T(8,128)(2,1)} %maximum_bitcast_fusion.src_ref, s32[2,512]{1,0:T(2,128)} %pad_add_fusion.mark_ref), custom_call_target="tpu_custom_call" | custom-call | tf_op jit(solution)/shard_map/pallas_call | solution.py:153
  92.5 1.7 copy.65
  94.2 1.7 fusion.30
  95.9 3.7 %collective-permute-start = (bf16[2,4,512,128]{3,2,1,0:T(8,128)(2,1)}, bf16[2,4,512,128]{3,2,1,0:T(8,128)(2,1)S(1)}, u32[]{:S(2)}, u32[]{:S(2)}) collective-permute-start(bf16[2,4,512,128]{3,2,1,0:T(8,128)(2,1)} %get-tuple-element.19), channel_id=1, source_target_pairs={{0,4},{4,8},{8,12},{12,16},{16,20},{20,24},{24,28},{28,32},{32,36}... | collective-permute-start | bytes 3145736 | tf_op jit(solution)/shard_map/ppermute | solution.py:217
  99.6 1.3 collective-permute-start.1
  102.4 1.0 fusion.31
  103.6 0.7 gather_fusion.1
  104.3 0.6 gather_fusion.4
  104.9 0.8 gather_fusion.2
  105.7 0.8 gather_fusion.3
  106.9 1.1 slice.60
  108.9 0.7 iota_reduce_fusion
  109.7 0.7 fusion.15
  110.4 1.3 gather_fusion.6
  111.7 1.3 gather_fusion.5
  113.0 2.6 copy.51.qs_ref
  116.2 0.9 slice_bitcast_fusion.2.q_ref
  117.1 4.4 %collective-permute-done = bf16[2,4,512,128]{3,2,1,0:T(8,128)(2,1)S(1)} collective-permute-done((bf16[2,4,512,128]{3,2,1,0:T(8,128)(2,1)}, bf16[2,4,512,128]{3,2,1,0:T(8,128)(2,1)S(1)}, u32[]{:S(2)}, u32[]{:S(2)}) %collective-permute-start) | collective-permute-done | bytes 1048608 | tf_op jit(solution)/shard_map/ppermute | solution.py:217
  121.4 3.9 %collective-permute-done.1 = bf16[2,4,512,128]{3,2,1,0:T(8,128)(2,1)} collective-permute-done((bf16[2,4,512,128]{3,2,1,0:T(8,128)(2,1)}, bf16[2,4,512,128]{3,2,1,0:T(8,128)(2,1)}, u32[]{:S(2)}, u32[]{:S(2)}) %collective-permute-start.1) | collective-permute-done | bytes 1048608 | tf_op jit(solution)/shard_map/ppermute | solution.py:220
  125.3 1.5 pad_maximum_fusion
  126.8 2.0 slice_bitcast_fusion
  128.8 36.5 %shard_map.101 = bf16[5,512,128]{2,1,0:T(8,128)(2,1)} custom-call(s32[45]{0:T(128)} %get-tuple-element.15.need_ref, s32[5]{0:T(128)} %get-tuple-element.29.qp_ref, s32[45]{0:T(128)} %gather_fusion.5, s32[45]{0:T(128)} %gather_fusion.6, bf16[5,512,128]{2,1,0:T(8,128)(2,1)} %slice_bitcast_fusion.2.q_ref, bf16[13,512,128]{2,1,0:T(8,128)(2,1)} %get-tuple-element.18.k_ref, ...), custom_call_target="tpu_custom_call" | custom-call | tf_op jit(solution)/shard_map/pallas_call | solution.py:84
  165.3 2.0 fusion.3
  167.4 28.2 %all_to_all.5 = bf16[16,5,32,128]{3,2,1,0:T(8,128)(2,1)S(1)} all-to-all(bf16[16,5,32,128]{3,2,1,0:T(8,128)(2,1)S(1)} %bitcast.51), channel_id=1, replica_groups=mesh['batch'=4,'ctx'=16,'head'=4] {'ctx'}, dimensions={0} | all-to-all | bytes 1310720 | tf_op jit(solution)/shard_map/all_to_all | solution.py:269
  196.1 8.9 %convolution_convert_fusion = bf16[512,5120]{1,0:T(8,128)(2,1)} fusion(bf16[640,5120]{1,0:T(8,128)(2,1)} %param.18, bf16[64,8,5,128]{3,2,1,0:T(8,128)(2,1)S(1)} %bitcast.56), kind=kOutput, calls=%fused_computation.7 | convolution fusion | flops 3358064640 | bytes 12451840 | tf_op jit(solution)/shard_map/dot_general | solution.py:282
  205.9 55.0 %reduce-scatter.2.cloned.1.call-done = bf16[512,1280]{1,0:T(8,128)(2,1)} async-done(((bf16[512,5120]{1,0:T(8,128)(2,1)}), bf16[512,1280]{1,0:T(8,128)(2,1)}) %reduce-scatter.2.cloned.1.call-update) | async-done | bytes 1310736 | tf_op jit(solution)/shard_map/reduce_scatter | solution.py:283
  260.9 3.6 %fusion.1 = bf16[512,1280]{1,0:T(8,128)(2,1)} fusion(f32[6,1280]{1,0:T(8,128)S(1)} %fusion.23, bf16[512,1280]{1,0:T(8,128)(2,1)} %reduce-scatter.2.cloned.1.call-done, s32[512]{0:T(512)S(1)} %eq.133), kind=kOutput, calls=%fused_computation.12 | convolution fusion | flops 49155072 | bytes 2654208 | tf_op jit(solution)/shard_map/dot_general | solution.py:291
  (73 shorter events, 7.0 us)
Async XLA Ops:
  6.5 199.1 %copy-start = (f32[50,1280]{1,0:T(8,128)S(1)}, f32[50,1280]{1,0:T(8,128)}, u32[]{:S(2)}) copy-start(f32[50,1280]{1,0:T(8,128)} %param.19) | copy-start | bytes 768004
  6.5 1.6 copy-start.2
  6.5 11.6 %copy-start.4 = (f32[640]{0:T(1024)S(1)}, f32[640]{0:T(1024)}, u32[]{:S(2)}) copy-start(f32[640]{0:T(1024)} %param.14) | copy-start | bytes 7684
  6.5 254.4 %reduce-scatter.2.cloned.1.call-start = ((), (), s32[]{:S(2)}) async-start(), calls=%async_computation.2 | async-start | bytes 6553600 | tf_op jit(solution)/shard_map/reduce_scatter | solution.py:283
  8.4 10.3 %copy-start.5 = (f32[640]{0:T(1024)S(1)}, f32[640]{0:T(1024)}, u32[]{:S(2)}) copy-start(f32[640]{0:T(1024)} %param.13) | copy-start | bytes 7684
  18.9 2.0 copy-start.6
  18.9 2.0 copy-start.7
  95.9 25.5 %collective-permute-start = (bf16[2,4,512,128]{3,2,1,0:T(8,128)(2,1)}, bf16[2,4,512,128]{3,2,1,0:T(8,128)(2,1)S(1)}, u32[]{:S(2)}, u32[]{:S(2)}) collective-permute-start(bf16[2,4,512,128]{3,2,1,0:T(8,128)(2,1)} %get-tuple-element.19), channel_id=1, source_target_pairs={{0,4},{4,8},{8,12},{12,16},{16,20},{20,24},{24,28},{28,32},{32,36}... | collective-permute-start | bytes 3145736 | tf_op jit(solution)/shard_map/ppermute | solution.py:217
  99.6 25.7 %collective-permute-start.1 = (bf16[2,4,512,128]{3,2,1,0:T(8,128)(2,1)}, bf16[2,4,512,128]{3,2,1,0:T(8,128)(2,1)}, u32[]{:S(2)}, u32[]{:S(2)}) collective-permute-start(bf16[2,4,512,128]{3,2,1,0:T(8,128)(2,1)} %get-tuple-element.20), channel_id=1, source_target_pairs={{4,0},{8,4},{12,8},{16,12},{20,16},{24,20},{28,24},{32,28},{36,32}... | collective-permute-start | bytes 3145736 | tf_op jit(solution)/shard_map/ppermute | solution.py:220
  103.4 2.3 copy-start.3
  116.1 9.2 %copy-start.1 = (bf16[2,5,512,128]{3,2,1,0:T(8,128)(2,1)S(1)}, bf16[2,5,512,128]{3,2,1,0:T(8,128)(2,1)}, u32[]{:S(2)}) copy-start(bf16[2,5,512,128]{3,2,1,0:T(8,128)(2,1)} %slice.60) | copy-start | bytes 3932164
  204.9 0.7 copy-start.8
Sparse Core Ops, SparseCore 0:
  205.1 55.8 reduce-scatter.1

commit v12 on v11

--- a/solution.py
+++ b/solution.py
@@ -34,13 +34,11 @@
         ) * score_scale
         if masked:
             mask = qs_ref[0] == ks_ref[0]
-            s = jnp.where(mask, s, -1e30)
+            s = jnp.where(mask, s, -jnp.inf)
         m_prev = m_scr[...]
         m_new = jnp.maximum(m_prev, jnp.max(s, axis=1, keepdims=True))
         alpha = jnp.exp(m_prev - m_new)
         p = jnp.exp(s - m_new[:, :1])
-        if masked:
-            p = jnp.where(mask, p, 0.0)
         l_scr[...] = alpha * l_scr[...] + jnp.sum(p, axis=1, keepdims=True)
         acc_scr[...] = alpha * acc_scr[...] + jnp.dot(
             p.astype(jnp.bfloat16), v_ref[0], preferred_element_type=jnp.float32

time: 272 us -> 271 us (level)
  blocking collectives: 37.7 us -> 43.6 us
  Pallas kernels: 106 us -> 102 us
  waiting for transfers between devices: 63.3 us -> 60.1 us
    all_to_all x1, blocking collectives: 28.2 us -> 34 us  [local(): got = lax.all_to_all(placed, 'ctx', split_axis=0, concat_axis=0, tiled=True)]
    pallas_call x1, Pallas kernels: 36.5 us -> 33 us  [flash(): pl.pallas_call(kern, grid_spec=grid_spec, out_shape=jax.ShapeDtypeStruct(...]
    reduce_scatter x1, waiting for transfers between devices: 55 us -> 51.9 us  [local(): lax.psum_scatter(head_terms.astype(jnp.bfloat16), 'head', scatter_dimensi...]
where the time goes in v12:
time: 271 us
  Pallas kernels  102 us (38%)
  waiting for transfers between devices  60.1 us (22%)
  blocking collectives  43.6 us (16%)
  local copies, waits for them, and re-layouts  22.9 us (8%)
  matrix products  14.8 us (5%)
  between operations  13.7 us (5%)
  other arithmetic  7.99 us (3%)
  starting transfers between devices  5.01 us (2%)
    pallas_call x1, Pallas kernels, relay(): pl.pallas_call(kern, out_shape=(jax.ShapeDtypeStruct((slots,) + tiles.sha...  69.5 us
    reduce_scatter x1, waiting for transfers between devices, local(): lax.psum_scatter(head_terms.astype(jnp.bfloat16), 'head', scatter_dimensi...  51.9 us
    all_to_all x1, blocking collectives, local(): got = lax.all_to_all(placed, 'ctx', split_axis=0, concat_axis=0, tiled=True)  34 us
    pallas_call x1, Pallas kernels, flash(): pl.pallas_call(kern, grid_spec=grid_spec, out_shape=jax.ShapeDtypeStruct(...  33 us
    psum x1, blocking collectives, local(): lax.psum((jnp.sum(query_float * query_float, axis=1), jnp.sum(key_float *...  9.55 us
    dot_general x1, matrix products, local(): jnp.dot(owned_attended, out_weight, preferred_element_type=jnp.float32)  8.85 us
  transfers between devices with their start and end apart: 3, of which 3 were waited for; matrix products, arithmetic and copies ran while one was open for 6% of the time, Pallas kernels for 0%

profile of v12, /device:TPU:1, one launch (start us, length us, event | category | flops | bytes accessed | tf_op | source)
XLA Modules:
  0.0 270.6 jit_solution(16513355676818917345)
XLA Ops:
  6.5 1.4 copy.37
  8.6 9.6 %all-reduce = (f32[512]{0:T(512)S(1)}, f32[512]{0:T(512)S(1)}) all-reduce(f32[512]{0:T(512)S(1)} %fusion.7, f32[512]{0:T(512)S(1)} %fusion.4), channel_id=1, replica_groups=mesh['batch'=4,'ctx'=16,'head'=4] {'head'}, use_global_device_ids=true, to_apply=%region_3.0 | all-reduce | flops 1024 | bytes 8192 | tf_op jit(solution)/shard_map/psum | solution.py:194
  19.3 1.3 copy.39
  20.9 0.6 pad_add_fusion.mark_ref
  21.6 1.5 maximum_bitcast_fusion.src_ref
  23.0 69.5 %shard_map.100 = (bf16[5,3,512,128]{3,2,1,0:T(8,128)(2,1)}, s32[16,2,512]{2,1,0:T(2,128)}) custom-call(bf16[5,3,512,128]{3,2,1,0:T(8,128)(2,1)} %maximum_bitcast_fusion.src_ref, s32[2,512]{1,0:T(2,128)} %pad_add_fusion.mark_ref), custom_call_target="tpu_custom_call" | custom-call | tf_op jit(solution)/shard_map/pallas_call | solution.py:151
  92.5 1.7 copy.65
  94.2 1.7 fusion.30
  95.9 3.7 %collective-permute-start = (bf16[2,4,512,128]{3,2,1,0:T(8,128)(2,1)}, bf16[2,4,512,128]{3,2,1,0:T(8,128)(2,1)S(1)}, u32[]{:S(2)}, u32[]{:S(2)}) collective-permute-start(bf16[2,4,512,128]{3,2,1,0:T(8,128)(2,1)} %get-tuple-element.19), channel_id=1, source_target_pairs={{0,4},{4,8},{8,12},{12,16},{16,20},{20,24},{24,28},{28,32},{32,36}... | collective-permute-start | bytes 3145736 | tf_op jit(solution)/shard_map/ppermute | solution.py:215
  99.6 1.3 collective-permute-start.1
  102.4 1.0 fusion.31
  103.6 0.7 gather_fusion.1
  104.3 0.6 gather_fusion.4
  104.9 0.8 gather_fusion.2
  105.7 0.8 gather_fusion.3
  106.9 1.1 slice.60
  108.9 0.7 iota_reduce_fusion
  109.7 0.7 fusion.15
  110.4 1.3 gather_fusion.6
  111.7 1.3 gather_fusion.5
  113.0 2.6 copy.51.qs_ref
  116.2 0.9 slice_bitcast_fusion.2.q_ref
  117.1 4.4 %collective-permute-done = bf16[2,4,512,128]{3,2,1,0:T(8,128)(2,1)S(1)} collective-permute-done((bf16[2,4,512,128]{3,2,1,0:T(8,128)(2,1)}, bf16[2,4,512,128]{3,2,1,0:T(8,128)(2,1)S(1)}, u32[]{:S(2)}, u32[]{:S(2)}) %collective-permute-start) | collective-permute-done | bytes 1048608 | tf_op jit(solution)/shard_map/ppermute | solution.py:215
  121.4 3.9 %collective-permute-done.1 = bf16[2,4,512,128]{3,2,1,0:T(8,128)(2,1)} collective-permute-done((bf16[2,4,512,128]{3,2,1,0:T(8,128)(2,1)}, bf16[2,4,512,128]{3,2,1,0:T(8,128)(2,1)}, u32[]{:S(2)}, u32[]{:S(2)}) %collective-permute-start.1) | collective-permute-done | bytes 1048608 | tf_op jit(solution)/shard_map/ppermute | solution.py:218
  125.3 1.5 pad_maximum_fusion
  126.8 2.0 slice_bitcast_fusion
  128.8 33.0 %shard_map.101 = bf16[5,512,128]{2,1,0:T(8,128)(2,1)} custom-call(s32[45]{0:T(128)} %get-tuple-element.15.need_ref, s32[5]{0:T(128)} %get-tuple-element.29.qp_ref, s32[45]{0:T(128)} %gather_fusion.5, s32[45]{0:T(128)} %gather_fusion.6, bf16[5,512,128]{2,1,0:T(8,128)(2,1)} %slice_bitcast_fusion.2.q_ref, bf16[13,512,128]{2,1,0:T(8,128)(2,1)} %get-tuple-element.18.k_ref, ...), custom_call_target="tpu_custom_call" | custom-call | tf_op jit(solution)/shard_map/pallas_call | solution.py:82
  161.8 2.0 fusion.3
  163.9 34.0 %all_to_all.5 = bf16[16,5,32,128]{3,2,1,0:T(8,128)(2,1)S(1)} all-to-all(bf16[16,5,32,128]{3,2,1,0:T(8,128)(2,1)S(1)} %bitcast.51), channel_id=1, replica_groups=mesh['batch'=4,'ctx'=16,'head'=4] {'ctx'}, dimensions={0} | all-to-all | bytes 1310720 | tf_op jit(solution)/shard_map/all_to_all | solution.py:267
  198.4 8.9 %convolution_convert_fusion = bf16[512,5120]{1,0:T(8,128)(2,1)} fusion(bf16[640,5120]{1,0:T(8,128)(2,1)} %param.18, bf16[64,8,5,128]{3,2,1,0:T(8,128)(2,1)S(1)} %bitcast.56), kind=kOutput, calls=%fused_computation.7 | convolution fusion | flops 3358064640 | bytes 12451840 | tf_op jit(solution)/shard_map/dot_general | solution.py:280
  208.2 51.9 %reduce-scatter.2.cloned.1.call-done = bf16[512,1280]{1,0:T(8,128)(2,1)} async-done(((bf16[512,5120]{1,0:T(8,128)(2,1)}), bf16[512,1280]{1,0:T(8,128)(2,1)}) %reduce-scatter.2.cloned.1.call-update) | async-done | bytes 1310736 | tf_op jit(solution)/shard_map/reduce_scatter | solution.py:281
  260.1 3.6 %fusion.1 = bf16[512,1280]{1,0:T(8,128)(2,1)} fusion(f32[6,1280]{1,0:T(8,128)S(1)} %fusion.23, bf16[512,1280]{1,0:T(8,128)(2,1)} %reduce-scatter.2.cloned.1.call-done, s32[512]{0:T(512)S(1)} %eq.133), kind=kOutput, calls=%fused_computation.12 | convolution fusion | flops 49155072 | bytes 2654208 | tf_op jit(solution)/shard_map/dot_general | solution.py:289
  (73 shorter events, 7.0 us)
Async XLA Ops:
  6.5 201.5 %copy-start = (f32[50,1280]{1,0:T(8,128)S(1)}, f32[50,1280]{1,0:T(8,128)}, u32[]{:S(2)}) copy-start(f32[50,1280]{1,0:T(8,128)} %param.19) | copy-start | bytes 768004
  6.5 1.6 copy-start.2
  6.5 11.6 %copy-start.4 = (f32[640]{0:T(1024)S(1)}, f32[640]{0:T(1024)}, u32[]{:S(2)}) copy-start(f32[640]{0:T(1024)} %param.14) | copy-start | bytes 7684
  6.5 253.6 %reduce-scatter.2.cloned.1.call-start = ((), (), s32[]{:S(2)}) async-start(), calls=%async_computation.2 | async-start | bytes 6553600 | tf_op jit(solution)/shard_map/reduce_scatter | solution.py:281
  8.4 10.3 %copy-start.5 = (f32[640]{0:T(1024)S(1)}, f32[640]{0:T(1024)}, u32[]{:S(2)}) copy-start(f32[640]{0:T(1024)} %param.13) | copy-start | bytes 7684
  18.9 2.0 copy-start.6
  18.9 2.0 copy-start.7
  95.9 25.5 %collective-permute-start = (bf16[2,4,512,128]{3,2,1,0:T(8,128)(2,1)}, bf16[2,4,512,128]{3,2,1,0:T(8,128)(2,1)S(1)}, u32[]{:S(2)}, u32[]{:S(2)}) collective-permute-start(bf16[2,4,512,128]{3,2,1,0:T(8,128)(2,1)} %get-tuple-element.19), channel_id=1, source_target_pairs={{0,4},{4,8},{8,12},{12,16},{16,20},{20,24},{24,28},{28,32},{32,36}... | collective-permute-start | bytes 3145736 | tf_op jit(solution)/shard_map/ppermute | solution.py:215
  99.6 25.7 %collective-permute-start.1 = (bf16[2,4,512,128]{3,2,1,0:T(8,128)(2,1)}, bf16[2,4,512,128]{3,2,1,0:T(8,128)(2,1)}, u32[]{:S(2)}, u32[]{:S(2)}) collective-permute-start(bf16[2,4,512,128]{3,2,1,0:T(8,128)(2,1)} %get-tuple-element.20), channel_id=1, source_target_pairs={{4,0},{8,4},{12,8},{16,12},{20,16},{24,20},{28,24},{32,28},{36,32}... | collective-permute-start | bytes 3145736 | tf_op jit(solution)/shard_map/ppermute | solution.py:218
  103.4 2.3 copy-start.3
  116.1 9.2 %copy-start.1 = (bf16[2,5,512,128]{3,2,1,0:T(8,128)(2,1)S(1)}, bf16[2,5,512,128]{3,2,1,0:T(8,128)(2,1)}, u32[]{:S(2)}) copy-start(bf16[2,5,512,128]{3,2,1,0:T(8,128)(2,1)} %slice.60) | copy-start | bytes 3932164
  207.3 0.7 copy-start.8
Sparse Core Ops, SparseCore 0:
  207.4 52.6 reduce-scatter.1
